TPU v7x, 32 devices: a whole 2x2x4 slice. The times are simulated.
32 devices in a mesh: dp: 8 (over z, y), mp: 4 (over x, core).
Axes of the slice: x: 2, y: 2, z: 4, core: 2. Of those that a mesh axis runs over, the one named last changes fastest.
Arguments:
- tokens: bfloat16 [16560, 1024], P('dp'), may hold values from -6 to 6
- offsets: int32 [48, 5], P('dp'), may hold values from 0 to 308, as said below
- first_gain: float32 [1024], replicated, may hold values from 0.1 to 1.9
- first_shift: float32 [1024], replicated, may hold values from -1.8 to 1.8
- qkv_weight: float32 [1024, 3, 1024], P('dp', None, 'mp'), may hold values from -0.1875 to 0.1875
- qv_bias: float32 [2, 1024], P(None, 'mp'), may hold values from -1.8 to 1.8
- proj_weight: float32 [1024, 1024], P('mp', 'dp'), may hold values from -0.5 to 0.5
- proj_bias: float32 [1024], replicated, may hold values from -1.8 to 1.8
- second_gain: float32 [1024], replicated, may hold values from 0.1 to 1.9
- second_shift: float32 [1024], replicated, may hold values from -1.8 to 1.8
- expand_weight: float32 [1024, 4096], P('dp', 'mp'), may hold values from -0.1875 to 0.1875
- expand_bias: float32 [4096], P('mp'), may hold values from -1.8 to 1.8
- shrink_weight: float32 [4096, 1024], P('mp', 'dp'), may hold values from -0.09375 to 0.09375
- shrink_bias: float32 [1024], replicated, may hold values from -1.8 to 1.8
- cotangent: bfloat16 [16560, 1024], P('dp'), may hold values from -6 to 6
Outputs:
- out: bfloat16 [16560, 1024], P('dp')
- d_tokens: float32 [16560, 1024], P('dp')
- d_first_gain: float32 [1024], replicated
- d_first_shift: float32 [1024], replicated
- d_qkv_weight: float32 [1024, 3, 1024], P('dp', None, 'mp')
- d_qv_bias: float32 [2, 1024], P(None, 'mp')
- d_proj_weight: float32 [1024, 1024], P('mp', 'dp')
- d_proj_bias: float32 [1024], replicated
- d_second_gain: float32 [1024], replicated
- d_second_shift: float32 [1024], replicated
- d_expand_weight: float32 [1024, 4096], P('dp', 'mp')
- d_expand_bias: float32 [4096], P('mp')
- d_shrink_weight: float32 [4096, 1024], P('mp', 'dp')
- d_shrink_bias: float32 [1024], replicated
Inputs may be any that keep to these rules, and one draw needn't show every extreme that they name: `offsets`: each row lists, rising, where the 5 crops of one crop set start within its 345 tokens: the first starts at 0, one crop spans 197 tokens, the others 37 each, and the last ends at the set's end.
All inputs are finite; a program needn't handle non-finite values.
Results may differ from a plain program's by a relative error of at most 0.015.
Values may be sent and summed in bfloat16 or wider, within the bound.
No kernel may reach another device: no remote copies, remote signals or barrier semaphores. Data moves between devices by JAX's collectives and lax.ppermute only.
A program may use at most 128 MiB of HBM per device.

v0:
```python
import functools

import jax
import jax.numpy as jnp
import numpy as np
from jax import lax
from jax.experimental import pallas as pl
from jax.experimental.pallas import tpu as pltpu
from jax.sharding import PartitionSpec as P

HEAD_DIM = 64
SET_TOKENS = 345
SET_ROWS = 352
LANES = 128
CHUNK = 256

norm_eps = 1e-06
masked_score = -1e30
root_half = 0.7071067811865476
density_scale = 0.3989422804014327
f32 = jnp.float32
bf16 = jnp.bfloat16
NN = (((1,), (0,)), ((), ()))
NT = (((1,), (1,)), ((), ()))
TN = (((0,), (0,)), ((), ()))
ANY = pl.BlockSpec(memory_space=pl.ANY)
HBM = pl.BlockSpec(memory_space=pltpu.HBM)


def dot(left, right, dims=NN):
    return lax.dot_general(left, right, dims, preferred_element_type=f32)


ROOM = {
    "ring_first": 4,
    "ring_add": 10,
    "ring_last": 8,
    "qkv": 20,
    "pad": 20,
    "assemble": 20,
    "first_low": 10,
    "attend": 10,
    "attend_back": 12,
    "proj_norm": 20,
    "mlp": 58,
    "mlp_grad": 58,
    "residual_back": 16,
    "qkv_grad": 20,
    "first_norm": 58,
}


def call(body, grid, in_specs, out_specs, out_shape, scratch, name, aliases=None):
    return pl.pallas_call(
        body,
        grid_spec=pltpu.PrefetchScalarGridSpec(
            num_scalar_prefetch=1,
            grid=grid,
            in_specs=in_specs,
            out_specs=out_specs,
            scratch_shapes=scratch,
        ),
        out_shape=out_shape,
        compiler_params=pltpu.CompilerParams(
            dimension_semantics=("arbitrary",) * len(grid), vmem_limit_bytes=ROOM[name] * 2**20
        ),
        cost_estimate=pl.CostEstimate(flops=1, bytes_accessed=1, transcendentals=0),
        name=name,
        input_output_aliases=aliases or {},
    )


def tie(value, *earlier):
    return lax.optimization_barrier((value, earlier))[0]


class Order:
    def __init__(self, info):
        self.info = info
        self.now = info
        self.due = ()
        self.hold = ()

    def after(self, value):
        return tie(value, self.now, self.due)

    def run(self, kernel, *values, wait=()):
        out = kernel(tie(self.info, self.now, wait, self.hold), *values)
        self.hold = ()
        self.now = out[0] if isinstance(out, (list, tuple)) else out
        return out


def shape(dims, dtype):
    return jax.ShapeDtypeStruct(tuple(dims), dtype)


def ring_order(count):
    width = 1
    while 2 * (2 * width) ** 2 <= count:
        width *= 2
    length = count // width
    if width == 1:
        return list(range(count))
    path = []
    for z in range(length):
        columns = range(1, width) if z % 2 == 0 else range(width - 1, 0, -1)
        path += [z * width + y for y in columns]
    path += [z * width for z in range(length - 1, -1, -1)]
    return path


class Ring:
    def __init__(self, count):
        self.count = count
        self.order = ring_order(count)
        self.place = {rank: i for i, rank in enumerate(self.order)}
        self.ahead = [(self.order[i], self.order[(i + 1) % count]) for i in range(count)]
        self.behind = [(self.order[i], self.order[(i - 1) % count]) for i in range(count)]

    def rank_at(self, rank, offset):
        return self.order[(self.place[rank] + offset) % self.count]

    def send_ahead(self, value):
        return lax.ppermute(value, "dp", self.ahead)

    def send_behind(self, value):
        return lax.ppermute(value, "dp", self.behind)

    def gather_steps(self, block, axis, order):
        half = block.shape[axis] // 2
        forward = backward = block
        for step in range(1, self.count // 2 + 1):
            if step == self.count // 2:
                forward = lax.slice_in_dim(forward, 0, half, axis=axis)
                backward = lax.slice_in_dim(backward, half, 2 * half, axis=axis)
            forward, backward = order.after((forward, backward))
            forward = self.send_ahead(forward)
            backward = self.send_behind(backward)
            yield forward, backward

    def piece_rows(self, rows):
        table = []
        middle = self.count // 2
        for rank in range(self.count):
            starts = [rank * rows]
            for step in range(1, middle + 1):
                ahead = self.rank_at(rank, -step) * rows
                behind = self.rank_at(rank, step) * rows
                if step == middle:
                    behind += rows // 2
                starts += [ahead, behind]
            table.append(starts)
        return np.array(table, np.int32)

    def block_ranks(self):
        middle = self.count // 2
        return np.array(
            [
                [self.rank_at(rank, d) for d in range(-middle, middle + 1)]
                for rank in range(self.count)
            ],
            np.int32,
        )

    def scatter_steps(self, whole, ranks, order):
        middle = self.count // 2
        dim, columns = whole.shape
        rows = dim // self.count
        half = rows // 2
        wide = columns
        grid = (columns // wide,)
        block = lambda d: pl.BlockSpec((rows, wide), lambda j, info: (info[ranks + middle + d], j))
        plain = lambda count: pl.BlockSpec((count, wide), lambda j, _: (0, j))
        kernel = call(
            ring_first_body,
            grid,
            [
                pl.BlockSpec((half, wide), lambda j, info: (2 * info[ranks + 2 * middle], j)),
                pl.BlockSpec((half, wide), lambda j, info: (2 * info[ranks] + 1, j)),
            ],
            [plain(half)] * 2,
            [shape((half, columns), bf16)] * 2,
            [],
            "ring_first",
        )
        forward, backward = order.run(kernel, whole, whole)
        for step in range(1, middle + 1):
            forward = self.send_ahead(order.after(forward))
            backward = self.send_behind(order.after(backward))
            yield forward, backward
            near = middle - step
            if near == 0:
                break
            kernel = call(
                ring_add_body,
                grid,
                [block(near), block(-near)] + [plain(forward.shape[0])] * 2,
                [plain(rows)] * 2,
                [shape((rows, columns), bf16)] * 2,
                [],
                "ring_add",
            )
            forward, backward = order.run(kernel, whole, whole, forward, backward)
        kernel = call(
            ring_last_body,
            grid,
            [block(0)] + [plain(rows)] * 2,
            plain(rows),
            shape((rows, columns), f32),
            [],
            "ring_last",
        )
        yield order.run(kernel, whole, forward, backward)


def across(value, step, chips):
    pairs = [
        (x * 2 + core, (x + step) % chips * 2 + core) for x in range(chips) for core in range(2)
    ]
    return lax.ppermute(value, "mp", pairs)


def partner(value, chips):
    return lax.ppermute(value, "mp", [(m, m ^ 1) for m in range(2 * chips)])


def layer_norm(values, gain, shift):
    centre = jnp.mean(values, axis=-1, keepdims=True)
    offset_rows = values - centre
    spread = jnp.mean(offset_rows * offset_rows, axis=-1, keepdims=True)
    return offset_rows * lax.rsqrt(spread + norm_eps) * gain + shift


def start_all(copies, sems):
    moves = [pltpu.make_async_copy(src, dst, sems.at[i]) for i, (src, dst) in enumerate(copies)]
    for move in moves:
        move.start()
    return moves


def wait_all(moves):
    for move in moves:
        move.wait()


def weight_copies(info, base, pieces, unit, targets):
    copies = []
    for i, piece in enumerate(pieces):
        rows = piece.shape[-2]
        place = pl.ds(pl.multiple_of(info[base + i], unit), rows)
        for source, target in targets:
            copies.append((source(piece), target(place)))
    return copies


def ring_first_body(info, ahead_ref, behind_ref, ahead_out, behind_out):
    ahead_out[...] = ahead_ref[...]
    behind_out[...] = behind_ref[...]


def ring_add_body(info, ahead_ref, behind_ref, got_ahead, got_behind, ahead_out, behind_out):
    rows, part = ahead_out.shape[0], got_ahead.shape[0]
    first, last = slice(0, part), slice(rows - part, rows)
    total = ahead_ref[first, :].astype(f32) + got_ahead[...].astype(f32)
    ahead_out[first, :] = total.astype(bf16)
    total = behind_ref[last, :].astype(f32) + got_behind[...].astype(f32)
    behind_out[last, :] = total.astype(bf16)
    if part < rows:
        ahead_out[part:, :] = ahead_ref[part:, :]
        behind_out[: rows - part, :] = behind_ref[: rows - part, :]


def ring_last_body(info, own_ref, got_ahead, got_behind, out_ref):
    both = got_ahead[...].astype(f32) + got_behind[...].astype(f32)
    out_ref[...] = own_ref[...].astype(f32) + both


def qkv_body(info, x_ref, bias_ref, *rest, base, unit, chips, count):
    pieces, (out_ref, whole_ref, weights, sems, out_sem) = rest[:count], rest[count:]
    part = weights.shape[1] // chips
    width = out_ref.shape[1] // chips
    keep = pltpu.make_async_copy(weights, whole_ref, out_sem)

    @pl.when(pl.program_id(0) == 0)
    def _():
        targets = [
            (
                lambda piece, b=b: piece.at[b],
                lambda place, b=b: weights.at[place, pl.ds(b * part, part)],
            )
            for b in range(chips)
        ]
        wait_all(start_all(weight_copies(info, base, pieces, unit, targets), sems))
        keep.start()

    def columns(b, _):
        to = pl.ds(pl.multiple_of(b * width, LANES), width)
        product = dot(x_ref[...], weights[:, pl.ds(pl.multiple_of(b * part, LANES), width)])
        out_ref[:, to] = (product + bias_ref[:, to]).astype(bf16)
        return 0

    lax.fori_loop(0, chips, columns, 0)

    @pl.when(pl.program_id(0) == pl.num_programs(0) - 1)
    def _():
        keep.wait()


def pad_body(info, in_ref, out_ref, rows, *, sets):
    total = in_ref.shape[0]
    rows[0:total, :] = in_ref[...].astype(f32)
    inside = lax.broadcasted_iota(jnp.int32, (SET_ROWS, 1), 0) < SET_TOKENS
    for g in range(out_ref.shape[0] // SET_ROWS):
        to = slice(g * SET_ROWS, (g + 1) * SET_ROWS)
        if g < sets:
            value = rows[g * SET_TOKENS : g * SET_TOKENS + SET_ROWS, :]
            out_ref[to, :] = jnp.where(inside, value, 0.0).astype(bf16)
        else:
            out_ref[to, :] = jnp.zeros((SET_ROWS, out_ref.shape[1]), bf16)


def assemble_body(info, *refs, base, sets):
    pieces, (out_ref, padded, packed) = refs[:-3], refs[-3:]
    half = pieces[0].shape[0]
    for i, piece in enumerate(pieces):
        place = pl.ds(pl.multiple_of(info[base + i] * half, 16), half)
        padded[place, :] = piece[...].astype(f32)
    target = out_ref if out_ref.dtype == f32 else packed
    for g in range(sets):
        target[g * SET_TOKENS : (g + 1) * SET_TOKENS, :] = padded[
            g * SET_ROWS : g * SET_ROWS + SET_TOKENS, :
        ]
    if out_ref.dtype != f32:
        out_ref[...] = packed[0 : out_ref.shape[0], :].astype(out_ref.dtype)


def first_low_body(info, x_ref, gain_ref, shift_ref, out_ref):
    out_ref[...] = layer_norm(x_ref[...].astype(f32), gain_ref[...], shift_ref[...]).astype(bf16)


def head_mask(head):
    lane = lax.broadcasted_iota(jnp.int32, (1, LANES), 1)
    return (lane < HEAD_DIM) if head == 0 else (lane >= HEAD_DIM)


def keep_head(value, head):
    return jnp.where(head_mask(head), value, jnp.zeros_like(value))


def attend_body(info, qkv_ref, key_ids, query_ids, out_ref, log_ref, block):
    @pl.when(pl.program_id(1) == 0)
    def _():
        block[...] = jnp.where(key_ids[0] == query_ids[0], 0.0, masked_score)

    factor = HEAD_DIM**-0.5
    query = qkv_ref[:, 0:LANES] * jnp.asarray(factor, bf16)
    key = qkv_ref[:, LANES : 2 * LANES]
    value = qkv_ref[:, 2 * LANES : 3 * LANES]
    halves = []
    for head in range(2):
        scores = dot(key, keep_head(query, head), NT) + block[...]
        peak = jnp.max(scores, axis=0, keepdims=True)
        raised = jnp.exp(scores - peak)
        total = jnp.sum(raised, axis=0, keepdims=True)
        mixed = dot(keep_head(value, head), raised.astype(bf16), TN)
        halves.append(mixed * (1.0 / total))
        log_ref[0, 0, head : head + 1, :] = peak + jnp.log(total)
    out_ref[...] = (halves[0] + halves[1]).T.astype(bf16)


def attend_back_body(info, qkv_ref, key_ids, query_ids, log_ref, *rest, first_half):
    grads = rest[:4]
    out_ref, sum_ref, block = rest[-3:]
    turn = pl.program_id(1)

    @pl.when(pl.program_id(0) == 0)
    def _():
        block[turn] = jnp.where(key_ids[0] == query_ids[0], 0.0, masked_score)

    factor = HEAD_DIM**-0.5
    query = qkv_ref[:, 0:LANES] * jnp.asarray(factor, bf16)
    key = qkv_ref[:, LANES : 2 * LANES]
    value = qkv_ref[:, 2 * LANES : 3 * LANES]
    parts = []
    for j in range(2):
        core = ((2 * turn + j) >= first_half).astype(jnp.int32)
        parts.append(jnp.where(core == info[0], grads[2 * j][...], grads[2 * j + 1][...]))
    grad = jnp.concatenate(parts, axis=0)
    grad_query = grad_key = grad_value = 0.0
    for head in range(2):
        query_one = keep_head(query, head)
        grad_one = keep_head(grad, head)
        scores = dot(key, query_one, NT) + block[turn]
        weights = jnp.exp(scores - log_ref[0, 0, head : head + 1, :])
        grad_value += dot(weights.astype(bf16), grad_one)
        grad_weights = dot(value, grad_one, NT)
        centre = jnp.sum(weights * grad_weights, axis=0, keepdims=True)
        low = (weights * (grad_weights - centre)).astype(bf16)
        grad_key += dot(low, query_one)
        grad_query += dot(keep_head(key, head), low, TN)
    grad_query = (grad_query * factor).T
    out_ref[:, 0:LANES] = grad_query.astype(bf16)
    out_ref[:, LANES : 2 * LANES] = grad_key.astype(bf16)
    out_ref[:, 2 * LANES : 3 * LANES] = grad_value.astype(bf16)

    @pl.when(turn == 0)
    def _():
        sum_ref[...] = jnp.zeros_like(sum_ref)

    sum_ref[0, :, 0:LANES] += jnp.sum(grad_query, axis=0, keepdims=True)
    sum_ref[0, :, 2 * LANES : 3 * LANES] += jnp.sum(grad_value, axis=0, keepdims=True)


def proj_moves(wholes, weights, chips, sems):
    width = weights.shape[1] // (2 * chips)
    part = wholes[0].shape[1] // chips
    copies = []
    for j, source in enumerate(wholes):
        for b in range(chips):
            columns = pl.ds((b + 1) * part - width, width)
            target = pl.ds((j * chips + b) * width, width)
            copies.append((source.at[:, columns], weights.at[:, target]))
    return [pltpu.make_async_copy(src, dst, sems.at[i]) for i, (src, dst) in enumerate(copies)]


def proj_norm_body(
    info, own_ref, got_ref, x_ref, bias_ref, gain_ref, shift_ref, *rest, chips
):
    wholes, (residual_ref, low_ref, weights, sems) = rest[:2], rest[2:]
    moves = proj_moves(wholes, weights, chips, sems)
    for move in moves:
        move.start()
    wait_all(moves)
    width = own_ref.shape[1]
    span = 2 * CHUNK

    def columns(i, _):
        at = pl.ds(pl.multiple_of(i * span, span), span)
        own_part = dot(own_ref[...], weights[at, :width], NT)
        residual_ref[:, at] = own_part + dot(got_ref[...], weights[at, width:], NT)
        return 0

    lax.fori_loop(0, residual_ref.shape[1] // span, columns, 0)
    step = row_step(residual_ref.shape[0])

    def rows(i, _):
        at = pl.ds(pl.multiple_of(i * step, 16), step)
        value = residual_ref[at, :] + x_ref[at, :].astype(f32) + bias_ref[...]
        residual_ref[at, :] = value
        low_ref[at, :] = layer_norm(value, gain_ref[...], shift_ref[...]).astype(bf16)
        return 0

    lax.fori_loop(0, residual_ref.shape[0] // step, rows, 0)


def row_step(rows):
    return 176 if rows % 176 == 0 else rows


def mlp_body(info, cot_ref, bias_ref, *rest, base, unit, count, parts, adds):
    pieces, rest = rest[:count], rest[count:]
    seconds, rest = rest[:parts], rest[parts:]
    gots, rest = rest[: 2 * adds], rest[2 * adds :]
    hidden_ref, pre_ref, rest = rest[0], rest[1], rest[2:]
    backs, outs, rest = rest[:parts], rest[parts : 2 * parts], rest[2 * parts :]
    sum_ref, expand, shrink, rows, sems, row_sems = rest
    width = expand.shape[1]
    turn = pl.program_id(0)

    @pl.when(turn == 0)
    def _():
        targets = [
            (
                lambda piece: piece.at[:, pl.ds(0, width)],
                lambda place: expand.at[place, :],
            ),
            (
                lambda piece: piece.at[:, pl.ds(width, width)],
                lambda place: shrink.at[place, :],
            ),
        ]
        moves = start_all(weight_copies(info, base, pieces, unit, targets), sems)
        start_all([(seconds[i], rows.at[i]) for i in range(parts)], row_sems)
        wait_all(moves)
        sum_ref[...] = jnp.zeros_like(sum_ref)

    pltpu.make_async_copy(seconds[0], rows.at[turn], row_sems.at[turn]).wait()
    span = 2 * CHUNK if width % (2 * CHUNK) == 0 else LANES

    def columns(i, _):
        at = pl.ds(pl.multiple_of(i * span, span), span)
        pre = dot(rows[turn], expand[:, at]) + bias_ref[:, at]
        below = 0.5 * (1.0 + lax.erf(pre * root_half))
        density = density_scale * jnp.exp(-0.5 * pre * pre)
        hidden_ref[:, at] = (pre * below).astype(bf16)
        grad = dot(cot_ref[...], shrink[:, at]) * (below + pre * density)
        sum_ref[:, at] += jnp.sum(grad, axis=0, keepdims=True)
        pre_ref[:, at] = grad.astype(bf16)
        return 0

    lax.fori_loop(0, width // span, columns, 0)

    def back(i, _):
        at = pl.ds(pl.multiple_of(i * span, span), span)
        for targets, left, right, kind in (
            (backs, pre_ref, expand, 0),
            (outs, hidden_ref, shrink, 1),
        ):
            product = dot(left[...], right[at, :], NT)
            for i in range(parts):

                @pl.when(turn == i)
                def _(i=i, targets=targets, product=product, kind=kind):
                    total = product
                    if adds:
                        total = total + gots[2 * i + kind][:, at].astype(f32)
                    targets[i][:, at] = total.astype(bf16)

        return 0

    lax.fori_loop(0, backs[0].shape[1] // span, back, 0)


def mlp_grad_body(info, cot_ref, *rest, cot_base, parts, groups):
    seconds, rest = rest[:parts], rest[parts:]
    hiddens, pres, rest = rest[:groups], rest[groups : 2 * groups], rest[2 * groups :]
    out_ref, left, right, sems = rest
    phase = pl.program_id(0)
    rows = left.shape[1] // parts
    span = out_ref.shape[0]

    def moves(index):
        pairs = []
        for i in range(parts):
            source = seconds[i]
            if index == 1:
                place = pl.multiple_of(info[cot_base + i] * rows, 16)
                source = cot_ref.at[pl.ds(place, rows)]
            pairs.append((source, left.at[index, pl.ds(i * rows, rows)]))
        start = 0
        for source in (pres, hiddens)[index]:
            pairs.append((source, right.at[index, pl.ds(start, source.shape[0])]))
            start += source.shape[0]
        return [
            pltpu.make_async_copy(src, dst, sems.at[index, i]) for i, (src, dst) in enumerate(pairs)
        ]

    @pl.when((phase == 0) & (pl.program_id(1) == 0))
    def _():
        for index in range(2):
            for move in moves(index):
                move.start()

    for index in range(2):

        @pl.when((phase == index) & (pl.program_id(1) == 0))
        def _(index=index):
            wait_all(moves(index))

    at = pl.ds(pl.multiple_of(pl.program_id(1) * span, span), span)
    out_ref[...] = dot(left[phase, :, at], right[phase], TN).astype(bf16)


def norm_back(value, grad, gain):
    centred = value - jnp.mean(value, axis=-1, keepdims=True)
    spread = jnp.mean(centred * centred, axis=-1, keepdims=True)
    scale = lax.rsqrt(spread + norm_eps)
    normal = centred * scale
    weighted = grad * gain
    middle = jnp.mean(weighted, axis=-1, keepdims=True)
    slope = jnp.mean(weighted * normal, axis=-1, keepdims=True)
    return normal, scale * (weighted - middle - normal * slope)


def residual_back_body(info, residual_ref, cot_ref, gain_ref, *rest, parts, chips):
    grads, rest = rest[:parts], rest[parts:]
    wholes, (grad_ref, low_ref, own_ref, send_ref, sum_ref, weights, sems) = rest[:2], rest[2:]
    moves = proj_moves(wholes, weights, chips, sems)

    @pl.when(pl.program_id(0) == 0)
    def _():
        for move in moves:
            move.start()
        sum_ref[...] = jnp.zeros_like(sum_ref)

    grad = grads[0][...].astype(f32)
    for other in grads[1:]:
        grad += other[...].astype(f32)
    normal, back = norm_back(residual_ref[...], grad, gain_ref[...])
    cotangent = cot_ref[...].astype(f32)
    total = cotangent + back
    grad_ref[...] = total
    low_ref[...] = total.astype(bf16)
    sum_ref[0:1, :] += jnp.sum(grad * normal, axis=0, keepdims=True)
    sum_ref[1:2, :] += jnp.sum(grad, axis=0, keepdims=True)
    sum_ref[2:3, :] += jnp.sum(total, axis=0, keepdims=True)
    sum_ref[3:4, :] += jnp.sum(cotangent, axis=0, keepdims=True)

    @pl.when(pl.program_id(0) == 0)
    def _():
        wait_all(moves)

    both = dot(low_ref[...], weights[...]).astype(bf16)
    width = own_ref.shape[1]
    own_ref[...] = both[:, :width]
    send_ref[...] = both[:, width:]


def qkv_grad_body(info, first_ref, grad_ref, own_ref, got_ref, att_own, att_got, *rest):
    out_ref = rest[-1]
    width = grad_ref.shape[1]
    out_ref[:, :width] = dot(first_ref[...], grad_ref[...], TN).astype(bf16)
    out_ref[:, width:] = (
        dot(own_ref[...], att_own[...], TN) + dot(got_ref[...], att_got[...], TN)
    ).astype(bf16)


def first_norm_body(info, *refs, chips):
    grads, (x_ref, res_ref, gain_ref, *rest) = refs[: 2 * chips], refs[2 * chips :]
    wholes, (low_ref, sum_ref, weights, lefts, total, sems) = rest[:2], rest[2:]
    half, width = lefts.shape[1:]
    part = wholes[0].shape[1] // chips

    def move(i):
        return pltpu.make_async_copy(
            wholes[i // chips].at[:, pl.ds(i % chips * part, width)], weights.at[i], sems.at[i]
        )

    for i in range(2 * chips):
        move(i).start()
    for i in range(2 * chips):
        lefts[i] = grads[i][...]
    total[...] = jnp.zeros_like(total)

    def term(i, _):
        pltpu.make_async_copy(
            wholes[0].at[:, pl.ds(0, width)], weights.at[i], sems.at[i]
        ).wait()
        total[...] += dot(lefts[i], weights[i], NT)
        return 0

    lax.fori_loop(0, 2 * chips, term, 0)
    step = row_step(total.shape[0])
    sum_ref[...] = jnp.zeros_like(sum_ref)

    def rows(i, _):
        at = pl.ds(pl.multiple_of(i * step, 16), step)
        grad = total[at, :]
        normal, back = norm_back(x_ref[at, :].astype(f32), grad, gain_ref[...])
        low_ref[at, :] = (back + res_ref[at, :]).astype(bf16)
        sum_ref[0:1, :] += jnp.sum(grad * normal, axis=0, keepdims=True)
        sum_ref[1:2, :] += jnp.sum(grad, axis=0, keepdims=True)
        return 0

    lax.fori_loop(0, total.shape[0] // step, rows, 0)


def shards(
    tokens,
    offsets,
    first_gain,
    first_shift,
    qkv_weight,
    qv_bias,
    proj_weight,
    proj_bias,
    second_gain,
    second_shift,
    expand_weight,
    expand_bias,
    shrink_weight,
    shrink_bias,
    cotangent,
):
    token_rows, dim = tokens.shape
    sets = offsets.shape[0]
    part = qkv_weight.shape[2]
    ff = expand_weight.shape[1]
    chips = lax.axis_size("mp") // 2
    ring = Ring(lax.axis_size("dp"))
    dp_index = lax.axis_index("dp")
    mp_index = lax.axis_index("mp")
    x_index, core = mp_index // 2, mp_index % 2
    sets_x = -(-sets // chips)
    slots = sets_x * chips
    rows_x = sets_x * SET_ROWS
    half = rows_x // 2
    pairs = part // LANES
    groups = chips * pairs
    unit_rows = dim // ring.count
    unit = unit_rows // 2
    width = 3 * part
    att_width = groups * LANES
    near = [(0, 0), (0, 1)]
    far_other = [(step, 1) for step in range(1, chips)]
    far_own = [(step, 0) for step in range(1, chips)]
    keys = near + far_other + far_own
    sem = pltpu.SemaphoreType.DMA
    row = lambda value: value.reshape(1, -1)
    whole = lambda *dims: pl.BlockSpec(dims, lambda *_: (0,) * len(dims))

    row_starts = lax.dynamic_index_in_dim(ring.piece_rows(unit_rows), dp_index, 0, False)
    block_ranks = lax.dynamic_index_in_dim(ring.block_ranks(), dp_index, 0, False)
    places = [(x_index - step) % chips * 2 + (core ^ other) for step, other in keys]
    info = jnp.concatenate(
        [jnp.stack([core, x_index, *places]).astype(jnp.int32), row_starts, block_ranks]
    )
    place_base = 2
    base = place_base + len(keys)
    ranks = base + ring.count + 1

    order = Order(info)

    qkv_shard = qkv_weight.astype(bf16).reshape(unit_rows, 3, pairs, LANES)
    qkv_shard = qkv_shard.transpose(0, 2, 1, 3).reshape(unit_rows, width)
    shard = jnp.concatenate([qkv_shard, proj_weight.astype(bf16).T], axis=1)
    bias_shard = jnp.zeros((pairs, 3, LANES), f32)
    bias_shard = bias_shard.at[:, 0].set(qv_bias[0].reshape(pairs, LANES))
    bias_shard = bias_shard.at[:, 2].set(qv_bias[1].reshape(pairs, LANES)).reshape(1, width)
    shards_x, bias_x = [shard], [bias_shard]
    for step in range(1, chips):
        shards_x.append(across(shard, step, chips))
        bias_x.append(across(bias_shard, step, chips))
    both_shards = jnp.stack(shards_x)
    mlp_shard = jnp.concatenate(
        [expand_weight.astype(bf16), shrink_weight.astype(bf16).T], axis=1
    )
    attn_steps = ring.gather_steps(both_shards, 1, order)
    mlp_steps = ring.gather_steps(mlp_shard, 0, order)
    attn_pieces, mlp_pieces = [both_shards], [mlp_shard]

    def next_step(steps, pieces):
        got = next(steps, None)
        if got is not None:
            pieces += got
        return got

    def pad_sets(value, wait):
        columns = pl.BlockSpec((token_rows, CHUNK), lambda i, _: (0, i))
        kernel = call(
            functools.partial(pad_body, sets=sets),
            (dim // CHUNK,),
            [columns],
            pl.BlockSpec((slots * SET_ROWS, CHUNK), lambda i, _: (0, i)),
            shape((slots * SET_ROWS, dim), bf16),
            [pltpu.VMEM((token_rows + 16, CHUNK), f32)],
            "pad",
        )
        return order.run(kernel, value, wait=wait)

    next_step(attn_steps, attn_pieces)
    x_rows = pad_sets(tokens, shards_x)
    next_step(attn_steps, attn_pieces)
    kernel = call(
        first_low_body,
        (sets_x,),
        [
            pl.BlockSpec((SET_ROWS, dim), lambda i, info: (info[1] * sets_x + i, 0)),
            whole(1, dim),
            whole(1, dim),
        ],
        pl.BlockSpec((SET_ROWS, dim), lambda i, _: (i, 0)),
        shape((rows_x, dim), bf16),
        [],
        "first_low",
    )
    first_low = order.run(kernel, x_rows, row(first_gain), row(first_shift), wait=attn_pieces[1:3])
    next_step(attn_steps, attn_pieces)
    starts = order.after(jnp.pad(offsets, ((0, slots - sets), (0, 0))))
    starts = lax.dynamic_slice_in_dim(starts, x_index * sets_x, sets_x, axis=0)
    positions = jnp.arange(SET_ROWS, dtype=jnp.int32)
    ids = jnp.sum((positions[None, :, None] >= starts[:, None, :]).astype(jnp.int32), axis=-1)
    ids = jnp.where(positions[None, :] < SET_TOKENS, ids, -1)
    key_ids, query_ids = ids[:, :, None], ids[:, None, :]
    cot = pad_sets(cotangent, (attn_pieces[3:5], key_ids, query_ids, mlp_shard))
    while next_step(attn_steps, attn_pieces):
        pass
    mlp_steps = ring.gather_steps(tie(mlp_shard, attn_pieces[-2:]), 0, order)
    next_step(mlp_steps, mlp_pieces)
    count = len(attn_pieces)
    copies = count * chips

    joint = chips * (width + part)
    kernel = call(
        functools.partial(qkv_body, base=base, unit=unit, chips=chips, count=count),
        (2,),
        [pl.BlockSpec((half, dim), lambda i, _: (i, 0)), whole(1, chips * width)] + [ANY] * count,
        [pl.BlockSpec((half, chips * width), lambda i, _: (i, 0)), HBM],
        [shape((rows_x, chips * width), bf16), shape((dim, joint), bf16)],
        [pltpu.VMEM((dim, joint), bf16), sem((copies,)), sem],
        "qkv",
    )
    qkv, weights = order.run(kernel, first_low, jnp.concatenate(bias_x, axis=1), *attn_pieces)
    order.due = mlp_pieces[-2:]
    both_weights = [weights, partner(order.after(weights), chips)]

    order.due = ()
    next_step(mlp_steps, mlp_pieces)
    kernel = call(
        attend_body,
        (sets_x, groups),
        [
            pl.BlockSpec((SET_ROWS, 3 * LANES), lambda s, i, _: (s, i)),
            pl.BlockSpec((1, SET_ROWS, 1), lambda s, i, _: (s, 0, 0)),
            pl.BlockSpec((1, 1, SET_ROWS), lambda s, i, _: (s, 0, 0)),
        ],
        [
            pl.BlockSpec((SET_ROWS, LANES), lambda s, i, _: (s, i)),
            pl.BlockSpec((1, 1, 2, SET_ROWS), lambda s, i, _: (s, i, 0, 0)),
        ],
        [
            shape((rows_x, att_width), bf16),
            shape((sets_x, groups, 2, SET_ROWS), f32),
        ],
        [pltpu.VMEM((SET_ROWS, SET_ROWS), f32)],
        "attend",
    )
    attended, logs = order.run(kernel, qkv, key_ids, query_ids)
    order.due = [*mlp_pieces[-2:], both_weights[1]]
    attended_other = partner(order.after(attended), chips)
    order.due = ()
    next_step(mlp_steps, mlp_pieces)

    own_half = lambda *dims: pl.BlockSpec(dims, lambda i, info: (info[0], 0))
    own_place = lambda *dims: pl.BlockSpec(dims, lambda i, info: (info[place_base], 0))
    proj_scratch = [pltpu.VMEM((dim, 2 * att_width), bf16), sem((2 * chips,))]
    kernel = call(
        functools.partial(proj_norm_body, chips=chips),
        (1,),
        [own_half(half, att_width)] * 2 + [own_place(half, dim)] + [whole(1, dim)] * 3 + [HBM] * 2,
        [whole(half, dim), whole(half, dim)],
        [shape((half, dim), f32), shape((half, dim), bf16)],
        proj_scratch,
        "proj_norm",
    )
    residual, second_low = order.run(
        kernel,
        attended,
        attended_other,
        x_rows,
        row(proj_bias),
        row(second_gain),
        row(second_shift),
        *both_weights,
    )
    order.due = mlp_pieces[-2:]
    second_low = order.after(second_low)
    order.due = ()
    seconds = {(0, 0): second_low, (0, 1): partner(second_low, chips)}
    for step in range(1, chips):
        seconds[(step, 0)] = across(second_low, step, chips)
    while next_step(mlp_steps, mlp_pieces):
        pass

    def feed(group, gots=()):
        parts = len(group)
        first = keys.index(group[0])
        kernel = call(
            functools.partial(
                mlp_body, base=base, unit=unit, count=count, parts=parts, adds=len(gots) // 2
            ),
            (parts,),
            [
                pl.BlockSpec((half, dim), lambda i, info: (info[place_base + first + i], 0)),
                whole(1, ff),
            ]
            + [HBM] * (count + parts)
            + [whole(half, dim)] * len(gots),
            [pl.BlockSpec((half, ff), lambda i, _: (i, 0))] * 2
            + [whole(half, dim)] * (2 * parts)
            + [whole(1, ff)],
            [shape((parts * half, ff), bf16)] * 2
            + [shape((half, dim), bf16)] * (2 * parts)
            + [shape((1, ff), f32)],
            [
                pltpu.VMEM((dim, ff), bf16),
                pltpu.VMEM((dim, ff), bf16),
                pltpu.VMEM((parts, half, dim), bf16),
                sem((2 * count,)),
                sem((parts,)),
            ],
            "mlp",
        )
        outs = order.run(
            kernel,
            cot,
            row(expand_bias),
            *mlp_pieces,
            *[seconds[key] for key in group],
            *gots,
        )
        backs, rows = outs[2 : 2 + parts], outs[2 + parts : 2 + 2 * parts]
        return outs[0], outs[1], list(backs), list(rows), outs[-1]

    first = feed(near)
    for step in range(1, chips):
        seconds[(step, 1)] = partner(order.after(seconds[(step, 0)]), chips)
    other = feed(far_other)
    gots = []
    for back, out in zip(other[2], other[3]):
        gots += [partner(back, chips), partner(out, chips)]
    own = feed(far_own, gots)
    feeds = [first, other, own]

    def along_x(own, sums):
        terms = [own[0], partner(own[1], chips)]
        return terms + [across(value, chips - 1 - i, chips) for i, value in enumerate(sums)]

    back_terms = along_x(first[2], own[2])
    expand_bias_grad = (first[4] + other[4] + own[4]).reshape(ff)
    span = 2 * CHUNK
    total_rows = len(keys) * half
    kernel = call(
        functools.partial(mlp_grad_body, cot_base=place_base, parts=len(keys), groups=3),
        (2, dim // span),
        [HBM] * (7 + len(keys)),
        pl.BlockSpec((span, ff), lambda p, i, _: (i, p)),
        shape((dim, 2 * ff), bf16),
        [
            pltpu.VMEM((2, total_rows, dim), bf16),
            pltpu.VMEM((2, total_rows, ff), bf16),
            sem((2, len(keys) + 3)),
        ],
        "mlp_grad",
    )
    mlp_grad = order.run(
        kernel,
        cot,
        *[seconds[key] for key in keys],
        *[outs[0] for outs in feeds],
        *[outs[1] for outs in feeds],
    )
    mlp_ring = ring.scatter_steps(mlp_grad, ranks, order)
    mlp_due = next(mlp_ring)

    step_rows = row_step(half)
    cot_rows = pl.BlockSpec(
        (step_rows, dim), lambda i, info: (info[place_base] * (half // step_rows) + i, 0)
    )
    plain_rows = lambda count: pl.BlockSpec((step_rows, count), lambda i, _: (i, 0))
    kernel = call(
        functools.partial(residual_back_body, parts=len(back_terms), chips=chips),
        (half // step_rows,),
        [plain_rows(dim), cot_rows, whole(1, dim)]
        + [plain_rows(dim)] * len(back_terms)
        + [HBM] * 2,
        [plain_rows(dim)] * 2 + [plain_rows(att_width)] * 2 + [whole(8, dim)],
        [
            shape((half, dim), f32),
            shape((half, dim), bf16),
            shape((half, att_width), bf16),
            shape((half, att_width), bf16),
            shape((8, dim), f32),
        ],
        proj_scratch,
        "residual_back",
    )
    grad_residual, residual_low, grad_own, grad_send, sums_two = order.run(
        kernel, residual, cot, row(second_gain), *back_terms, *both_weights
    )
    order.due = mlp_due
    grad_got = partner(order.after(grad_send), chips)
    residual_other = partner(order.after(residual_low), chips)
    order.due = ()
    mlp_due = next(mlp_ring)
    if chips == 2:
        out_near = order.after(residual) + shrink_bias + first[3][0].astype(f32)
        out_near = (out_near + partner(order.after(first[3][1]), chips).astype(f32)).astype(bf16)
        out_far = own[3][0]
        cut = half // 2
        out_sends = iter([out_far[:cut], out_far[cut:], out_near[:cut], out_near[cut:]])
        out_gots = [across(order.after(next(out_sends)), 1, chips)]
    else:
        out_terms = along_x(order.after(first[3]), order.after(own[3]))

    def attend_back(b):
        half_block = lambda j: pl.BlockSpec(
            (row_step(half), LANES), lambda i, s, _: (lax.rem(2 * s + j, sets_x), b * pairs + i)
        )
        kernel = call(
            functools.partial(attend_back_body, first_half=sets_x),
            (pairs, sets_x),
            [
                pl.BlockSpec((SET_ROWS, 3 * LANES), lambda i, s, _: (s, b * pairs + i)),
                pl.BlockSpec((1, SET_ROWS, 1), lambda i, s, _: (s, 0, 0)),
                pl.BlockSpec((1, 1, SET_ROWS), lambda i, s, _: (s, 0, 0)),
                pl.BlockSpec((1, 1, 2, SET_ROWS), lambda i, s, _: (s, b * pairs + i, 0, 0)),
                half_block(0),
                half_block(0),
                half_block(1),
                half_block(1),
            ],
            [
                pl.BlockSpec((SET_ROWS, 3 * LANES), lambda i, s, _: (s, i)),
                pl.BlockSpec((1, 1, 3 * LANES), lambda i, s, _: (i, 0, 0)),
            ],
            [shape((rows_x, width), bf16), shape((pairs, 1, 3 * LANES), f32)],
            [pltpu.VMEM((sets_x, SET_ROWS, SET_ROWS), f32)],
            "attend_back",
        )
        ids = key_ids, query_ids
        return order.run(kernel, qkv, *ids, logs, grad_own, grad_got, grad_own, grad_got)

    def qkv_grad(b, before):
        columns = lambda count: pl.BlockSpec((count, span), lambda i, _: (0, i))
        kernel = call(
            qkv_grad_body,
            (dim // span,),
            [
                columns(rows_x),
                whole(rows_x, width),
                columns(half),
                columns(half),
                pl.BlockSpec((half, part), lambda i, info: (info[0], b)),
                pl.BlockSpec((half, part), lambda i, info: (1 - info[0], b)),
            ]
            + [ANY] * len(before),
            pl.BlockSpec((span, width + part), lambda i, _: (i, b)),
            shape((dim, joint), bf16),
            [],
            "qkv_grad",
            {7 + i: i for i in range(len(before))},
        )
        return order.run(
            kernel,
            first_low,
            grads_qkv[b],
            residual_low,
            residual_other,
            attended,
            attended,
            *before,
        )

    def out_due(i):
        if chips != 2 or i > 3:
            return ()
        if i < 3:
            out_gots.append(across(order.after(next(out_sends)), 1, chips))
        return out_gots[i]

    grads_qkv, grads_other, qkv_sums, begun = {}, {}, {}, ()
    for b in range(1, chips):
        grads_qkv[b], qkv_sums[b] = attend_back(b)
        order.due = mlp_due, residual_other, out_due(b - 1)
        grads_other[b] = partner(order.after(grads_qkv[b]), chips)
        order.due = ()
        mlp_due = next(mlp_ring, ())
        begun = (qkv_grad(b, begun),)
    grads_qkv[0], qkv_sums[0] = attend_back(0)
    order.due = mlp_due, [grads_other[b] for b in range(1, chips)], out_due(1)
    grads_other[0] = partner(order.after(grads_qkv[0]), chips)
    order.due = ()
    mlp_due = next(mlp_ring, ())
    attn_ring = ring.scatter_steps(qkv_grad(0, begun), ranks, order)
    order.due = [grads_other[b] for b in range(chips)]
    next(attn_ring)
    order.due = ()
    for mlp_grad in mlp_ring:
        pass
    expand_part, shrink_part = mlp_grad[:, :ff], mlp_grad[:, ff:].T
    order.due = out_due(2)
    attn_due = next(attn_ring)
    order.due = ()

    kernel = call(
        functools.partial(first_norm_body, chips=chips),
        (1,),
        [own_half(half, width)] * (2 * chips)
        + [own_place(half, dim), whole(half, dim), whole(1, dim)]
        + [HBM] * 2,
        [whole(half, dim), whole(8, dim)],
        [shape((half, dim), bf16), shape((8, dim), f32)],
        [
            pltpu.VMEM((2 * chips, dim, width), bf16),
            pltpu.VMEM((2 * chips, half, width), bf16),
            pltpu.VMEM((half, dim), f32),
            sem((2 * chips,)),
        ],
        "first_norm",
    )
    tokens_low, sums_one = order.run(
        kernel,
        *[grads_qkv[b] for b in range(chips)],
        *[grads_other[b] for b in range(chips)],
        x_rows,
        grad_residual,
        row(first_gain),
        *both_weights,
    )

    def assemble(rows, dtype):
        block = lambda count, at: pl.BlockSpec((count, CHUNK), lambda i, _: (at, i))
        kernel = call(
            functools.partial(assemble_body, base=place_base, sets=sets),
            (dim // CHUNK,),
            [block(half, rows[key][1]) for key in keys],
            block(token_rows, 0),
            shape((token_rows, dim), dtype),
            [
                pltpu.VMEM((slots * SET_ROWS, CHUNK), f32),
                pltpu.VMEM((token_rows + 16, CHUNK), f32),
            ],
            "assemble",
        )
        return order.run(kernel, *[rows[key][0] for key in keys])

    order.due = attn_due, out_due(3)
    tokens_low = order.after(tokens_low)
    order.due = ()
    grads, outs = {(0, 0): (tokens_low, 0)}, {}
    for step in range(1, chips):
        grads[(step, 0)] = across(tokens_low, step, chips), 0
    next(attn_ring)
    if chips == 2:
        out_rows = jnp.concatenate([out_near, out_far]).astype(f32)
        out_rows = out_rows + jnp.concatenate(order.after(out_gots)).astype(f32)
    else:
        out_rows = order.after(residual) + shrink_bias
        for term in out_terms:
            out_rows = out_rows + term.astype(f32)
        low = out_rows.astype(bf16)
        out_rows = jnp.concatenate([low] + [across(low, step, chips) for step in range(1, chips)])
    out_rows = out_rows.astype(bf16)
    out_other = partner(out_rows, chips)
    for step in range(chips):
        outs[(step, 0)], outs[(step, 1)] = (out_rows, step), (out_other, step)

    bias_sums = jnp.stack([qkv_sums[b] for b in range(chips)]).reshape(chips, pairs, 3, LANES)
    bias_sums = jnp.stack([bias_sums[:, :, 0], bias_sums[:, :, 2]], axis=1)
    hidden_sums = jnp.pad(expand_bias_grad, (0, -ff % dim)).reshape(-1, dim)
    shared = jnp.concatenate([sums_one[0:2], sums_two[2:3], sums_two[0:2], sums_two[3:4]])
    shared = shared + partner(shared, chips)
    small = jnp.concatenate([shared, bias_sums.reshape(-1, dim), hidden_sums])
    bits = [1 << i for i in range(ring.count.bit_length() - 1)]

    def add_ranks(small, bit):
        pairs = [(r, r ^ bit) for r in range(ring.count)]
        return small + lax.ppermute(order.after(small), "dp", pairs)

    def add_chips(small):
        shared = small[:6]
        own, *others = small[6:7].reshape(chips, 2 * part)
        if chips == 2:
            sent = jnp.concatenate([shared.reshape(-1), others[0]])
            got = across(order.after(sent), 1, chips)
            shared = shared + got[: 6 * dim].reshape(6, dim)
            own = own + got[6 * dim :]
        else:
            bit = 1
            while bit < chips:
                flips = [(m, m ^ (2 * bit)) for m in range(2 * chips)]
                shared = shared + lax.ppermute(shared, "mp", flips)
                bit *= 2
            for step in range(1, chips):
                own = own + across(others[step - 1], chips - step, chips)
        own = jnp.pad(own, (0, dim - 2 * part)).reshape(1, dim)
        return jnp.concatenate([shared, own, small[7:]])

    outputs = assemble(outs, bf16)
    small = add_ranks(small, bits[0])
    order.hold = (small, expand_part, shrink_part)
    next(attn_ring)
    grads[(0, 1)] = partner(order.after(tokens_low), chips), 0
    for step in range(1, chips):
        grads[(step, 1)] = partner(order.after(grads[(step, 0)][0]), chips), 0
    small = add_chips(small)
    grad_tokens = assemble(grads, f32)
    for attn_sum in attn_ring:
        pass
    for bit in bits[1:]:
        small = add_ranks(small, bit)
    shared = small[:6]
    bias_own = small[6, : 2 * part].reshape(2, part)
    expand_bias_grad = small[7:].reshape(-1)[:ff]
    attn_part = attn_sum[:, : width + part]
    for step in range(1, chips):
        sent = attn_sum[:, step * (width + part) : (step + 1) * (width + part)].astype(bf16)
        attn_part = attn_part + across(sent, chips - step, chips).astype(f32)

    qkv_part = attn_part[:, :width].reshape(unit_rows, pairs, 3, LANES)
    qkv_part = qkv_part.transpose(0, 2, 1, 3).reshape(unit_rows, 3, part)
    return (
        outputs,
        grad_tokens,
        shared[0],
        shared[1],
        qkv_part,
        bias_own,
        attn_part[:, width:].T,
        shared[2],
        shared[3],
        shared[4],
        expand_part,
        expand_bias_grad,
        shrink_part,
        shared[5],
    )


def solution(mesh):
    placed = (
        P("dp", None),
        P("dp", None),
        P(),
        P(),
        P("dp", None, "mp"),
        P(None, "mp"),
        P("mp", "dp"),
        P(),
        P(),
        P(),
        P("dp", "mp"),
        P("mp"),
        P("mp", "dp"),
        P(),
        P("dp", None),
    )
    return jax.shard_map(
        shards,
        mesh=mesh,
        in_specs=placed,
        out_specs=(
            P("dp", None),
            P("dp", None),
            P(),
            P(),
            P("dp", None, "mp"),
            P(None, "mp"),
            P("mp", "dp"),
            P(),
            P(),
            P(),
            P("dp", "mp"),
            P("mp"),
            P("mp", "dp"),
            P(),
        ),
        check_vma=False,
    )
```

profile of v0, /device:TPU:0, one launch (start us, length us, event | category | flops | bytes accessed | tf_op | source)
XLA Modules:
  0.0 356.7 jit_solution(17185427113724983595)
XLA Ops:
  3.1 3.0 collective-permute-start
  6.9 5.5 %collective-permute-done = bf16[128,1024]{1,0:T(8,128)(2,1)S(1)} collective-permute-done((bf16[128,1024]{1,0:T(8,128)(2,1)S(1)}, bf16[128,1024]{1,0:T(8,128)(2,1)S(1)}, u32[]{:S(2)}, u32[]{:S(2)}) %collective-permute-start) | collective-permute-done | bytes 262176 | tf_op jit(solution)/shard_map/ppermute | solution.py:221
  14.5 2.2 copy-done.24
  16.7 3.0 pad.92.x_ref.refs_4_
  19.7 2.1 copy-done.8
  21.8 3.8 %collective-permute-done.1.rest_1_ = bf16[2,128,1024]{2,1,0:T(8,128)(2,1)S(1)} collective-permute-done((bf16[2,128,1024]{2,1,0:T(8,128)(2,1)S(1)}, bf16[2,128,1024]{2,1,0:T(8,128)(2,1)S(1)}, u32[]{:S(2)}, u32[]{:S(2)}) %collective-permute-start.1) | collective-permute-done | bytes 524320 | tf_op jit(solution)/shard_map/ppermute | solution.py:125
  30.0 2.2 copy-done.9
  32.2 2.1 first_low.1.x_ref.first_ref
  34.5 4.1 %collective-permute-done.3.rest_3_ = bf16[2,128,1024]{2,1,0:T(8,128)(2,1)} collective-permute-done((bf16[2,128,1024]{2,1,0:T(8,128)(2,1)S(1)}, bf16[2,128,1024]{2,1,0:T(8,128)(2,1)}, u32[]{:S(2)}, u32[]{:S(2)}) %collective-permute-start.3) | collective-permute-done | bytes 524320 | tf_op jit(solution)/shard_map/ppermute | solution.py:125
  44.4 2.2 copy-done.25
  46.6 3.0 pad.93.cot_ref
  49.7 2.0 copy-done.7
  55.7 4.6 %collective-permute-done.8.rest_7_ = bf16[2,64,1024]{2,1,0:T(8,128)(2,1)S(1)} collective-permute-done((bf16[2,64,1024]{2,1,0:T(8,128)(2,1)S(1)}, bf16[2,64,1024]{2,1,0:T(8,128)(2,1)S(1)}, u32[]{:S(2)}, u32[]{:S(2)}) %collective-permute-start.8) | collective-permute-done | bytes 262176 | tf_op jit(solution)/shard_map/ppermute | solution.py:125
  62.9 2.8 collective-permute-start.10
  67.4 2.1 collective-permute-done.5
  71.9 6.9 %qkv.1 = (bf16[1056,1536]{1,0:T(8,128)(2,1)S(1)}, bf16[1024,2048]{1,0:T(8,128)(2,1)S(1)}) custom-call(s32[24]{0:T(128)S(1)} %concatenate.35.info, bf16[1056,1024]{1,0:T(8,128)(2,1)S(1)} %first_low.1.x_ref.first_ref, f32[1,1536]{1,0:T(1,128)S(1)} %pad_maximum_fusion.7.bias_ref, bf16[2,128,1024]{2,1,0:T(8,128)(2,1)S(1)} %pad_maximum_fusion.rest_0_, ...), custom_call_target="tpu_custom_call" | custom-call | flops 1 | bytes 1 | tf_op jit(solution)/shard_map/qkv/pallas_call | solution.py:88
  78.9 2.1 collective-permute-start.12
  81.0 12.3 %attend.1 = (bf16[1056,512]{1,0:T(8,128)(2,1)S(1)}, f32[3,4,2,352]{3,2,1,0:T(2,128)S(1)}) custom-call(s32[24]{0:T(128)S(1)} %concatenate.35.info, bf16[1056,1536]{1,0:T(8,128)(2,1)S(1)} %get-tuple-element.188.qkv_ref, s32[3,352,1]{2,1,0:T(8,128)S(1)} %broadcast_select_fusion.key_ids, s32[3,1,352]{2,1,0:T(1,128)S(1)} %broadcast_select_fusion.1.query_ids), custom_call_target="tpu_custom_call" | custom-call | flops 1 | bytes 1 | tf_op jit(solution)/shard_map/attend/pallas_call | solution.py:88
  98.0 3.3 proj_norm.1
  102.7 6.9 %collective-permute-done.16.rest_5_ = bf16[128,2048]{1,0:T(8,128)(2,1)S(1)} collective-permute-done((bf16[128,2048]{1,0:T(8,128)(2,1)S(1)}, bf16[128,2048]{1,0:T(8,128)(2,1)S(1)}, u32[]{:S(2)}, u32[]{:S(2)}) %collective-permute-start.16) | collective-permute-done | bytes 524320 | tf_op jit(solution)/shard_map/ppermute | solution.py:125
  114.9 6.4 %collective-permute-done.18.rest_7_ = bf16[64,2048]{1,0:T(8,128)(2,1)S(1)} collective-permute-done((bf16[64,2048]{1,0:T(8,128)(2,1)S(1)}, bf16[64,2048]{1,0:T(8,128)(2,1)S(1)}, u32[]{:S(2)}, u32[]{:S(2)}) %collective-permute-start.18) | collective-permute-done | bytes 262176 | tf_op jit(solution)/shard_map/ppermute | solution.py:125
  123.2 19.3 %mlp.3 = (bf16[1056,1024]{1,0:T(8,128)(2,1)}, bf16[1056,1024]{1,0:T(8,128)(2,1)}, bf16[528,1024]{1,0:T(8,128)(2,1)}, bf16[528,1024]{1,0:T(8,128)(2,1)}, bf16[528...) custom-call(s32[24]{0:T(128)} %copy-done.31, bf16[2112,1024]{1,0:T(8,128)(2,1)} %copy-done.7, ...), custom_call_target="tpu_custom_call" | custom-call | flops 1 | bytes 1 | tf_op jit(solution)/shard_map/mlp/pallas_call | solution.py:88
  142.6 2.7 collective-permute-done.22.rest_9_.rest_2_
  146.4 10.8 %mlp.4 = (bf16[528,1024]{1,0:T(8,128)(2,1)}, bf16[528,1024]{1,0:T(8,128)(2,1)}, bf16[528,1024]{1,0:T(8,128)(2,1)}, bf16[528,1024]{1,0:T(8,128)(2,1)}, f32[1,1024]{1,0:T(1,128)}) custom-call(s32[24]{0:T(128)} %copy-done.31, bf16[2112,1024]{1,0:T(8,128)(2,1)} %copy-done.7, f32[1,1024]{1,0:T(1,128)} %bitcast.83, bf16[128,2048]{1,0:T(8,128)(2,1)} %pad_maximum_fusion.1.rest_0_, ...), custom_call_target="tpu_custom_call" | custom-call | flops 1 | bytes 1 | tf_op jit(solution)/shard_map/mlp/pallas_call | solution.py:88
  157.9 2.3 collective-permute-done.23.rest_10_
  160.2 3.1 collective-permute-done.24.rest_11_
  164.3 11.5 %mlp.5 = (bf16[528,1024]{1,0:T(8,128)(2,1)}, bf16[528,1024]{1,0:T(8,128)(2,1)}, bf16[528,1024]{1,0:T(8,128)(2,1)}, bf16[528,1024]{1,0:T(8,128)(2,1)}, f32[1,1024]{1,0:T(1,128)}) custom-call(s32[24]{0:T(128)} %copy-done.31, bf16[2112,1024]{1,0:T(8,128)(2,1)} %copy-done.7, f32[1,1024]{1,0:T(1,128)} %bitcast.84, bf16[128,2048]{1,0:T(8,128)(2,1)} %pad_maximum_fusion.1.rest_0_, ...), custom_call_target="tpu_custom_call" | custom-call | flops 1 | bytes 1 | tf_op jit(solution)/shard_map/mlp/pallas_call | solution.py:88
  176.5 16.5 %mlp_grad.1.ahead_ref.behind_ref.own_ref = bf16[1024,2048]{1,0:T(8,128)(2,1)} custom-call(s32[24]{0:T(128)} %copy-done.31, bf16[2112,1024]{1,0:T(8,128)(2,1)} %copy-done.7, bf16[528,1024]{1,0:T(8,128)(2,1)} %copy-done.23, bf16[528,1024]{1,0:T(8,128)(2,1)} %copy-done.51, bf16[528,1024]{1,0:T(8,128)(2,1)} %copy-done.52, bf16[528,1024]{1,0:T(8,128)(2,1)} %copy-done.55, ...), custom_call_target="tpu_custom_call" | custom-call | flops 1 | bytes 1 | tf_op jit(solution)/shard_map/mlp_grad/pallas_call | solution.py:88
  193.0 2.2 copy-done.5
  197.9 4.3 %collective-permute-done.26.rest_2_ = bf16[528,1024]{1,0:T(8,128)(2,1)} collective-permute-done((bf16[528,1024]{1,0:T(8,128)(2,1)}, bf16[528,1024]{1,0:T(8,128)(2,1)}, u32[]{:S(2)}, u32[]{:S(2)}) %collective-permute-start.26) | collective-permute-done | bytes 1081376 | tf_op jit(solution)/shard_map/ppermute | solution.py:221
  205.0 6.3 %residual_back.1 = (f32[528,1024]{1,0:T(8,128)S(1)}, bf16[528,1024]{1,0:T(8,128)(2,1)S(1)}, bf16[528,512]{1,0:T(8,128)(2,1)S(1)}, bf16[528,512]{1,0:T(8,128)(2,1)S(1)}, f32[8,1024]{1,0:T(8,128)S(1)}) custom-call(s32[24]{0:T(128)S(1)} %copy-done.32, f32[528,1024]{1,0:T(8,128)S(1)} %copy-done.19, bf16[2112,1024]{1,0:T(8,128)(2,1)S(1)} %bitcast.63, ...), custom_call_target="tpu_custom_call" | custom-call | flops 1 | bytes 1 | tf_op jit(solution)/shard_map/residual_back/pallas_call | solution.py:88
  216.7 9.8 %attend_back.2 = (bf16[1056,768]{1,0:T(8,128)(2,1)S(1)}, f32[2,1,384]{2,1,0:T(1,128)S(1)}) custom-call(s32[24]{0:T(128)S(1)} %copy-done.32, bf16[1056,1536]{1,0:T(8,128)(2,1)S(1)} %copy-done.17, s32[3,352,1]{2,1,0:T(8,128)S(1)} %broadcast_select_fusion.key_ids, s32[3,1,352]{2,1,0:T(1,128)S(1)} %broadcast_select_fusion.1.query_ids, ...), custom_call_target="tpu_custom_call" | custom-call | flops 1 | bytes 1 | tf_op jit(solution)/shard_map/attend_back/pallas_call | solution.py:88
  233.8 4.3 %qkv_grad.2.rest_0_ = bf16[1024,2048]{1,0:T(8,128)(2,1)S(1)} custom-call(s32[24]{0:T(128)S(1)} %copy-done.32, bf16[1056,1024]{1,0:T(8,128)(2,1)S(1)} %copy-done.15, bf16[1056,768]{1,0:T(8,128)(2,1)S(1)} %get-tuple-element.263.grad_ref.refs_1_, bf16[528,1024]{1,0:T(8,128)(2,1)S(1)} %get-tuple-element.245.own_ref, ...), custom_call_target="tpu_custom_call" | custom-call | flops 1 | bytes 1 | tf_op jit(solution)/shard_map/qkv_grad/pallas_call | solution.py:88
  238.1 9.8 %attend_back.3 = (bf16[1056,768]{1,0:T(8,128)(2,1)S(1)}, f32[2,1,384]{2,1,0:T(1,128)S(1)}) custom-call(s32[24]{0:T(128)S(1)} %copy-done.32, bf16[1056,1536]{1,0:T(8,128)(2,1)S(1)} %copy-done.17, s32[3,352,1]{2,1,0:T(8,128)S(1)} %broadcast_select_fusion.key_ids, s32[3,1,352]{2,1,0:T(1,128)S(1)} %broadcast_select_fusion.1.query_ids, ...), custom_call_target="tpu_custom_call" | custom-call | flops 1 | bytes 1 | tf_op jit(solution)/shard_map/attend_back/pallas_call | solution.py:88
  256.1 4.3 %qkv_grad.3.ahead_ref.behind_ref.own_ref = bf16[1024,2048]{1,0:T(8,128)(2,1)S(1)} custom-call(s32[24]{0:T(128)S(1)} %copy-done.32, bf16[1056,1024]{1,0:T(8,128)(2,1)S(1)} %copy-done.15, bf16[1056,768]{1,0:T(8,128)(2,1)S(1)} %get-tuple-element.265.grad_ref.refs_0_, bf16[528,1024]{1,0:T(8,128)(2,1)S(1)} %get-tuple-element.245.own_ref, ...), custom_call_target="tpu_custom_call", output_to_operand_aliasing={{}: (7, {})} | custom-call | flops 1 | bytes 1 | tf_op jit(solution)/shard_map/qkv_grad/pallas_call | solution.py:88
  263.2 5.7 %collective-permute-done.35.got_ahead = bf16[128,2048]{1,0:T(8,128)(2,1)S(1)} collective-permute-done((bf16[128,2048]{1,0:T(8,128)(2,1)S(1)}, bf16[128,2048]{1,0:T(8,128)(2,1)S(1)}, u32[]{:S(2)}, u32[]{:S(2)}) %collective-permute-start.35) | collective-permute-done | bytes 524320 | tf_op jit(solution)/shard_map/ppermute | solution.py:125
  271.7 2.0 collective-permute-done.41.got_ahead
  278.5 11.9 %first_norm.1 = (bf16[528,1024]{1,0:T(8,128)(2,1)}, f32[8,1024]{1,0:T(8,128)}) custom-call(s32[24]{0:T(128)} %copy-done.31, bf16[1056,768]{1,0:T(8,128)(2,1)} %copy-done.22, bf16[1056,768]{1,0:T(8,128)(2,1)} %copy-done.21, bf16[1056,768]{1,0:T(8,128)(2,1)} %copy-done.60, bf16[1056,768]{1,0:T(8,128)(2,1)} %copy-done.59, bf16[2112,1024]{1,0:T(8,128)(2,1)} %copy-done.8, ...), custom_call_target="tpu_custom_call" | custom-call | flops 1 | bytes 1 | tf_op jit(solution)/shard_map/first_norm/pallas_call | solution.py:88
  290.5 2.1 ring_add.10
  293.6 2.1 add_convert_fusion.refs_0_.refs_3_
  302.5 5.8 %assemble.2 = bf16[2070,1024]{1,0:T(8,128)(2,1)} custom-call(s32[24]{0:T(128)S(1)} %copy-done.33, bf16[1056,1024]{1,0:T(8,128)(2,1)S(1)} %add_convert_fusion.refs_0_.refs_3_, bf16[1056,1024]{1,0:T(8,128)(2,1)} %collective-permute-done.48.refs_1_.refs_2_, bf16[1056,1024]{1,0:T(8,128)(2,1)} %collective-permute-done.48.refs_1_.refs_2_, ...), custom_call_target="tpu_custom_call" | custom-call | flops 1 | bytes 1 | tf_op jit(solution)/shard_map/assemble/pallas_call | solution.py:88
  309.8 5.7 %collective-permute-done.50 = f32[8,1024]{1,0:T(8,128)S(1)} collective-permute-done((f32[8,1024]{1,0:T(8,128)S(1)}, f32[8,1024]{1,0:T(8,128)S(1)}, u32[]{:S(2)}, u32[]{:S(2)}) %collective-permute-start.50) | collective-permute-done | bytes 32800 | tf_op jit(solution)/shard_map/ppermute | solution.py:1140
  317.9 4.7 %collective-permute-done.54.refs_3_ = bf16[528,1024]{1,0:T(8,128)(2,1)} collective-permute-done((bf16[528,1024]{1,0:T(8,128)(2,1)}, bf16[528,1024]{1,0:T(8,128)(2,1)}, u32[]{:S(2)}, u32[]{:S(2)}) %collective-permute-start.54) | collective-permute-done | bytes 1081376 | tf_op jit(solution)/shard_map/ppermute | solution.py:221
  327.2 6.3 %assemble.3 = f32[2070,1024]{1,0:T(8,128)} custom-call(s32[24]{0:T(128)S(1)} %copy-done.33, bf16[528,1024]{1,0:T(8,128)(2,1)S(1)} %copy-done.27, bf16[528,1024]{1,0:T(8,128)(2,1)S(1)} %collective-permute-done.53.refs_1_, bf16[528,1024]{1,0:T(8,128)(2,1)S(1)} %collective-permute-done.55.refs_2_, bf16[528,1024]{1,0:T(8,128)(2,1)} %collective-permute-done.54.refs_3_), custom_call_target="tpu_custom_call" | custom-call | flops 1 | bytes 1 | tf_op jit(solution)/shard_map/assemble/pallas_call | solution.py:88
  333.5 5.1 %collective-permute-done.57.got_ahead = bf16[128,2048]{1,0:T(8,128)(2,1)} collective-permute-done((bf16[128,2048]{1,0:T(8,128)(2,1)}, bf16[128,2048]{1,0:T(8,128)(2,1)}, u32[]{:S(2)}, u32[]{:S(2)}) %collective-permute-start.57) | collective-permute-done | bytes 524320 | tf_op jit(solution)/shard_map/ppermute | solution.py:125
  342.3 2.4 collective-permute-done.59
  344.7 2.5 collective-permute-start.60
  350.9 3.9 %collective-permute-done.61 = bf16[128,1024]{1,0:T(8,128)(2,1)S(1)} collective-permute-done((bf16[128,1024]{1,0:T(8,128)(2,1)S(1)}, bf16[128,1024]{1,0:T(8,128)(2,1)S(1)}, u32[]{:S(2)}, u32[]{:S(2)}) %collective-permute-start.61) | collective-permute-done | bytes 262176 | tf_op jit(solution)/shard_map/ppermute | solution.py:221
  (345 shorter events, 104.8 us)
Async XLA Ops:
  3.1 9.3 %collective-permute-start = (bf16[128,1024]{1,0:T(8,128)(2,1)S(1)}, bf16[128,1024]{1,0:T(8,128)(2,1)S(1)}, u32[]{:S(2)}, u32[]{:S(2)}) collective-permute-start(bf16[128,1024]{1,0:T(8,128)(2,1)S(1)} %get-tuple-element.389), channel_id=1, source_target_pairs={{0,2},{1,3},{2,0},{3,1},{4,6},{5,7},{6,4},{7,5},{8,10},{9,11},{10,... | collective-permute-start | bytes 786440 | tf_op jit(solution)/shard_map/ppermute | solution.py:221
  12.5 13.2 %collective-permute-start.1 = (bf16[2,128,1024]{2,1,0:T(8,128)(2,1)S(1)}, bf16[2,128,1024]{2,1,0:T(8,128)(2,1)S(1)}, u32[]{:S(2)}, u32[]{:S(2)}) collective-permute-start(bf16[2,128,1024]{2,1,0:T(8,128)(2,1)S(1)} %pad_maximum_fusion.rest_0_), channel_id=1, source_target_pairs={{4,12},{12,20},{20,28},{28,24},{24,16},{16,8},{8,0},{0,4},{5,13},{... | collective-permute-start | bytes 1572872 | tf_op jit(solution)/shard_map/ppermute | solution.py:125
  14.3 12.6 %collective-permute-start.2 = (bf16[2,128,1024]{2,1,0:T(8,128)(2,1)S(1)}, bf16[2,128,1024]{2,1,0:T(8,128)(2,1)}, u32[]{:S(2)}, u32[]{:S(2)}) collective-permute-start(bf16[2,128,1024]{2,1,0:T(8,128)(2,1)S(1)} %pad_maximum_fusion.rest_0_), channel_id=1, source_target_pairs={{4,0},{12,4},{20,12},{28,20},{24,28},{16,24},{8,16},{0,8},{5,1},{1... | collective-permute-start | bytes 1572872 | tf_op jit(solution)/shard_map/ppermute | solution.py:128
  26.9 11.7 %collective-permute-start.3 = (bf16[2,128,1024]{2,1,0:T(8,128)(2,1)S(1)}, bf16[2,128,1024]{2,1,0:T(8,128)(2,1)}, u32[]{:S(2)}, u32[]{:S(2)}) collective-permute-start(bf16[2,128,1024]{2,1,0:T(8,128)(2,1)S(1)} %collective-permute-done.1.rest_1_), channel_id=1, source_target_pairs={{4,12},{12,20},{20,28},{28,24},{24,16},{16,8},{8,0},{0,4},{5,13},{... | collective-permute-start | bytes 1572872 | tf_op jit(solution)/shard_map/ppermute | solution.py:125
  28.5 11.6 %collective-permute-start.4 = (bf16[2,128,1024]{2,1,0:T(8,128)(2,1)}, bf16[2,128,1024]{2,1,0:T(8,128)(2,1)}, u32[]{:S(2)}, u32[]{:S(2)}) collective-permute-start(bf16[2,128,1024]{2,1,0:T(8,128)(2,1)} %collective-permute-done.2.rest_2_), channel_id=1, source_target_pairs={{4,0},{12,4},{20,12},{28,20},{24,28},{16,24},{8,16},{0,8},{5,1},{1... | collective-permute-start | bytes 1572872 | tf_op jit(solution)/shard_map/ppermute | solution.py:128
  40.1 11.6 %collective-permute-start.6 = (bf16[2,128,1024]{2,1,0:T(8,128)(2,1)}, bf16[2,128,1024]{2,1,0:T(8,128)(2,1)}, u32[]{:S(2)}, u32[]{:S(2)}) collective-permute-start(bf16[2,128,1024]{2,1,0:T(8,128)(2,1)} %collective-permute-done.3.rest_3_), channel_id=1, source_target_pairs={{4,12},{12,20},{20,28},{28,24},{24,16},{16,8},{8,0},{0,4},{5,13},{... | collective-permute-start | bytes 1572872 | tf_op jit(solution)/shard_map/ppermute | solution.py:125
  41.7 11.0 %collective-permute-start.7 = (bf16[2,128,1024]{2,1,0:T(8,128)(2,1)}, bf16[2,128,1024]{2,1,0:T(8,128)(2,1)}, u32[]{:S(2)}, u32[]{:S(2)}) collective-permute-start(bf16[2,128,1024]{2,1,0:T(8,128)(2,1)} %collective-permute-done.4.rest_4_), channel_id=1, source_target_pairs={{4,0},{12,4},{20,12},{28,20},{24,28},{16,24},{8,16},{0,8},{5,1},{1... | collective-permute-start | bytes 1572872 | tf_op jit(solution)/shard_map/ppermute | solution.py:128
  55.3 6.9 %collective-permute-start.9 = (bf16[2,64,1024]{2,1,0:T(8,128)(2,1)S(1)}, bf16[2,64,1024]{2,1,0:T(8,128)(2,1)S(1)}, u32[]{:S(2)}, u32[]{:S(2)}) collective-permute-start(bf16[2,64,1024]{2,1,0:T(8,128)(2,1)S(1)} %slice.189), channel_id=1, source_target_pairs={{4,0},{12,4},{20,12},{28,20},{24,28},{16,24},{8,16},{0,8},{5,1},{1... | collective-permute-start | bytes 786440 | tf_op jit(solution)/shard_map/ppermute | solution.py:128
  62.9 15.9 %collective-permute-start.10 = (bf16[128,2048]{1,0:T(8,128)(2,1)}, bf16[128,2048]{1,0:T(8,128)(2,1)}, u32[]{:S(2)}, u32[]{:S(2)}) collective-permute-start(bf16[128,2048]{1,0:T(8,128)(2,1)} %pad_maximum_fusion.1.rest_0_), channel_id=1, source_target_pairs={{4,12},{12,20},{20,28},{28,24},{24,16},{16,8},{8,0},{0,4},{5,13},{... | collective-permute-start | bytes 1572872 | tf_op jit(solution)/shard_map/ppermute | solution.py:125
  65.8 13.1 %collective-permute-start.11 = (bf16[128,2048]{1,0:T(8,128)(2,1)}, bf16[128,2048]{1,0:T(8,128)(2,1)}, u32[]{:S(2)}, u32[]{:S(2)}) collective-permute-start(bf16[128,2048]{1,0:T(8,128)(2,1)} %pad_maximum_fusion.1.rest_0_), channel_id=1, source_target_pairs={{4,0},{12,4},{20,12},{28,20},{24,28},{16,24},{8,16},{0,8},{5,1},{1... | collective-permute-start | bytes 1572872 | tf_op jit(solution)/shard_map/ppermute | solution.py:128
  78.8 16.4 %collective-permute-start.14 = (bf16[1024,2048]{1,0:T(8,128)(2,1)S(1)}, bf16[1024,2048]{1,0:T(8,128)(2,1)S(1)}, u32[]{:S(2)}, u32[]{:S(2)}) collective-permute-start(bf16[1024,2048]{1,0:T(8,128)(2,1)S(1)} %get-tuple-element.198.rest_0_.rest_3_.refs_7_), channel_id=1, source_target_pairs={{0,1},{1,0},{2,3},{3,2},{4,5},{5,4},{6,7},{7,6},{8,9},{9,8},{10,11... | collective-permute-start | bytes 12582920 | tf_op jit(solution)/shard_map/ppermute | solution.py:225
  78.9 16.1 %collective-permute-start.12 = (bf16[128,2048]{1,0:T(8,128)(2,1)}, bf16[128,2048]{1,0:T(8,128)(2,1)S(1)}, u32[]{:S(2)}, u32[]{:S(2)}) collective-permute-start(bf16[128,2048]{1,0:T(8,128)(2,1)} %collective-permute-done.10.rest_1_), channel_id=1, source_target_pairs={{4,12},{12,20},{20,28},{28,24},{24,16},{16,8},{8,0},{0,4},{5,13},{... | collective-permute-start | bytes 1572872 | tf_op jit(solution)/shard_map/ppermute | solution.py:125
  81.0 14.2 %collective-permute-start.13 = (bf16[128,2048]{1,0:T(8,128)(2,1)}, bf16[128,2048]{1,0:T(8,128)(2,1)S(1)}, u32[]{:S(2)}, u32[]{:S(2)}) collective-permute-start(bf16[128,2048]{1,0:T(8,128)(2,1)} %collective-permute-done.11.rest_2_), channel_id=1, source_target_pairs={{4,0},{12,4},{20,12},{28,20},{24,28},{16,24},{8,16},{0,8},{5,1},{1... | collective-permute-start | bytes 1572872 | tf_op jit(solution)/shard_map/ppermute | solution.py:128
  95.3 14.3 %collective-permute-start.16 = (bf16[128,2048]{1,0:T(8,128)(2,1)S(1)}, bf16[128,2048]{1,0:T(8,128)(2,1)S(1)}, u32[]{:S(2)}, u32[]{:S(2)}) collective-permute-start(bf16[128,2048]{1,0:T(8,128)(2,1)S(1)} %collective-permute-done.12.rest_3_), channel_id=1, source_target_pairs={{4,12},{12,20},{20,28},{28,24},{24,16},{16,8},{8,0},{0,4},{5,13},{... | collective-permute-start | bytes 1572872 | tf_op jit(solution)/shard_map/ppermute | solution.py:125
  97.3 14.0 %collective-permute-start.17 = (bf16[128,2048]{1,0:T(8,128)(2,1)S(1)}, bf16[128,2048]{1,0:T(8,128)(2,1)S(1)}, u32[]{:S(2)}, u32[]{:S(2)}) collective-permute-start(bf16[128,2048]{1,0:T(8,128)(2,1)S(1)} %collective-permute-done.13.rest_4_), channel_id=1, source_target_pairs={{4,0},{12,4},{20,12},{28,20},{24,28},{16,24},{8,16},{0,8},{5,1},{1... | collective-permute-start | bytes 1572872 | tf_op jit(solution)/shard_map/ppermute | solution.py:128
  111.2 10.3 %collective-permute-start.20 = (bf16[528,1024]{1,0:T(8,128)(2,1)S(1)}, bf16[528,1024]{1,0:T(8,128)(2,1)S(1)}, u32[]{:S(2)}, u32[]{:S(2)}) collective-permute-start(bf16[528,1024]{1,0:T(8,128)(2,1)S(1)} %get-tuple-element.207.rest_9_.rest_0_), channel_id=1, source_target_pairs={{0,1},{1,0},{2,3},{3,2},{4,5},{5,4},{6,7},{7,6},{8,9},{9,8},{10,11... | collective-permute-start | bytes 3244040 | tf_op jit(solution)/shard_map/ppermute | solution.py:225
  111.2 31.3 %collective-permute-start.21 = (bf16[528,1024]{1,0:T(8,128)(2,1)S(1)}, bf16[528,1024]{1,0:T(8,128)(2,1)S(1)}, u32[]{:S(2)}, u32[]{:S(2)}) collective-permute-start(bf16[528,1024]{1,0:T(8,128)(2,1)S(1)} %get-tuple-element.207.rest_9_.rest_0_), channel_id=1, source_target_pairs={{0,2},{1,3},{2,0},{3,1},{4,6},{5,7},{6,4},{7,5},{8,10},{9,11},{10,... | collective-permute-start | bytes 3244040 | tf_op jit(solution)/shard_map/ppermute | solution.py:221
  112.8 8.5 %collective-permute-start.18 = (bf16[64,2048]{1,0:T(8,128)(2,1)S(1)}, bf16[64,2048]{1,0:T(8,128)(2,1)S(1)}, u32[]{:S(2)}, u32[]{:S(2)}) collective-permute-start(bf16[64,2048]{1,0:T(8,128)(2,1)S(1)} %slice.190), channel_id=1, source_target_pairs={{4,12},{12,20},{20,28},{28,24},{24,16},{16,8},{8,0},{0,4},{5,13},{... | collective-permute-start | bytes 786440 | tf_op jit(solution)/shard_map/ppermute | solution.py:125
  113.4 8.2 %collective-permute-start.19 = (bf16[64,2048]{1,0:T(8,128)(2,1)S(1)}, bf16[64,2048]{1,0:T(8,128)(2,1)S(1)}, u32[]{:S(2)}, u32[]{:S(2)}) collective-permute-start(bf16[64,2048]{1,0:T(8,128)(2,1)S(1)} %slice.191), channel_id=1, source_target_pairs={{4,0},{12,4},{20,12},{28,20},{24,28},{16,24},{8,16},{0,8},{5,1},{1... | collective-permute-start | bytes 786440 | tf_op jit(solution)/shard_map/ppermute | solution.py:128
  157.8 40.1 %collective-permute-start.25 = (bf16[528,1024]{1,0:T(8,128)(2,1)}, bf16[528,1024]{1,0:T(8,128)(2,1)}, u32[]{:S(2)}, u32[]{:S(2)}) collective-permute-start(bf16[528,1024]{1,0:T(8,128)(2,1)} %get-tuple-element.224), channel_id=1, source_target_pairs={{0,1},{1,0},{2,3},{3,2},{4,5},{5,4},{6,7},{7,6},{8,9},{9,8},{10,11... | collective-permute-start | bytes 3244040 | tf_op jit(solution)/shard_map/ppermute | solution.py:225
  175.9 26.3 %collective-permute-start.26 = (bf16[528,1024]{1,0:T(8,128)(2,1)}, bf16[528,1024]{1,0:T(8,128)(2,1)}, u32[]{:S(2)}, u32[]{:S(2)}) collective-permute-start(bf16[528,1024]{1,0:T(8,128)(2,1)} %get-tuple-element.225), channel_id=1, source_target_pairs={{0,2},{1,3},{2,0},{3,1},{4,6},{5,7},{6,4},{7,5},{8,10},{9,11},{10,... | collective-permute-start | bytes 3244040 | tf_op jit(solution)/shard_map/ppermute | solution.py:221
  195.8 16.9 %collective-permute-start.27 = (bf16[64,2048]{1,0:T(8,128)(2,1)S(1)}, bf16[64,2048]{1,0:T(8,128)(2,1)S(1)}, u32[]{:S(2)}, u32[]{:S(2)}) collective-permute-start(bf16[64,2048]{1,0:T(8,128)(2,1)S(1)} %get-tuple-element.228), channel_id=1, source_target_pairs={{4,12},{12,20},{20,28},{28,24},{24,16},{16,8},{8,0},{0,4},{5,13},{... | collective-permute-start | bytes 786440 | tf_op jit(solution)/shard_map/ppermute | solution.py:125
  196.5 16.1 %collective-permute-start.28 = (bf16[64,2048]{1,0:T(8,128)(2,1)S(1)}, bf16[64,2048]{1,0:T(8,128)(2,1)S(1)}, u32[]{:S(2)}, u32[]{:S(2)}) collective-permute-start(bf16[64,2048]{1,0:T(8,128)(2,1)S(1)} %get-tuple-element.230), channel_id=1, source_target_pairs={{4,0},{12,4},{20,12},{28,20},{24,28},{16,24},{8,16},{0,8},{5,1},{1... | collective-permute-start | bytes 786440 | tf_op jit(solution)/shard_map/ppermute | solution.py:128
  212.7 15.9 %collective-permute-start.32 = (bf16[528,1024]{1,0:T(8,128)(2,1)S(1)}, bf16[528,1024]{1,0:T(8,128)(2,1)S(1)}, u32[]{:S(2)}, u32[]{:S(2)}) collective-permute-start(bf16[528,1024]{1,0:T(8,128)(2,1)S(1)} %get-tuple-element.245.own_ref), channel_id=1, source_target_pairs={{0,1},{1,0},{2,3},{3,2},{4,5},{5,4},{6,7},{7,6},{8,9},{9,8},{10,11... | collective-permute-start | bytes 3244040 | tf_op jit(solution)/shard_map/ppermute | solution.py:225
  214.0 14.6 %collective-permute-start.37 = (bf16[264,1024]{1,0:T(8,128)(2,1)S(1)}, bf16[264,1024]{1,0:T(8,128)(2,1)S(1)}, u32[]{:S(2)}, u32[]{:S(2)}) collective-permute-start(bf16[264,1024]{1,0:T(8,128)(2,1)S(1)} %get-tuple-element.262), channel_id=1, source_target_pairs={{0,2},{1,3},{2,0},{3,1},{4,6},{5,7},{6,4},{7,5},{8,10},{9,11},{10,... | collective-permute-start | bytes 1622024 | tf_op jit(solution)/shard_map/ppermute | solution.py:221
  214.6 13.6 %collective-permute-start.30 = (bf16[128,2048]{1,0:T(8,128)(2,1)S(1)}, bf16[128,2048]{1,0:T(8,128)(2,1)S(1)}, u32[]{:S(2)}, u32[]{:S(2)}) collective-permute-start(bf16[128,2048]{1,0:T(8,128)(2,1)S(1)} %get-tuple-element.239), channel_id=1, source_target_pairs={{4,12},{12,20},{20,28},{28,24},{24,16},{16,8},{8,0},{0,4},{5,13},{... | collective-permute-start | bytes 1572872 | tf_op jit(solution)/shard_map/ppermute | solution.py:125
  215.3 13.3 %collective-permute-start.31 = (bf16[128,2048]{1,0:T(8,128)(2,1)S(1)}, bf16[128,2048]{1,0:T(8,128)(2,1)S(1)}, u32[]{:S(2)}, u32[]{:S(2)}) collective-permute-start(bf16[128,2048]{1,0:T(8,128)(2,1)S(1)} %get-tuple-element.241), channel_id=1, source_target_pairs={{4,0},{12,4},{20,12},{28,20},{24,28},{16,24},{8,16},{0,8},{5,1},{1... | collective-permute-start | bytes 1572872 | tf_op jit(solution)/shard_map/ppermute | solution.py:128
  228.6 19.4 %collective-permute-start.38 = (bf16[1056,768]{1,0:T(8,128)(2,1)S(1)}, bf16[1056,768]{1,0:T(8,128)(2,1)S(1)}, u32[]{:S(2)}, u32[]{:S(2)}) collective-permute-start(bf16[1056,768]{1,0:T(8,128)(2,1)S(1)} %get-tuple-element.263.grad_ref.refs_1_), channel_id=1, source_target_pairs={{0,1},{1,0},{2,3},{3,2},{4,5},{5,4},{6,7},{7,6},{8,9},{9,8},{10,11... | collective-permute-start | bytes 4866056 | tf_op jit(solution)/shard_map/ppermute | solution.py:225
  229.4 18.6 %collective-permute-start.39 = (bf16[264,1024]{1,0:T(8,128)(2,1)S(1)}, bf16[264,1024]{1,0:T(8,128)(2,1)S(1)}, u32[]{:S(2)}, u32[]{:S(2)}) collective-permute-start(bf16[264,1024]{1,0:T(8,128)(2,1)S(1)} %get-tuple-element.264), channel_id=1, source_target_pairs={{0,2},{1,3},{2,0},{3,1},{4,6},{5,7},{6,4},{7,5},{8,10},{9,11},{10,... | collective-permute-start | bytes 1622024 | tf_op jit(solution)/shard_map/ppermute | solution.py:221
  231.7 16.3 %collective-permute-start.33 = (bf16[128,2048]{1,0:T(8,128)(2,1)S(1)}, bf16[128,2048]{1,0:T(8,128)(2,1)S(1)}, u32[]{:S(2)}, u32[]{:S(2)}) collective-permute-start(bf16[128,2048]{1,0:T(8,128)(2,1)S(1)} %get-tuple-element.249), channel_id=1, source_target_pairs={{4,12},{12,20},{20,28},{28,24},{24,16},{16,8},{8,0},{0,4},{5,13},{... | collective-permute-start | bytes 1572872 | tf_op jit(solution)/shard_map/ppermute | solution.py:125
  232.3 15.7 %collective-permute-start.34 = (bf16[128,2048]{1,0:T(8,128)(2,1)S(1)}, bf16[128,2048]{1,0:T(8,128)(2,1)S(1)}, u32[]{:S(2)}, u32[]{:S(2)}) collective-permute-start(bf16[128,2048]{1,0:T(8,128)(2,1)S(1)} %get-tuple-element.251), channel_id=1, source_target_pairs={{4,0},{12,4},{20,12},{28,20},{24,28},{16,24},{8,16},{0,8},{5,1},{1... | collective-permute-start | bytes 1572872 | tf_op jit(solution)/shard_map/ppermute | solution.py:128
  233.8 17.6 %collective-permute-start.43 = (bf16[528,1024]{1,0:T(8,128)(2,1)S(1)}, bf16[528,1024]{1,0:T(8,128)(2,1)S(1)}, u32[]{:S(2)}, u32[]{:S(2)}) collective-permute-start(bf16[528,1024]{1,0:T(8,128)(2,1)S(1)} %copy-done.78), channel_id=1, source_target_pairs={{0,1},{1,0},{2,3},{3,2},{4,5},{5,4},{6,7},{7,6},{8,9},{9,8},{10,11... | collective-permute-start | bytes 3244040 | tf_op jit(solution)/shard_map/ppermute | solution.py:225
  250.1 11.0 %collective-permute-start.40 = (bf16[1056,768]{1,0:T(8,128)(2,1)S(1)}, bf16[1056,768]{1,0:T(8,128)(2,1)S(1)}, u32[]{:S(2)}, u32[]{:S(2)}) collective-permute-start(bf16[1056,768]{1,0:T(8,128)(2,1)S(1)} %get-tuple-element.265.grad_ref.refs_0_), channel_id=1, source_target_pairs={{0,1},{1,0},{2,3},{3,2},{4,5},{5,4},{6,7},{7,6},{8,9},{9,8},{10,11... | collective-permute-start | bytes 4866056 | tf_op jit(solution)/shard_map/ppermute | solution.py:225
  253.5 22.1 %collective-permute-start.44 = (bf16[264,1024]{1,0:T(8,128)(2,1)S(1)}, bf16[264,1024]{1,0:T(8,128)(2,1)S(1)}, u32[]{:S(2)}, u32[]{:S(2)}) collective-permute-start(bf16[264,1024]{1,0:T(8,128)(2,1)S(1)} %get-tuple-element.277), channel_id=1, source_target_pairs={{0,2},{1,3},{2,0},{3,1},{4,6},{5,7},{6,4},{7,5},{8,10},{9,11},{10,... | collective-permute-start | bytes 1622024 | tf_op jit(solution)/shard_map/ppermute | solution.py:221
  254.1 14.8 %collective-permute-start.35 = (bf16[128,2048]{1,0:T(8,128)(2,1)S(1)}, bf16[128,2048]{1,0:T(8,128)(2,1)S(1)}, u32[]{:S(2)}, u32[]{:S(2)}) collective-permute-start(bf16[128,2048]{1,0:T(8,128)(2,1)S(1)} %get-tuple-element.257), channel_id=1, source_target_pairs={{4,12},{12,20},{20,28},{28,24},{24,16},{16,8},{8,0},{0,4},{5,13},{... | collective-permute-start | bytes 1572872 | tf_op jit(solution)/shard_map/ppermute | solution.py:125
  254.6 14.8 %collective-permute-start.36 = (bf16[128,2048]{1,0:T(8,128)(2,1)S(1)}, bf16[128,2048]{1,0:T(8,128)(2,1)S(1)}, u32[]{:S(2)}, u32[]{:S(2)}) collective-permute-start(bf16[128,2048]{1,0:T(8,128)(2,1)S(1)} %get-tuple-element.259), channel_id=1, source_target_pairs={{4,0},{12,4},{20,12},{28,20},{24,28},{16,24},{8,16},{0,8},{5,1},{1... | collective-permute-start | bytes 1572872 | tf_op jit(solution)/shard_map/ppermute | solution.py:128
  261.1 12.7 %collective-permute-start.41 = (bf16[64,2048]{1,0:T(8,128)(2,1)S(1)}, bf16[64,2048]{1,0:T(8,128)(2,1)S(1)}, u32[]{:S(2)}, u32[]{:S(2)}) collective-permute-start(bf16[64,2048]{1,0:T(8,128)(2,1)S(1)} %get-tuple-element.266), channel_id=1, source_target_pairs={{4,12},{12,20},{20,28},{28,24},{24,16},{16,8},{8,0},{0,4},{5,13},{... | collective-permute-start | bytes 786440 | tf_op jit(solution)/shard_map/ppermute | solution.py:125
  261.6 12.3 %collective-permute-start.42 = (bf16[64,2048]{1,0:T(8,128)(2,1)S(1)}, bf16[64,2048]{1,0:T(8,128)(2,1)S(1)}, u32[]{:S(2)}, u32[]{:S(2)}) collective-permute-start(bf16[64,2048]{1,0:T(8,128)(2,1)S(1)} %get-tuple-element.268), channel_id=1, source_target_pairs={{4,0},{12,4},{20,12},{28,20},{24,28},{16,24},{8,16},{0,8},{5,1},{1... | collective-permute-start | bytes 786440 | tf_op jit(solution)/shard_map/ppermute | solution.py:128
  270.2 22.4 %collective-permute-start.47 = (bf16[264,1024]{1,0:T(8,128)(2,1)}, bf16[264,1024]{1,0:T(8,128)(2,1)}, u32[]{:S(2)}, u32[]{:S(2)}) collective-permute-start(bf16[264,1024]{1,0:T(8,128)(2,1)} %get-tuple-element.283), channel_id=1, source_target_pairs={{0,2},{1,3},{2,0},{3,1},{4,6},{5,7},{6,4},{7,5},{8,10},{9,11},{10,... | collective-permute-start | bytes 1622024 | tf_op jit(solution)/shard_map/ppermute | solution.py:221
  276.5 14.0 %collective-permute-start.45 = (bf16[128,2048]{1,0:T(8,128)(2,1)}, bf16[128,2048]{1,0:T(8,128)(2,1)S(1)}, u32[]{:S(2)}, u32[]{:S(2)}) collective-permute-start(bf16[128,2048]{1,0:T(8,128)(2,1)} %get-tuple-element.278), channel_id=1, source_target_pairs={{4,12},{12,20},{20,28},{28,24},{24,16},{16,8},{8,0},{0,4},{5,13},{... | collective-permute-start | bytes 1572872 | tf_op jit(solution)/shard_map/ppermute | solution.py:125
  276.9 13.5 %collective-permute-start.46 = (bf16[128,2048]{1,0:T(8,128)(2,1)}, bf16[128,2048]{1,0:T(8,128)(2,1)}, u32[]{:S(2)}, u32[]{:S(2)}) collective-permute-start(bf16[128,2048]{1,0:T(8,128)(2,1)} %get-tuple-element.280), channel_id=1, source_target_pairs={{4,0},{12,4},{20,12},{28,20},{24,28},{16,24},{8,16},{0,8},{5,1},{1... | collective-permute-start | bytes 1572872 | tf_op jit(solution)/shard_map/ppermute | solution.py:128
  295.7 6.8 %collective-permute-start.48 = (bf16[1056,1024]{1,0:T(8,128)(2,1)S(1)}, bf16[1056,1024]{1,0:T(8,128)(2,1)}, u32[]{:S(2)}, u32[]{:S(2)}) collective-permute-start(bf16[1056,1024]{1,0:T(8,128)(2,1)S(1)} %add_convert_fusion.refs_0_.refs_3_), channel_id=1, source_target_pairs={{0,1},{1,0},{2,3},{3,2},{4,5},{5,4},{6,7},{7,6},{8,9},{9,8},{10,11... | collective-permute-start | bytes 6488072 | tf_op jit(solution)/shard_map/ppermute | solution.py:225
  296.0 26.6 %collective-permute-start.54 = (bf16[528,1024]{1,0:T(8,128)(2,1)}, bf16[528,1024]{1,0:T(8,128)(2,1)}, u32[]{:S(2)}, u32[]{:S(2)}) collective-permute-start(bf16[528,1024]{1,0:T(8,128)(2,1)} %get-tuple-element.303.refs_0_), channel_id=1, source_target_pairs={{0,2},{1,3},{2,0},{3,1},{4,6},{5,7},{6,4},{7,5},{8,10},{9,11},{10,... | collective-permute-start | bytes 3244040 | tf_op jit(solution)/shard_map/ppermute | solution.py:221
  300.1 15.4 %collective-permute-start.51 = (bf16[128,2048]{1,0:T(8,128)(2,1)}, bf16[128,2048]{1,0:T(8,128)(2,1)S(1)}, u32[]{:S(2)}, u32[]{:S(2)}) collective-permute-start(bf16[128,2048]{1,0:T(8,128)(2,1)} %copy-done.42), channel_id=1, source_target_pairs={{4,12},{12,20},{20,28},{28,24},{24,16},{16,8},{8,0},{0,4},{5,13},{... | collective-permute-start | bytes 1572872 | tf_op jit(solution)/shard_map/ppermute | solution.py:125
  300.9 14.6 %collective-permute-start.52 = (bf16[128,2048]{1,0:T(8,128)(2,1)}, bf16[128,2048]{1,0:T(8,128)(2,1)S(1)}, u32[]{:S(2)}, u32[]{:S(2)}) collective-permute-start(bf16[128,2048]{1,0:T(8,128)(2,1)} %copy-done.41), channel_id=1, source_target_pairs={{4,0},{12,4},{20,12},{28,20},{24,28},{16,24},{8,16},{0,8},{5,1},{1... | collective-permute-start | bytes 1572872 | tf_op jit(solution)/shard_map/ppermute | solution.py:128
  308.3 7.2 %collective-permute-start.50 = (f32[8,1024]{1,0:T(8,128)S(1)}, f32[8,1024]{1,0:T(8,128)S(1)}, u32[]{:S(2)}, u32[]{:S(2)}) collective-permute-start(f32[8,1024]{1,0:T(8,128)S(1)} %pad_maximum_fusion.4), channel_id=1, source_target_pairs={{0,4},{4,0},{8,12},{12,8},{16,20},{20,16},{24,28},{28,24},{1,5},{5... | collective-permute-start | bytes 98312 | tf_op jit(solution)/shard_map/ppermute | solution.py:1140
  324.7 13.9 %collective-permute-start.57 = (bf16[128,2048]{1,0:T(8,128)(2,1)}, bf16[128,2048]{1,0:T(8,128)(2,1)}, u32[]{:S(2)}, u32[]{:S(2)}) collective-permute-start(bf16[128,2048]{1,0:T(8,128)(2,1)} %copy-done.44), channel_id=1, source_target_pairs={{4,12},{12,20},{20,28},{28,24},{24,16},{16,8},{8,0},{0,4},{5,13},{... | collective-permute-start | bytes 1572872 | tf_op jit(solution)/shard_map/ppermute | solution.py:125
  325.2 13.6 %collective-permute-start.58 = (bf16[128,2048]{1,0:T(8,128)(2,1)}, bf16[128,2048]{1,0:T(8,128)(2,1)}, u32[]{:S(2)}, u32[]{:S(2)}) collective-permute-start(bf16[128,2048]{1,0:T(8,128)(2,1)} %copy-done.43), channel_id=1, source_target_pairs={{4,0},{12,4},{20,12},{28,20},{24,28},{16,24},{8,16},{0,8},{5,1},{1... | collective-permute-start | bytes 1572872 | tf_op jit(solution)/shard_map/ppermute | solution.py:128
  (97 other events, 820.5 us)
where the time goes:
time: 358 us; the launch traced here: 357 us
  Pallas kernels  158 us (44%)
  waiting for transfers between devices  88.3 us (25%)
  starting transfers between devices  55.9 us (16%)
  local copies, waits for them, and re-layouts  47.4 us (13%)
  other arithmetic  5.19 us (1%)
    pallas_call x28, Pallas kernels, run(): out = kernel(tie(self.info, self.now, wait, self.hold), *values)  158 us
    ppermute x16, waiting for transfers between devices, send_ahead(): return lax.ppermute(value, 'dp', self.ahead)  40.3 us
    unnamed x173, local copies, waits for them, and re-layouts  38.9 us
    ppermute x11, waiting for transfers between devices, across(): return lax.ppermute(value, 'mp', pairs)  20.8 us
    ppermute x16, starting transfers between devices, send_ahead(): return lax.ppermute(value, 'dp', self.ahead)  18.9 us
    ppermute x16, starting transfers between devices, send_behind(): return lax.ppermute(value, 'dp', self.behind)  15.1 us
    ppermute x11, starting transfers between devices, across(): return lax.ppermute(value, 'mp', pairs)  14.5 us
    ppermute x16, waiting for transfers between devices, partner(): return lax.ppermute(value, 'mp', [(m, m ^ 1) for m in range(2 * chips)])  10.2 us
  transfers between devices with their start and end apart: 62, of which 33 were waited for; matrix products, arithmetic and copies ran while one was open for 3% of the time, Pallas kernels for 41%

commit v1 on v0

--- a/solution.py
+++ b/solution.py
@@ -277,21 +277,29 @@
 
 
 def qkv_body(info, x_ref, bias_ref, *rest, base, unit, chips, count):
-    pieces, (out_ref, whole_ref, weights, sems, out_sem) = rest[:count], rest[count:]
+    steps = count // 2 + 1
+    own, rest = rest[:count], rest[count:]
+    far, (out_ref, whole_ref, weights, sems, out_sem) = (
+        rest[: steps * (chips - 1)],
+        rest[steps * (chips - 1) :],
+    )
     part = weights.shape[1] // chips
     width = out_ref.shape[1] // chips
     keep = pltpu.make_async_copy(weights, whole_ref, out_sem)
 
     @pl.when(pl.program_id(0) == 0)
     def _():
-        targets = [
-            (
-                lambda piece, b=b: piece.at[b],
-                lambda place, b=b: weights.at[place, pl.ds(b * part, part)],
-            )
-            for b in range(chips)
-        ]
-        wait_all(start_all(weight_copies(info, base, pieces, unit, targets), sems))
+        copies = []
+        for b in range(chips):
+            for i, piece in enumerate(own):
+                rows = piece.shape[0]
+                source = piece
+                if b:
+                    joined = far[(b - 1) * steps + (i + 1) // 2]
+                    source = joined.at[pl.ds(rows if i and i % 2 == 0 else 0, rows)]
+                place = pl.ds(pl.multiple_of(info[base + i], unit), rows)
+                copies.append((source, weights.at[place, pl.ds(b * part, part)]))
+        wait_all(start_all(copies, sems))
         keep.start()
 
     def columns(b, _):
@@ -461,7 +469,7 @@
 def mlp_body(info, cot_ref, bias_ref, *rest, base, unit, count, parts, adds):
     pieces, rest = rest[:count], rest[count:]
     seconds, rest = rest[:parts], rest[parts:]
-    gots, rest = rest[: 2 * adds], rest[2 * adds :]
+    gots, rest = rest[:adds], rest[adds:]
     hidden_ref, pre_ref, rest = rest[0], rest[1], rest[2:]
     backs, outs, rest = rest[:parts], rest[parts : 2 * parts], rest[2 * parts :]
     sum_ref, expand, shrink, rows, sems, row_sems = rest
@@ -513,8 +521,8 @@
                 @pl.when(turn == i)
                 def _(i=i, targets=targets, product=product, kind=kind):
                     total = product
-                    if adds:
-                        total = total + gots[2 * i + kind][:, at].astype(f32)
+                    if adds and kind == 0:
+                        total = total + gots[i][:, at].astype(f32)
                     targets[i][:, at] = total.astype(bf16)
 
         return 0
@@ -718,23 +726,31 @@
     bias_shard = jnp.zeros((pairs, 3, LANES), f32)
     bias_shard = bias_shard.at[:, 0].set(qv_bias[0].reshape(pairs, LANES))
     bias_shard = bias_shard.at[:, 2].set(qv_bias[1].reshape(pairs, LANES)).reshape(1, width)
-    shards_x, bias_x = [shard], [bias_shard]
+    high = bias_shard.astype(bf16)
+    both = jnp.concatenate([high, (bias_shard - high.astype(f32)).astype(bf16)])
+    below = jnp.pad(both, ((0, 14), (0, part)))
+    joined = jnp.concatenate([shard, below])
+    attn_steps = ring.gather_steps(shard, 0, order)
+    attn_pieces = [shard]
+    far_pieces = {step: [across(joined, step, chips)] for step in range(1, chips)}
+    bias_x = [bias_shard]
     for step in range(1, chips):
-        shards_x.append(across(shard, step, chips))
-        bias_x.append(across(bias_shard, step, chips))
-    both_shards = jnp.stack(shards_x)
-    mlp_shard = jnp.concatenate(
-        [expand_weight.astype(bf16), shrink_weight.astype(bf16).T], axis=1
-    )
-    attn_steps = ring.gather_steps(both_shards, 1, order)
-    mlp_steps = ring.gather_steps(mlp_shard, 0, order)
-    attn_pieces, mlp_pieces = [both_shards], [mlp_shard]
+        got = far_pieces[step][0][unit_rows : unit_rows + 2, :width].astype(f32)
+        bias_x.append(got[0:1] + got[1:2])
 
     def next_step(steps, pieces):
         got = next(steps, None)
         if got is not None:
             pieces += got
         return got
+
+    def send_far(got):
+        joined = jnp.concatenate(order.after(got))
+        for step in range(1, chips):
+            far_pieces[step].append(across(joined, step, chips))
+
+    def last_far(i=-1):
+        return [far_pieces[step][i] for step in range(1, chips)]
 
     def pad_sets(value, wait):
         columns = pl.BlockSpec((token_rows, CHUNK), lambda i, _: (0, i))
@@ -749,9 +765,16 @@
         )
         return order.run(kernel, value, wait=wait)
 
-    next_step(attn_steps, attn_pieces)
-    x_rows = pad_sets(tokens, shards_x)
-    next_step(attn_steps, attn_pieces)
+    got = next_step(attn_steps, attn_pieces)
+    order.due = last_far()
+    after = next_step(attn_steps, attn_pieces)
+    order.due = ()
+    send_far(got)
+    x_rows = pad_sets(tokens, ())
+    order.due = last_far()
+    got = next_step(attn_steps, attn_pieces)
+    order.due = ()
+    send_far(after)
     kernel = call(
         first_low_body,
         (sets_x,),
@@ -765,33 +788,45 @@
         [],
         "first_low",
     )
-    first_low = order.run(kernel, x_rows, row(first_gain), row(first_shift), wait=attn_pieces[1:3])
-    next_step(attn_steps, attn_pieces)
-    starts = order.after(jnp.pad(offsets, ((0, slots - sets), (0, 0))))
+    first_low = order.run(kernel, x_rows, row(first_gain), row(first_shift))
+    while got:
+        order.due = last_far(-2)
+        after = next_step(attn_steps, attn_pieces)
+        if after is None:
+            shrink_shard = tie(shrink_weight, far_pieces[1][0]).astype(bf16).T
+            mlp_shard = jnp.concatenate([expand_weight.astype(bf16), shrink_shard], axis=1)
+            mlp_pieces = [mlp_shard]
+            mlp_steps = ring.gather_steps(tie(mlp_shard, got), 0, order)
+            next_step(mlp_steps, mlp_pieces)
+        order.due = ()
+        send_far(got)
+        got = after
+    order.due = last_far(-2) + last_far()
+    starts = tie(jnp.pad(offsets, ((0, slots - sets), (0, 0))), order.now)
     starts = lax.dynamic_slice_in_dim(starts, x_index * sets_x, sets_x, axis=0)
     positions = jnp.arange(SET_ROWS, dtype=jnp.int32)
     ids = jnp.sum((positions[None, :, None] >= starts[:, None, :]).astype(jnp.int32), axis=-1)
     ids = jnp.where(positions[None, :] < SET_TOKENS, ids, -1)
     key_ids, query_ids = ids[:, :, None], ids[:, None, :]
-    cot = pad_sets(cotangent, (attn_pieces[3:5], key_ids, query_ids, mlp_shard))
-    while next_step(attn_steps, attn_pieces):
-        pass
-    mlp_steps = ring.gather_steps(tie(mlp_shard, attn_pieces[-2:]), 0, order)
+    cot = pad_sets(cotangent, (key_ids, query_ids))
     next_step(mlp_steps, mlp_pieces)
+    order.due = ()
     count = len(attn_pieces)
     copies = count * chips
+    far_list = [piece for step in range(1, chips) for piece in far_pieces[step]]
 
     joint = chips * (width + part)
     kernel = call(
         functools.partial(qkv_body, base=base, unit=unit, chips=chips, count=count),
         (2,),
-        [pl.BlockSpec((half, dim), lambda i, _: (i, 0)), whole(1, chips * width)] + [ANY] * count,
+        [pl.BlockSpec((half, dim), lambda i, _: (i, 0)), whole(1, chips * width)]
+        + [ANY] * (count + len(far_list)),
         [pl.BlockSpec((half, chips * width), lambda i, _: (i, 0)), HBM],
         [shape((rows_x, chips * width), bf16), shape((dim, joint), bf16)],
         [pltpu.VMEM((dim, joint), bf16), sem((copies,)), sem],
         "qkv",
     )
-    qkv, weights = order.run(kernel, first_low, jnp.concatenate(bias_x, axis=1), *attn_pieces)
+    qkv, weights = order.run(kernel, first_low, jnp.concatenate(bias_x, axis=1), *attn_pieces, *far_list)
     order.due = mlp_pieces[-2:]
     both_weights = [weights, partner(order.after(weights), chips)]
 
@@ -844,12 +879,12 @@
         row(second_shift),
         *both_weights,
     )
-    order.due = mlp_pieces[-2:]
-    second_low = order.after(second_low)
-    order.due = ()
-    seconds = {(0, 0): second_low, (0, 1): partner(second_low, chips)}
+    seconds = {(0, 0): second_low}
     for step in range(1, chips):
         seconds[(step, 0)] = across(second_low, step, chips)
+    order.due = mlp_pieces[-2:]
+    seconds[(0, 1)] = partner(order.after(second_low), chips)
+    order.due = ()
     while next_step(mlp_steps, mlp_pieces):
         pass
 
@@ -858,7 +893,7 @@
         first = keys.index(group[0])
         kernel = call(
             functools.partial(
-                mlp_body, base=base, unit=unit, count=count, parts=parts, adds=len(gots) // 2
+                mlp_body, base=base, unit=unit, count=count, parts=parts, adds=len(gots)
             ),
             (parts,),
             [
@@ -897,10 +932,7 @@
     for step in range(1, chips):
         seconds[(step, 1)] = partner(order.after(seconds[(step, 0)]), chips)
     other = feed(far_other)
-    gots = []
-    for back, out in zip(other[2], other[3]):
-        gots += [partner(back, chips), partner(out, chips)]
-    own = feed(far_own, gots)
+    own = feed(far_own, [partner(back, chips) for back in other[2]])
     feeds = [first, other, own]
 
     def along_x(own, sums):
@@ -967,12 +999,17 @@
     if chips == 2:
         out_near = order.after(residual) + shrink_bias + first[3][0].astype(f32)
         out_near = (out_near + partner(order.after(first[3][1]), chips).astype(f32)).astype(bf16)
-        out_far = own[3][0]
+        out_far = own[3][0].astype(f32)
+        out_far = (out_far + partner(other[3][0], chips).astype(f32)).astype(bf16)
         cut = half // 2
         out_sends = iter([out_far[:cut], out_far[cut:], out_near[:cut], out_near[cut:]])
         out_gots = [across(order.after(next(out_sends)), 1, chips)]
     else:
-        out_terms = along_x(order.after(first[3]), order.after(own[3]))
+        out_own = [
+            (mine.astype(f32) + partner(order.after(got), chips).astype(f32)).astype(bf16)
+            for mine, got in zip(own[3], other[3])
+        ]
+        out_terms = along_x(order.after(first[3]), out_own)
 
     def attend_back(b):
         half_block = lambda j: pl.BlockSpec(
@@ -1003,10 +1040,10 @@
         return order.run(kernel, qkv, *ids, logs, grad_own, grad_got, grad_own, grad_got)
 
     def qkv_grad(b, before):
-        columns = lambda count: pl.BlockSpec((count, span), lambda i, _: (0, i))
+        columns = lambda count: pl.BlockSpec((count, CHUNK), lambda i, _: (0, i))
         kernel = call(
             qkv_grad_body,
-            (dim // span,),
+            (dim // CHUNK,),
             [
                 columns(rows_x),
                 whole(rows_x, width),
@@ -1016,7 +1053,7 @@
                 pl.BlockSpec((half, part), lambda i, info: (1 - info[0], b)),
             ]
             + [ANY] * len(before),
-            pl.BlockSpec((span, width + part), lambda i, _: (i, b)),
+            pl.BlockSpec((CHUNK, width + part), lambda i, _: (i, b)),
             shape((dim, joint), bf16),
             [],
             "qkv_grad",

time: 358 us -> 340 us (0.950)
  waiting for transfers between devices: 88.3 us -> 65.3 us
  other arithmetic: 5.19 us -> 14.3 us
  local copies, waits for them, and re-layouts: 47.4 us -> 41.4 us
    ppermute x16, waiting for transfers between devices: 40.3 us -> 20.4 us  [send_ahead(): return lax.ppermute(value, 'dp', self.ahead)]
    unnamed x173 -> x184, local copies, waits for them, and re-layouts: 38.9 us -> 32.8 us
    concatenate x1 -> x8, other arithmetic: 0.83 us -> 5.19 us  [the longest x4 3.27 us: send_far(): joined = jnp.concatenate(order.after(got))]
    ppermute x11 -> x14, waiting for transfers between devices: 20.8 us -> 19.2 us  [across(): return lax.ppermute(value, 'mp', pairs)]
    ppermute x11 -> x14, starting transfers between devices: 14.5 us -> 15.9 us  [across(): return lax.ppermute(value, 'mp', pairs)]
  transfers between devices with their start and end apart: 62 -> 65, of which waited for: 33 -> 29; matrix products, arithmetic and copies ran while one was open for 3% -> 6% of each run, Pallas kernels for 41% -> 43%
where the time goes in v1:
time: 340 us; the launch traced here: 339 us
  Pallas kernels  159 us (47%)
  waiting for transfers between devices  65.3 us (19%)
  starting transfers between devices  56.8 us (17%)
  local copies, waits for them, and re-layouts  41.4 us (12%)
  other arithmetic  14.3 us (4%)
    pallas_call x28, Pallas kernels, run(): out = kernel(tie(self.info, self.now, wait, self.hold), *values)  159 us
    unnamed x184, local copies, waits for them, and re-layouts  32.8 us
    ppermute x16, starting transfers between devices, send_ahead(): return lax.ppermute(value, 'dp', self.ahead)  21.8 us
    ppermute x16, waiting for transfers between devices, send_ahead(): return lax.ppermute(value, 'dp', self.ahead)  20.4 us
    ppermute x14, waiting for transfers between devices, across(): return lax.ppermute(value, 'mp', pairs)  19.2 us
    ppermute x14, starting transfers between devices, across(): return lax.ppermute(value, 'mp', pairs)  15.9 us
    ppermute x16, starting transfers between devices, send_behind(): return lax.ppermute(value, 'dp', self.behind)  12.2 us
    ppermute x16, waiting for transfers between devices, partner(): return lax.ppermute(value, 'mp', [(m, m ^ 1) for m in range(2 * chips)])  9.91 us
  transfers between devices with their start and end apart: 65, of which 29 were waited for; matrix products, arithmetic and copies ran while one was open for 6% of the time, Pallas kernels for 43%

profile of v1, /device:TPU:0, one launch (start us, length us, event | category | flops | bytes accessed | tf_op | source)
XLA Modules:
  0.0 339.2 jit_solution(2133635782104566814)
XLA Ops:
  3.9 3.0 collective-permute-start.1
  7.7 1.9 collective-permute-start
  9.7 3.6 %collective-permute-done.1.rest_1_ = bf16[128,1024]{1,0:T(8,128)(2,1)S(1)} collective-permute-done((bf16[128,1024]{1,0:T(8,128)(2,1)S(1)}, bf16[128,1024]{1,0:T(8,128)(2,1)S(1)}, u32[]{:S(2)}, u32[]{:S(2)}) %collective-permute-start.1) | collective-permute-done | bytes 262176 | tf_op jit(solution)/shard_map/ppermute | solution.py:125
  19.0 2.2 copy-done.23
  21.2 3.0 pad.117.x_ref.refs_4_
  24.3 2.1 first_low.1.x_ref.first_ref
  26.4 2.1 copy-done.8
  32.8 1.8 convert_element_type.97
  34.7 1.9 copy.99
  38.7 1.9 pad_maximum_fusion.3.rest_0_
  43.3 1.8 collective-permute-done.10.rest_11_
  52.2 2.2 copy-done.24
  54.4 3.0 pad.118.cot_ref
  57.4 2.0 copy-done.7
  62.8 7.3 %qkv.1 = (bf16[1056,1536]{1,0:T(8,128)(2,1)S(1)}, bf16[1024,2048]{1,0:T(8,128)(2,1)S(1)}) custom-call(s32[24]{0:T(128)S(1)} %concatenate.53.info, bf16[1056,1024]{1,0:T(8,128)(2,1)S(1)} %first_low.1.x_ref.first_ref, f32[1,1536]{1,0:T(1,128)S(1)} %pad_maximum_fusion.11.bias_ref, bf16[128,1024]{1,0:T(8,128)(2,1)S(1)} %pad_maximum_fusion.5.rest_0_, ...), custom_call_target="tpu_custom_call" | custom-call | flops 1 | bytes 1 | tf_op jit(solution)/shard_map/qkv/pallas_call | solution.py:88
  75.1 12.3 %attend.1 = (bf16[1056,512]{1,0:T(8,128)(2,1)S(1)}, f32[3,4,2,352]{3,2,1,0:T(2,128)S(1)}) custom-call(s32[24]{0:T(128)S(1)} %concatenate.53.info, bf16[1056,1536]{1,0:T(8,128)(2,1)S(1)} %get-tuple-element.205.qkv_ref, s32[3,352,1]{2,1,0:T(8,128)S(1)} %broadcast_select_fusion.key_ids, s32[3,1,352]{2,1,0:T(1,128)S(1)} %broadcast_select_fusion.1.query_ids), custom_call_target="tpu_custom_call" | custom-call | flops 1 | bytes 1 | tf_op jit(solution)/shard_map/attend/pallas_call | solution.py:88
  92.0 3.3 proj_norm.1
  103.1 19.3 %mlp.3 = (bf16[1056,1024]{1,0:T(8,128)(2,1)}, bf16[1056,1024]{1,0:T(8,128)(2,1)}, bf16[528,1024]{1,0:T(8,128)(2,1)}, bf16[528,1024]{1,0:T(8,128)(2,1)}, bf16[528...) custom-call(s32[24]{0:T(128)} %copy-done.40, bf16[2112,1024]{1,0:T(8,128)(2,1)} %copy-done.7, ...), custom_call_target="tpu_custom_call" | custom-call | flops 1 | bytes 1 | tf_op jit(solution)/shard_map/mlp/pallas_call | solution.py:88
  122.4 3.3 collective-permute-done.24.rest_9_.rest_3_
  125.6 2.7 collective-permute-done.25.rest_9_.rest_2_
  129.3 10.9 %mlp.4 = (bf16[528,1024]{1,0:T(8,128)(2,1)}, bf16[528,1024]{1,0:T(8,128)(2,1)}, bf16[528,1024]{1,0:T(8,128)(2,1)}, bf16[528,1024]{1,0:T(8,128)(2,1)}, f32[1,1024]{1,0:T(1,128)}) custom-call(s32[24]{0:T(128)} %copy-done.40, bf16[2112,1024]{1,0:T(8,128)(2,1)} %copy-done.7, f32[1,1024]{1,0:T(1,128)} %bitcast.80, bf16[128,2048]{1,0:T(8,128)(2,1)} %pad_maximum_fusion.3.rest_0_, ...), custom_call_target="tpu_custom_call" | custom-call | flops 1 | bytes 1 | tf_op jit(solution)/shard_map/mlp/pallas_call | solution.py:88
  140.8 2.6 collective-permute-done.26.rest_10_
  144.3 11.2 %mlp.5 = (bf16[528,1024]{1,0:T(8,128)(2,1)}, bf16[528,1024]{1,0:T(8,128)(2,1)}, bf16[528,1024]{1,0:T(8,128)(2,1)}, bf16[528,1024]{1,0:T(8,128)(2,1)}, f32[1,1024]{1,0:T(1,128)}) custom-call(s32[24]{0:T(128)} %copy-done.40, bf16[2112,1024]{1,0:T(8,128)(2,1)} %copy-done.7, f32[1,1024]{1,0:T(1,128)} %bitcast.81, bf16[128,2048]{1,0:T(8,128)(2,1)} %pad_maximum_fusion.3.rest_0_, ...), custom_call_target="tpu_custom_call" | custom-call | flops 1 | bytes 1 | tf_op jit(solution)/shard_map/mlp/pallas_call | solution.py:88
  156.8 16.5 %mlp_grad.1.ahead_ref.behind_ref.own_ref = bf16[1024,2048]{1,0:T(8,128)(2,1)} custom-call(s32[24]{0:T(128)} %copy-done.40, bf16[2112,1024]{1,0:T(8,128)(2,1)} %copy-done.7, bf16[528,1024]{1,0:T(8,128)(2,1)} %copy-done.22, bf16[528,1024]{1,0:T(8,128)(2,1)} %copy-done.60, bf16[528,1024]{1,0:T(8,128)(2,1)} %copy-done.62, bf16[528,1024]{1,0:T(8,128)(2,1)} %copy-done.61, ...), custom_call_target="tpu_custom_call" | custom-call | flops 1 | bytes 1 | tf_op jit(solution)/shard_map/mlp_grad/pallas_call | solution.py:88
  173.3 2.2 copy-done.5
  178.2 3.6 %collective-permute-done.28.rest_2_ = bf16[528,1024]{1,0:T(8,128)(2,1)} collective-permute-done((bf16[528,1024]{1,0:T(8,128)(2,1)}, bf16[528,1024]{1,0:T(8,128)(2,1)}, u32[]{:S(2)}, u32[]{:S(2)}) %collective-permute-start.28) | collective-permute-done | bytes 1081376 | tf_op jit(solution)/shard_map/ppermute | solution.py:221
  184.7 6.0 %residual_back.1 = (f32[528,1024]{1,0:T(8,128)S(1)}, bf16[528,1024]{1,0:T(8,128)(2,1)S(1)}, bf16[528,512]{1,0:T(8,128)(2,1)S(1)}, bf16[528,512]{1,0:T(8,128)(2,1)S(1)}, f32[8,1024]{1,0:T(8,128)S(1)}) custom-call(s32[24]{0:T(128)S(1)} %copy-done.41, f32[528,1024]{1,0:T(8,128)S(1)} %copy-done.18, bf16[2112,1024]{1,0:T(8,128)(2,1)S(1)} %bitcast.60, ...), custom_call_target="tpu_custom_call" | custom-call | flops 1 | bytes 1 | tf_op jit(solution)/shard_map/residual_back/pallas_call | solution.py:88
  190.8 2.3 add_convert_fusion.2
  198.2 9.8 %attend_back.2 = (bf16[1056,768]{1,0:T(8,128)(2,1)S(1)}, f32[2,1,384]{2,1,0:T(1,128)S(1)}) custom-call(s32[24]{0:T(128)S(1)} %copy-done.41, bf16[1056,1536]{1,0:T(8,128)(2,1)S(1)} %copy-done.16, s32[3,352,1]{2,1,0:T(8,128)S(1)} %broadcast_select_fusion.key_ids, s32[3,1,352]{2,1,0:T(1,128)S(1)} %broadcast_select_fusion.1.query_ids, ...), custom_call_target="tpu_custom_call" | custom-call | flops 1 | bytes 1 | tf_op jit(solution)/shard_map/attend_back/pallas_call | solution.py:88
  208.0 2.2 collective-permute-done.32.got_ahead
  216.2 5.1 %qkv_grad.2.rest_0_ = bf16[1024,2048]{1,0:T(8,128)(2,1)S(1)} custom-call(s32[24]{0:T(128)S(1)} %copy-done.41, bf16[1056,1024]{1,0:T(8,128)(2,1)S(1)} %copy-done.14, bf16[1056,768]{1,0:T(8,128)(2,1)S(1)} %get-tuple-element.281.grad_ref.refs_1_, bf16[528,1024]{1,0:T(8,128)(2,1)S(1)} %get-tuple-element.262.own_ref, ...), custom_call_target="tpu_custom_call" | custom-call | flops 1 | bytes 1 | tf_op jit(solution)/shard_map/qkv_grad/pallas_call | solution.py:88
  221.3 9.8 %attend_back.3 = (bf16[1056,768]{1,0:T(8,128)(2,1)S(1)}, f32[2,1,384]{2,1,0:T(1,128)S(1)}) custom-call(s32[24]{0:T(128)S(1)} %copy-done.41, bf16[1056,1536]{1,0:T(8,128)(2,1)S(1)} %copy-done.16, s32[3,352,1]{2,1,0:T(8,128)S(1)} %broadcast_select_fusion.key_ids, s32[3,1,352]{2,1,0:T(1,128)S(1)} %broadcast_select_fusion.1.query_ids, ...), custom_call_target="tpu_custom_call" | custom-call | flops 1 | bytes 1 | tf_op jit(solution)/shard_map/attend_back/pallas_call | solution.py:88
  239.3 5.1 %qkv_grad.3.ahead_ref.behind_ref.own_ref = bf16[1024,2048]{1,0:T(8,128)(2,1)S(1)} custom-call(s32[24]{0:T(128)S(1)} %copy-done.41, bf16[1056,1024]{1,0:T(8,128)(2,1)S(1)} %copy-done.14, bf16[1056,768]{1,0:T(8,128)(2,1)S(1)} %get-tuple-element.283.grad_ref.refs_0_, bf16[528,1024]{1,0:T(8,128)(2,1)S(1)} %get-tuple-element.262.own_ref, ...), custom_call_target="tpu_custom_call", output_to_operand_aliasing={{}: (7, {})} | custom-call | flops 1 | bytes 1 | tf_op jit(solution)/shard_map/qkv_grad/pallas_call | solution.py:88
  247.1 4.9 %collective-permute-done.37.got_ahead = bf16[128,2048]{1,0:T(8,128)(2,1)S(1)} collective-permute-done((bf16[128,2048]{1,0:T(8,128)(2,1)S(1)}, bf16[128,2048]{1,0:T(8,128)(2,1)S(1)}, u32[]{:S(2)}, u32[]{:S(2)}) %collective-permute-start.37) | collective-permute-done | bytes 524320 | tf_op jit(solution)/shard_map/ppermute | solution.py:125
  254.3 2.7 collective-permute-done.44.got_ahead
  262.0 11.9 %first_norm.1 = (bf16[528,1024]{1,0:T(8,128)(2,1)}, f32[8,1024]{1,0:T(8,128)}) custom-call(s32[24]{0:T(128)} %copy-done.40, bf16[1056,768]{1,0:T(8,128)(2,1)} %copy-done.21, bf16[1056,768]{1,0:T(8,128)(2,1)} %copy-done.20, bf16[1056,768]{1,0:T(8,128)(2,1)} %copy-done.67, bf16[1056,768]{1,0:T(8,128)(2,1)} %copy-done.66, bf16[2112,1024]{1,0:T(8,128)(2,1)} %copy-done.8, ...), custom_call_target="tpu_custom_call" | custom-call | flops 1 | bytes 1 | tf_op jit(solution)/shard_map/first_norm/pallas_call | solution.py:88
  274.0 2.1 ring_add.10
  277.1 2.1 add_convert_fusion.refs_0_.refs_3_
  281.1 2.5 collective-permute-done.52
  285.8 5.8 %assemble.2 = bf16[2070,1024]{1,0:T(8,128)(2,1)} custom-call(s32[24]{0:T(128)S(1)} %copy-done.42, bf16[1056,1024]{1,0:T(8,128)(2,1)S(1)} %add_convert_fusion.refs_0_.refs_3_, bf16[1056,1024]{1,0:T(8,128)(2,1)} %collective-permute-done.51.refs_1_.refs_2_, bf16[1056,1024]{1,0:T(8,128)(2,1)} %collective-permute-done.51.refs_1_.refs_2_, ...), custom_call_target="tpu_custom_call" | custom-call | flops 1 | bytes 1 | tf_op jit(solution)/shard_map/assemble/pallas_call | solution.py:88
  293.1 5.7 %collective-permute-done.53 = f32[8,1024]{1,0:T(8,128)S(1)} collective-permute-done((f32[8,1024]{1,0:T(8,128)S(1)}, f32[8,1024]{1,0:T(8,128)S(1)}, u32[]{:S(2)}, u32[]{:S(2)}) %collective-permute-start.53) | collective-permute-done | bytes 32800 | tf_op jit(solution)/shard_map/ppermute | solution.py:1177
  301.3 4.8 %collective-permute-done.57.refs_3_ = bf16[528,1024]{1,0:T(8,128)(2,1)} collective-permute-done((bf16[528,1024]{1,0:T(8,128)(2,1)}, bf16[528,1024]{1,0:T(8,128)(2,1)}, u32[]{:S(2)}, u32[]{:S(2)}) %collective-permute-start.57) | collective-permute-done | bytes 1081376 | tf_op jit(solution)/shard_map/ppermute | solution.py:221
  310.7 6.3 %assemble.3 = f32[2070,1024]{1,0:T(8,128)} custom-call(s32[24]{0:T(128)S(1)} %copy-done.42, bf16[528,1024]{1,0:T(8,128)(2,1)S(1)} %copy-done.26, bf16[528,1024]{1,0:T(8,128)(2,1)S(1)} %collective-permute-done.56.refs_1_, bf16[528,1024]{1,0:T(8,128)(2,1)S(1)} %collective-permute-done.58.refs_2_, bf16[528,1024]{1,0:T(8,128)(2,1)} %collective-permute-done.57.refs_3_), custom_call_target="tpu_custom_call" | custom-call | flops 1 | bytes 1 | tf_op jit(solution)/shard_map/assemble/pallas_call | solution.py:88
  317.0 4.1 %collective-permute-done.60.got_ahead = bf16[128,2048]{1,0:T(8,128)(2,1)} collective-permute-done((bf16[128,2048]{1,0:T(8,128)(2,1)}, bf16[128,2048]{1,0:T(8,128)(2,1)}, u32[]{:S(2)}, u32[]{:S(2)}) %collective-permute-start.60) | collective-permute-done | bytes 524320 | tf_op jit(solution)/shard_map/ppermute | solution.py:125
  321.3 1.9 ring_last.3
  324.8 2.3 collective-permute-done.62
  327.2 2.5 collective-permute-start.63
  333.3 3.9 %collective-permute-done.64 = bf16[128,1024]{1,0:T(8,128)(2,1)S(1)} collective-permute-done((bf16[128,1024]{1,0:T(8,128)(2,1)S(1)}, bf16[128,1024]{1,0:T(8,128)(2,1)S(1)}, u32[]{:S(2)}, u32[]{:S(2)}) %collective-permute-start.64) | collective-permute-done | bytes 262176 | tf_op jit(solution)/shard_map/ppermute | solution.py:221
  (372 shorter events, 105.5 us)
Async XLA Ops:
  3.9 9.4 %collective-permute-start.1 = (bf16[128,1024]{1,0:T(8,128)(2,1)S(1)}, bf16[128,1024]{1,0:T(8,128)(2,1)S(1)}, u32[]{:S(2)}, u32[]{:S(2)}) collective-permute-start(bf16[128,1024]{1,0:T(8,128)(2,1)S(1)} %pad_maximum_fusion.5.rest_0_), channel_id=1, source_target_pairs={{4,12},{12,20},{20,28},{28,24},{24,16},{16,8},{8,0},{0,4},{5,13},{... | collective-permute-start | bytes 786440 | tf_op jit(solution)/shard_map/ppermute | solution.py:125
  6.9 7.8 %collective-permute-start.2 = (bf16[128,1024]{1,0:T(8,128)(2,1)S(1)}, bf16[128,1024]{1,0:T(8,128)(2,1)S(1)}, u32[]{:S(2)}, u32[]{:S(2)}) collective-permute-start(bf16[128,1024]{1,0:T(8,128)(2,1)S(1)} %pad_maximum_fusion.5.rest_0_), channel_id=1, source_target_pairs={{4,0},{12,4},{20,12},{28,20},{24,28},{16,24},{8,16},{0,8},{5,1},{1... | collective-permute-start | bytes 786440 | tf_op jit(solution)/shard_map/ppermute | solution.py:128
  7.7 9.3 %collective-permute-start = (bf16[144,1024]{1,0:T(8,128)(2,1)S(1)}, bf16[144,1024]{1,0:T(8,128)(2,1)}, u32[]{:S(2)}, u32[]{:S(2)}) collective-permute-start(bf16[144,1024]{1,0:T(8,128)(2,1)S(1)} %pad_maximum_fusion.4), channel_id=1, source_target_pairs={{0,2},{1,3},{2,0},{3,1},{4,6},{5,7},{6,4},{7,5},{8,10},{9,11},{10,... | collective-permute-start | bytes 884744 | tf_op jit(solution)/shard_map/ppermute | solution.py:221
  15.5 13.1 %collective-permute-start.5 = (bf16[256,1024]{1,0:T(8,128)(2,1)}, bf16[256,1024]{1,0:T(8,128)(2,1)}, u32[]{:S(2)}, u32[]{:S(2)}) collective-permute-start(bf16[256,1024]{1,0:T(8,128)(2,1)} %pad_maximum_fusion), channel_id=1, source_target_pairs={{0,2},{1,3},{2,0},{3,1},{4,6},{5,7},{6,4},{7,5},{8,10},{9,11},{10,... | collective-permute-start | bytes 1572872 | tf_op jit(solution)/shard_map/ppermute | solution.py:221
  17.0 11.5 %collective-permute-start.3 = (bf16[128,1024]{1,0:T(8,128)(2,1)S(1)}, bf16[128,1024]{1,0:T(8,128)(2,1)S(1)}, u32[]{:S(2)}, u32[]{:S(2)}) collective-permute-start(bf16[128,1024]{1,0:T(8,128)(2,1)S(1)} %collective-permute-done.1.rest_1_), channel_id=1, source_target_pairs={{4,12},{12,20},{20,28},{28,24},{24,16},{16,8},{8,0},{0,4},{5,13},{... | collective-permute-start | bytes 786440 | tf_op jit(solution)/shard_map/ppermute | solution.py:125
  18.6 10.0 %collective-permute-start.4 = (bf16[128,1024]{1,0:T(8,128)(2,1)S(1)}, bf16[128,1024]{1,0:T(8,128)(2,1)S(1)}, u32[]{:S(2)}, u32[]{:S(2)}) collective-permute-start(bf16[128,1024]{1,0:T(8,128)(2,1)S(1)} %collective-permute-done.2.rest_2_), channel_id=1, source_target_pairs={{4,0},{12,4},{20,12},{28,20},{24,28},{16,24},{8,16},{0,8},{5,1},{1... | collective-permute-start | bytes 786440 | tf_op jit(solution)/shard_map/ppermute | solution.py:128
  28.6 8.0 %collective-permute-start.6 = (bf16[128,1024]{1,0:T(8,128)(2,1)S(1)}, bf16[128,1024]{1,0:T(8,128)(2,1)S(1)}, u32[]{:S(2)}, u32[]{:S(2)}) collective-permute-start(bf16[128,1024]{1,0:T(8,128)(2,1)S(1)} %collective-permute-done.3.rest_3_), channel_id=1, source_target_pairs={{4,12},{12,20},{20,28},{28,24},{24,16},{16,8},{8,0},{0,4},{5,13},{... | collective-permute-start | bytes 786440 | tf_op jit(solution)/shard_map/ppermute | solution.py:125
  31.5 13.6 %collective-permute-start.10 = (bf16[256,1024]{1,0:T(8,128)(2,1)}, bf16[256,1024]{1,0:T(8,128)(2,1)}, u32[]{:S(2)}, u32[]{:S(2)}) collective-permute-start(bf16[256,1024]{1,0:T(8,128)(2,1)} %pad_maximum_fusion.1), channel_id=1, source_target_pairs={{0,2},{1,3},{2,0},{3,1},{4,6},{5,7},{6,4},{7,5},{8,10},{9,11},{10,... | collective-permute-start | bytes 1572872 | tf_op jit(solution)/shard_map/ppermute | solution.py:221
  41.5 18.4 %collective-permute-start.11 = (bf16[256,1024]{1,0:T(8,128)(2,1)}, bf16[256,1024]{1,0:T(8,128)(2,1)}, u32[]{:S(2)}, u32[]{:S(2)}) collective-permute-start(bf16[256,1024]{1,0:T(8,128)(2,1)} %pad_maximum_fusion.2), channel_id=1, source_target_pairs={{0,2},{1,3},{2,0},{3,1},{4,6},{5,7},{6,4},{7,5},{8,10},{9,11},{10,... | collective-permute-start | bytes 1572872 | tf_op jit(solution)/shard_map/ppermute | solution.py:221
  45.1 14.8 %collective-permute-start.13 = (bf16[128,2048]{1,0:T(8,128)(2,1)}, bf16[128,2048]{1,0:T(8,128)(2,1)}, u32[]{:S(2)}, u32[]{:S(2)}) collective-permute-start(bf16[128,2048]{1,0:T(8,128)(2,1)} %pad_maximum_fusion.3.rest_0_), channel_id=1, source_target_pairs={{4,12},{12,20},{20,28},{28,24},{24,16},{16,8},{8,0},{0,4},{5,13},{... | collective-permute-start | bytes 1572872 | tf_op jit(solution)/shard_map/ppermute | solution.py:125
  46.7 13.2 %collective-permute-start.14 = (bf16[128,2048]{1,0:T(8,128)(2,1)}, bf16[128,2048]{1,0:T(8,128)(2,1)}, u32[]{:S(2)}, u32[]{:S(2)}) collective-permute-start(bf16[128,2048]{1,0:T(8,128)(2,1)} %pad_maximum_fusion.3.rest_0_), channel_id=1, source_target_pairs={{4,0},{12,4},{20,12},{28,20},{24,28},{16,24},{8,16},{0,8},{5,1},{1... | collective-permute-start | bytes 1572872 | tf_op jit(solution)/shard_map/ppermute | solution.py:128
  48.5 11.4 %collective-permute-start.12 = (bf16[128,1024]{1,0:T(8,128)(2,1)}, bf16[128,1024]{1,0:T(8,128)(2,1)}, u32[]{:S(2)}, u32[]{:S(2)}) collective-permute-start(bf16[128,1024]{1,0:T(8,128)(2,1)} %pad_maximum_fusion.6), channel_id=1, source_target_pairs={{0,2},{1,3},{2,0},{3,1},{4,6},{5,7},{6,4},{7,5},{8,10},{9,11},{10,... | collective-permute-start | bytes 786440 | tf_op jit(solution)/shard_map/ppermute | solution.py:221
  59.9 11.8 %collective-permute-start.15 = (bf16[128,2048]{1,0:T(8,128)(2,1)}, bf16[128,2048]{1,0:T(8,128)(2,1)S(1)}, u32[]{:S(2)}, u32[]{:S(2)}) collective-permute-start(bf16[128,2048]{1,0:T(8,128)(2,1)} %collective-permute-done.13.rest_1_), channel_id=1, source_target_pairs={{4,12},{12,20},{20,28},{28,24},{24,16},{16,8},{8,0},{0,4},{5,13},{... | collective-permute-start | bytes 1572872 | tf_op jit(solution)/shard_map/ppermute | solution.py:125
  61.5 11.4 %collective-permute-start.16 = (bf16[128,2048]{1,0:T(8,128)(2,1)}, bf16[128,2048]{1,0:T(8,128)(2,1)S(1)}, u32[]{:S(2)}, u32[]{:S(2)}) collective-permute-start(bf16[128,2048]{1,0:T(8,128)(2,1)} %collective-permute-done.14.rest_2_), channel_id=1, source_target_pairs={{4,0},{12,4},{20,12},{28,20},{24,28},{16,24},{8,16},{0,8},{5,1},{1... | collective-permute-start | bytes 1572872 | tf_op jit(solution)/shard_map/ppermute | solution.py:128
  72.9 16.2 %collective-permute-start.19 = (bf16[1024,2048]{1,0:T(8,128)(2,1)S(1)}, bf16[1024,2048]{1,0:T(8,128)(2,1)S(1)}, u32[]{:S(2)}, u32[]{:S(2)}) collective-permute-start(bf16[1024,2048]{1,0:T(8,128)(2,1)S(1)} %get-tuple-element.218.rest_0_.rest_3_.refs_7_), channel_id=1, source_target_pairs={{0,1},{1,0},{2,3},{3,2},{4,5},{5,4},{6,7},{7,6},{8,9},{9,8},{10,11... | collective-permute-start | bytes 12582920 | tf_op jit(solution)/shard_map/ppermute | solution.py:225
  73.0 16.1 %collective-permute-start.17 = (bf16[128,2048]{1,0:T(8,128)(2,1)S(1)}, bf16[128,2048]{1,0:T(8,128)(2,1)S(1)}, u32[]{:S(2)}, u32[]{:S(2)}) collective-permute-start(bf16[128,2048]{1,0:T(8,128)(2,1)S(1)} %collective-permute-done.15.rest_3_), channel_id=1, source_target_pairs={{4,12},{12,20},{20,28},{28,24},{24,16},{16,8},{8,0},{0,4},{5,13},{... | collective-permute-start | bytes 1572872 | tf_op jit(solution)/shard_map/ppermute | solution.py:125
  74.6 14.5 %collective-permute-start.18 = (bf16[128,2048]{1,0:T(8,128)(2,1)S(1)}, bf16[128,2048]{1,0:T(8,128)(2,1)S(1)}, u32[]{:S(2)}, u32[]{:S(2)}) collective-permute-start(bf16[128,2048]{1,0:T(8,128)(2,1)S(1)} %collective-permute-done.16.rest_4_), channel_id=1, source_target_pairs={{4,0},{12,4},{20,12},{28,20},{24,28},{16,24},{8,16},{0,8},{5,1},{1... | collective-permute-start | bytes 1572872 | tf_op jit(solution)/shard_map/ppermute | solution.py:128
  89.3 8.8 %collective-permute-start.21 = (bf16[64,2048]{1,0:T(8,128)(2,1)S(1)}, bf16[64,2048]{1,0:T(8,128)(2,1)S(1)}, u32[]{:S(2)}, u32[]{:S(2)}) collective-permute-start(bf16[64,2048]{1,0:T(8,128)(2,1)S(1)} %slice.205), channel_id=1, source_target_pairs={{4,12},{12,20},{20,28},{28,24},{24,16},{16,8},{8,0},{0,4},{5,13},{... | collective-permute-start | bytes 786440 | tf_op jit(solution)/shard_map/ppermute | solution.py:125
  90.9 8.4 %collective-permute-start.22 = (bf16[64,2048]{1,0:T(8,128)(2,1)S(1)}, bf16[64,2048]{1,0:T(8,128)(2,1)S(1)}, u32[]{:S(2)}, u32[]{:S(2)}) collective-permute-start(bf16[64,2048]{1,0:T(8,128)(2,1)S(1)} %slice.206), channel_id=1, source_target_pairs={{4,0},{12,4},{20,12},{28,20},{24,28},{16,24},{8,16},{0,8},{5,1},{1... | collective-permute-start | bytes 786440 | tf_op jit(solution)/shard_map/ppermute | solution.py:128
  99.4 26.3 %collective-permute-start.24 = (bf16[528,1024]{1,0:T(8,128)(2,1)S(1)}, bf16[528,1024]{1,0:T(8,128)(2,1)S(1)}, u32[]{:S(2)}, u32[]{:S(2)}) collective-permute-start(bf16[528,1024]{1,0:T(8,128)(2,1)S(1)} %get-tuple-element.225.rest_9_.rest_0_), channel_id=1, source_target_pairs={{0,2},{1,3},{2,0},{3,1},{4,6},{5,7},{6,4},{7,5},{8,10},{9,11},{10,... | collective-permute-start | bytes 3244040 | tf_op jit(solution)/shard_map/ppermute | solution.py:221
  140.4 37.8 %collective-permute-start.27 = (bf16[528,1024]{1,0:T(8,128)(2,1)}, bf16[528,1024]{1,0:T(8,128)(2,1)}, u32[]{:S(2)}, u32[]{:S(2)}) collective-permute-start(bf16[528,1024]{1,0:T(8,128)(2,1)} %get-tuple-element.241), channel_id=1, source_target_pairs={{0,1},{1,0},{2,3},{3,2},{4,5},{5,4},{6,7},{7,6},{8,9},{9,8},{10,11... | collective-permute-start | bytes 3244040 | tf_op jit(solution)/shard_map/ppermute | solution.py:225
  155.5 26.3 %collective-permute-start.28 = (bf16[528,1024]{1,0:T(8,128)(2,1)}, bf16[528,1024]{1,0:T(8,128)(2,1)}, u32[]{:S(2)}, u32[]{:S(2)}) collective-permute-start(bf16[528,1024]{1,0:T(8,128)(2,1)} %get-tuple-element.242), channel_id=1, source_target_pairs={{0,2},{1,3},{2,0},{3,1},{4,6},{5,7},{6,4},{7,5},{8,10},{9,11},{10,... | collective-permute-start | bytes 3244040 | tf_op jit(solution)/shard_map/ppermute | solution.py:221
  156.7 34.1 %collective-permute-start.39 = (bf16[528,1024]{1,0:T(8,128)(2,1)}, bf16[528,1024]{1,0:T(8,128)(2,1)}, u32[]{:S(2)}, u32[]{:S(2)}) collective-permute-start(bf16[528,1024]{1,0:T(8,128)(2,1)} %get-tuple-element.279), channel_id=1, source_target_pairs={{0,1},{1,0},{2,3},{3,2},{4,5},{5,4},{6,7},{7,6},{8,9},{9,8},{10,11... | collective-permute-start | bytes 3244040 | tf_op jit(solution)/shard_map/ppermute | solution.py:225
  176.1 14.6 %collective-permute-start.29 = (bf16[64,2048]{1,0:T(8,128)(2,1)S(1)}, bf16[64,2048]{1,0:T(8,128)(2,1)S(1)}, u32[]{:S(2)}, u32[]{:S(2)}) collective-permute-start(bf16[64,2048]{1,0:T(8,128)(2,1)S(1)} %get-tuple-element.245), channel_id=1, source_target_pairs={{4,12},{12,20},{20,28},{28,24},{24,16},{16,8},{8,0},{0,4},{5,13},{... | collective-permute-start | bytes 786440 | tf_op jit(solution)/shard_map/ppermute | solution.py:125
  177.8 12.9 %collective-permute-start.30 = (bf16[64,2048]{1,0:T(8,128)(2,1)S(1)}, bf16[64,2048]{1,0:T(8,128)(2,1)S(1)}, u32[]{:S(2)}, u32[]{:S(2)}) collective-permute-start(bf16[64,2048]{1,0:T(8,128)(2,1)S(1)} %get-tuple-element.247), channel_id=1, source_target_pairs={{4,0},{12,4},{20,12},{28,20},{24,28},{16,24},{8,16},{0,8},{5,1},{1... | collective-permute-start | bytes 786440 | tf_op jit(solution)/shard_map/ppermute | solution.py:128
  190.7 20.8 %collective-permute-start.34 = (bf16[528,1024]{1,0:T(8,128)(2,1)S(1)}, bf16[528,1024]{1,0:T(8,128)(2,1)S(1)}, u32[]{:S(2)}, u32[]{:S(2)}) collective-permute-start(bf16[528,1024]{1,0:T(8,128)(2,1)S(1)} %get-tuple-element.262.own_ref), channel_id=1, source_target_pairs={{0,1},{1,0},{2,3},{3,2},{4,5},{5,4},{6,7},{7,6},{8,9},{9,8},{10,11... | collective-permute-start | bytes 3244040 | tf_op jit(solution)/shard_map/ppermute | solution.py:225
  194.9 16.6 %collective-permute-start.40 = (bf16[264,1024]{1,0:T(8,128)(2,1)S(1)}, bf16[264,1024]{1,0:T(8,128)(2,1)S(1)}, u32[]{:S(2)}, u32[]{:S(2)}) collective-permute-start(bf16[264,1024]{1,0:T(8,128)(2,1)S(1)} %get-tuple-element.280), channel_id=1, source_target_pairs={{0,2},{1,3},{2,0},{3,1},{4,6},{5,7},{6,4},{7,5},{8,10},{9,11},{10,... | collective-permute-start | bytes 1622024 | tf_op jit(solution)/shard_map/ppermute | solution.py:221
  196.1 14.1 %collective-permute-start.32 = (bf16[128,2048]{1,0:T(8,128)(2,1)S(1)}, bf16[128,2048]{1,0:T(8,128)(2,1)S(1)}, u32[]{:S(2)}, u32[]{:S(2)}) collective-permute-start(bf16[128,2048]{1,0:T(8,128)(2,1)S(1)} %get-tuple-element.256), channel_id=1, source_target_pairs={{4,12},{12,20},{20,28},{28,24},{24,16},{16,8},{8,0},{0,4},{5,13},{... | collective-permute-start | bytes 1572872 | tf_op jit(solution)/shard_map/ppermute | solution.py:125
  197.8 13.8 %collective-permute-start.33 = (bf16[128,2048]{1,0:T(8,128)(2,1)S(1)}, bf16[128,2048]{1,0:T(8,128)(2,1)S(1)}, u32[]{:S(2)}, u32[]{:S(2)}) collective-permute-start(bf16[128,2048]{1,0:T(8,128)(2,1)S(1)} %get-tuple-element.258), channel_id=1, source_target_pairs={{4,0},{12,4},{20,12},{28,20},{24,28},{16,24},{8,16},{0,8},{5,1},{1... | collective-permute-start | bytes 1572872 | tf_op jit(solution)/shard_map/ppermute | solution.py:128
  211.6 19.6 %collective-permute-start.41 = (bf16[1056,768]{1,0:T(8,128)(2,1)S(1)}, bf16[1056,768]{1,0:T(8,128)(2,1)S(1)}, u32[]{:S(2)}, u32[]{:S(2)}) collective-permute-start(bf16[1056,768]{1,0:T(8,128)(2,1)S(1)} %get-tuple-element.281.grad_ref.refs_1_), channel_id=1, source_target_pairs={{0,1},{1,0},{2,3},{3,2},{4,5},{5,4},{6,7},{7,6},{8,9},{9,8},{10,11... | collective-permute-start | bytes 4866056 | tf_op jit(solution)/shard_map/ppermute | solution.py:225
  212.4 18.7 %collective-permute-start.42 = (bf16[264,1024]{1,0:T(8,128)(2,1)S(1)}, bf16[264,1024]{1,0:T(8,128)(2,1)S(1)}, u32[]{:S(2)}, u32[]{:S(2)}) collective-permute-start(bf16[264,1024]{1,0:T(8,128)(2,1)S(1)} %get-tuple-element.282), channel_id=1, source_target_pairs={{0,2},{1,3},{2,0},{3,1},{4,6},{5,7},{6,4},{7,5},{8,10},{9,11},{10,... | collective-permute-start | bytes 1622024 | tf_op jit(solution)/shard_map/ppermute | solution.py:221
  214.1 17.1 %collective-permute-start.35 = (bf16[128,2048]{1,0:T(8,128)(2,1)S(1)}, bf16[128,2048]{1,0:T(8,128)(2,1)S(1)}, u32[]{:S(2)}, u32[]{:S(2)}) collective-permute-start(bf16[128,2048]{1,0:T(8,128)(2,1)S(1)} %get-tuple-element.266), channel_id=1, source_target_pairs={{4,12},{12,20},{20,28},{28,24},{24,16},{16,8},{8,0},{0,4},{5,13},{... | collective-permute-start | bytes 1572872 | tf_op jit(solution)/shard_map/ppermute | solution.py:125
  214.7 16.4 %collective-permute-start.36 = (bf16[128,2048]{1,0:T(8,128)(2,1)S(1)}, bf16[128,2048]{1,0:T(8,128)(2,1)S(1)}, u32[]{:S(2)}, u32[]{:S(2)}) collective-permute-start(bf16[128,2048]{1,0:T(8,128)(2,1)S(1)} %get-tuple-element.268), channel_id=1, source_target_pairs={{4,0},{12,4},{20,12},{28,20},{24,28},{16,24},{8,16},{0,8},{5,1},{1... | collective-permute-start | bytes 1572872 | tf_op jit(solution)/shard_map/ppermute | solution.py:128
  216.2 17.7 %collective-permute-start.46 = (bf16[528,1024]{1,0:T(8,128)(2,1)S(1)}, bf16[528,1024]{1,0:T(8,128)(2,1)S(1)}, u32[]{:S(2)}, u32[]{:S(2)}) collective-permute-start(bf16[528,1024]{1,0:T(8,128)(2,1)S(1)} %copy-done.84), channel_id=1, source_target_pairs={{0,1},{1,0},{2,3},{3,2},{4,5},{5,4},{6,7},{7,6},{8,9},{9,8},{10,11... | collective-permute-start | bytes 3244040 | tf_op jit(solution)/shard_map/ppermute | solution.py:225
  232.6 12.4 %collective-permute-start.43 = (bf16[1056,768]{1,0:T(8,128)(2,1)S(1)}, bf16[1056,768]{1,0:T(8,128)(2,1)S(1)}, u32[]{:S(2)}, u32[]{:S(2)}) collective-permute-start(bf16[1056,768]{1,0:T(8,128)(2,1)S(1)} %get-tuple-element.283.grad_ref.refs_0_), channel_id=1, source_target_pairs={{0,1},{1,0},{2,3},{3,2},{4,5},{5,4},{6,7},{7,6},{8,9},{9,8},{10,11... | collective-permute-start | bytes 4866056 | tf_op jit(solution)/shard_map/ppermute | solution.py:225
  236.0 23.1 %collective-permute-start.47 = (bf16[264,1024]{1,0:T(8,128)(2,1)S(1)}, bf16[264,1024]{1,0:T(8,128)(2,1)S(1)}, u32[]{:S(2)}, u32[]{:S(2)}) collective-permute-start(bf16[264,1024]{1,0:T(8,128)(2,1)S(1)} %get-tuple-element.295), channel_id=1, source_target_pairs={{0,2},{1,3},{2,0},{3,1},{4,6},{5,7},{6,4},{7,5},{8,10},{9,11},{10,... | collective-permute-start | bytes 1622024 | tf_op jit(solution)/shard_map/ppermute | solution.py:221
  237.3 14.8 %collective-permute-start.37 = (bf16[128,2048]{1,0:T(8,128)(2,1)S(1)}, bf16[128,2048]{1,0:T(8,128)(2,1)S(1)}, u32[]{:S(2)}, u32[]{:S(2)}) collective-permute-start(bf16[128,2048]{1,0:T(8,128)(2,1)S(1)} %get-tuple-element.274), channel_id=1, source_target_pairs={{4,12},{12,20},{20,28},{28,24},{24,16},{16,8},{8,0},{0,4},{5,13},{... | collective-permute-start | bytes 1572872 | tf_op jit(solution)/shard_map/ppermute | solution.py:125
  238.2 14.8 %collective-permute-start.38 = (bf16[128,2048]{1,0:T(8,128)(2,1)S(1)}, bf16[128,2048]{1,0:T(8,128)(2,1)S(1)}, u32[]{:S(2)}, u32[]{:S(2)}) collective-permute-start(bf16[128,2048]{1,0:T(8,128)(2,1)S(1)} %get-tuple-element.276), channel_id=1, source_target_pairs={{4,0},{12,4},{20,12},{28,20},{24,28},{16,24},{8,16},{0,8},{5,1},{1... | collective-permute-start | bytes 1572872 | tf_op jit(solution)/shard_map/ppermute | solution.py:128
  245.0 11.9 %collective-permute-start.44 = (bf16[64,2048]{1,0:T(8,128)(2,1)S(1)}, bf16[64,2048]{1,0:T(8,128)(2,1)S(1)}, u32[]{:S(2)}, u32[]{:S(2)}) collective-permute-start(bf16[64,2048]{1,0:T(8,128)(2,1)S(1)} %get-tuple-element.284), channel_id=1, source_target_pairs={{4,12},{12,20},{20,28},{28,24},{24,16},{16,8},{8,0},{0,4},{5,13},{... | collective-permute-start | bytes 786440 | tf_op jit(solution)/shard_map/ppermute | solution.py:125
  246.0 11.6 %collective-permute-start.45 = (bf16[64,2048]{1,0:T(8,128)(2,1)S(1)}, bf16[64,2048]{1,0:T(8,128)(2,1)S(1)}, u32[]{:S(2)}, u32[]{:S(2)}) collective-permute-start(bf16[64,2048]{1,0:T(8,128)(2,1)S(1)} %get-tuple-element.286), channel_id=1, source_target_pairs={{4,0},{12,4},{20,12},{28,20},{24,28},{16,24},{8,16},{0,8},{5,1},{1... | collective-permute-start | bytes 786440 | tf_op jit(solution)/shard_map/ppermute | solution.py:128
  253.7 22.4 %collective-permute-start.50 = (bf16[264,1024]{1,0:T(8,128)(2,1)}, bf16[264,1024]{1,0:T(8,128)(2,1)}, u32[]{:S(2)}, u32[]{:S(2)}) collective-permute-start(bf16[264,1024]{1,0:T(8,128)(2,1)} %get-tuple-element.301), channel_id=1, source_target_pairs={{0,2},{1,3},{2,0},{3,1},{4,6},{5,7},{6,4},{7,5},{8,10},{9,11},{10,... | collective-permute-start | bytes 1622024 | tf_op jit(solution)/shard_map/ppermute | solution.py:221
  260.0 14.0 %collective-permute-start.48 = (bf16[128,2048]{1,0:T(8,128)(2,1)}, bf16[128,2048]{1,0:T(8,128)(2,1)S(1)}, u32[]{:S(2)}, u32[]{:S(2)}) collective-permute-start(bf16[128,2048]{1,0:T(8,128)(2,1)} %get-tuple-element.296), channel_id=1, source_target_pairs={{4,12},{12,20},{20,28},{28,24},{24,16},{16,8},{8,0},{0,4},{5,13},{... | collective-permute-start | bytes 1572872 | tf_op jit(solution)/shard_map/ppermute | solution.py:125
  260.5 13.4 %collective-permute-start.49 = (bf16[128,2048]{1,0:T(8,128)(2,1)}, bf16[128,2048]{1,0:T(8,128)(2,1)}, u32[]{:S(2)}, u32[]{:S(2)}) collective-permute-start(bf16[128,2048]{1,0:T(8,128)(2,1)} %get-tuple-element.298), channel_id=1, source_target_pairs={{4,0},{12,4},{20,12},{28,20},{24,28},{16,24},{8,16},{0,8},{5,1},{1... | collective-permute-start | bytes 1572872 | tf_op jit(solution)/shard_map/ppermute | solution.py:128
  279.5 26.6 %collective-permute-start.57 = (bf16[528,1024]{1,0:T(8,128)(2,1)}, bf16[528,1024]{1,0:T(8,128)(2,1)}, u32[]{:S(2)}, u32[]{:S(2)}) collective-permute-start(bf16[528,1024]{1,0:T(8,128)(2,1)} %get-tuple-element.321.refs_0_), channel_id=1, source_target_pairs={{0,2},{1,3},{2,0},{3,1},{4,6},{5,7},{6,4},{7,5},{8,10},{9,11},{10,... | collective-permute-start | bytes 3244040 | tf_op jit(solution)/shard_map/ppermute | solution.py:221
  283.6 15.2 %collective-permute-start.54 = (bf16[128,2048]{1,0:T(8,128)(2,1)}, bf16[128,2048]{1,0:T(8,128)(2,1)S(1)}, u32[]{:S(2)}, u32[]{:S(2)}) collective-permute-start(bf16[128,2048]{1,0:T(8,128)(2,1)} %copy-done.49), channel_id=1, source_target_pairs={{4,12},{12,20},{20,28},{28,24},{24,16},{16,8},{8,0},{0,4},{5,13},{... | collective-permute-start | bytes 1572872 | tf_op jit(solution)/shard_map/ppermute | solution.py:125
  284.2 14.6 %collective-permute-start.55 = (bf16[128,2048]{1,0:T(8,128)(2,1)}, bf16[128,2048]{1,0:T(8,128)(2,1)S(1)}, u32[]{:S(2)}, u32[]{:S(2)}) collective-permute-start(bf16[128,2048]{1,0:T(8,128)(2,1)} %copy-done.48), channel_id=1, source_target_pairs={{4,0},{12,4},{20,12},{28,20},{24,28},{16,24},{8,16},{0,8},{5,1},{1... | collective-permute-start | bytes 1572872 | tf_op jit(solution)/shard_map/ppermute | solution.py:128
  307.2 13.9 %collective-permute-start.60 = (bf16[128,2048]{1,0:T(8,128)(2,1)}, bf16[128,2048]{1,0:T(8,128)(2,1)}, u32[]{:S(2)}, u32[]{:S(2)}) collective-permute-start(bf16[128,2048]{1,0:T(8,128)(2,1)} %copy-done.51), channel_id=1, source_target_pairs={{4,12},{12,20},{20,28},{28,24},{24,16},{16,8},{8,0},{0,4},{5,13},{... | collective-permute-start | bytes 1572872 | tf_op jit(solution)/shard_map/ppermute | solution.py:125
  307.7 13.6 %collective-permute-start.61 = (bf16[128,2048]{1,0:T(8,128)(2,1)}, bf16[128,2048]{1,0:T(8,128)(2,1)}, u32[]{:S(2)}, u32[]{:S(2)}) collective-permute-start(bf16[128,2048]{1,0:T(8,128)(2,1)} %copy-done.50), channel_id=1, source_target_pairs={{4,0},{12,4},{20,12},{28,20},{24,28},{16,24},{8,16},{0,8},{5,1},{1... | collective-permute-start | bytes 1572872 | tf_op jit(solution)/shard_map/ppermute | solution.py:128
  (106 other events, 870.4 us)

commit v2 on v1

--- a/solution.py
+++ b/solution.py
@@ -35,9 +35,10 @@
     "ring_first": 4,
     "ring_add": 10,
     "ring_last": 8,
+    "ring_end": 8,
     "qkv": 20,
     "pad": 20,
-    "assemble": 20,
+    "assemble": 58,
     "first_low": 10,
     "attend": 10,
     "attend_back": 12,
@@ -48,6 +49,9 @@
     "qkv_grad": 20,
     "first_norm": 58,
 }
+
+
+COST = {"ring_end": 2 * 10**10}
 
 
 def call(body, grid, in_specs, out_specs, out_shape, scratch, name, aliases=None):
@@ -64,7 +68,9 @@
         compiler_params=pltpu.CompilerParams(
             dimension_semantics=("arbitrary",) * len(grid), vmem_limit_bytes=ROOM[name] * 2**20
         ),
-        cost_estimate=pl.CostEstimate(flops=1, bytes_accessed=1, transcendentals=0),
+        cost_estimate=pl.CostEstimate(
+            flops=COST.get(name, 1), bytes_accessed=1, transcendentals=0
+        ),
         name=name,
         input_output_aliases=aliases or {},
     )
@@ -163,7 +169,7 @@
             np.int32,
         )
 
-    def scatter_steps(self, whole, ranks, order):
+    def scatter_steps(self, whole, ranks, order, last="ring_last"):
         middle = self.count // 2
         dim, columns = whole.shape
         rows = dim // self.count
@@ -209,7 +215,7 @@
             plain(rows),
             shape((rows, columns), f32),
             [],
-            "ring_last",
+            last,
         )
         yield order.run(kernel, whole, forward, backward)
 
@@ -626,6 +632,7 @@
 
 def first_norm_body(info, *refs, chips):
     grads, (x_ref, res_ref, gain_ref, *rest) = refs[: 2 * chips], refs[2 * chips :]
+    two_ref, biases, hiddens, rest = rest[0], rest[1 : 1 + chips], rest[1 + chips : 4 + chips], rest[4 + chips :]
     wholes, (low_ref, sum_ref, weights, lefts, total, sems) = rest[:2], rest[2:]
     half, width = lefts.shape[1:]
     part = wholes[0].shape[1] // chips
@@ -651,6 +658,17 @@
     lax.fori_loop(0, 2 * chips, term, 0)
     step = row_step(total.shape[0])
     sum_ref[...] = jnp.zeros_like(sum_ref)
+    for i, j in enumerate((2, 0, 1, 3)):
+        sum_ref[2 + i : 3 + i, :] = two_ref[j : j + 1, :]
+    pairs = biases[0].shape[0]
+    for b in range(chips):
+        for kind in range(2):
+            for pair in range(pairs):
+                to = ((b * 2 + kind) * pairs + pair) * LANES
+                value = biases[b][pair, :, kind * 2 * LANES : (kind * 2 + 1) * LANES]
+                sum_ref[6:7, to : to + LANES] = value
+    ff = hiddens[0].shape[1]
+    sum_ref[7:8, 0:ff] = hiddens[0][...] + hiddens[1][...] + hiddens[2][...]
 
     def rows(i, _):
         at = pl.ds(pl.multiple_of(i * step, 16), step)
@@ -940,7 +958,6 @@
         return terms + [across(value, chips - 1 - i, chips) for i, value in enumerate(sums)]
 
     back_terms = along_x(first[2], own[2])
-    expand_bias_grad = (first[4] + other[4] + own[4]).reshape(ff)
     span = 2 * CHUNK
     total_rows = len(keys) * half
     kernel = call(
@@ -1001,8 +1018,9 @@
         out_near = (out_near + partner(order.after(first[3][1]), chips).astype(f32)).astype(bf16)
         out_far = own[3][0].astype(f32)
         out_far = (out_far + partner(other[3][0], chips).astype(f32)).astype(bf16)
-        cut = half // 2
-        out_sends = iter([out_far[:cut], out_far[cut:], out_near[:cut], out_near[cut:]])
+        out_rows = jnp.concatenate([out_far, out_near])
+        cuts = [0, half // 16 * 8, half * 5 // 32 * 8, 2 * half]
+        out_sends = iter([out_rows[i:j] for i, j in zip(cuts, cuts[1:])])
         out_gots = [across(order.after(next(out_sends)), 1, chips)]
     else:
         out_own = [
@@ -1071,9 +1089,9 @@
         )
 
     def out_due(i):
-        if chips != 2 or i > 3:
+        if chips != 2:
             return ()
-        if i < 3:
+        if i < 2:
             out_gots.append(across(order.after(next(out_sends)), 1, chips))
         return out_gots[i]
 
@@ -1090,22 +1108,34 @@
     grads_other[0] = partner(order.after(grads_qkv[0]), chips)
     order.due = ()
     mlp_due = next(mlp_ring, ())
-    attn_ring = ring.scatter_steps(qkv_grad(0, begun), ranks, order)
+    attn_ring = ring.scatter_steps(qkv_grad(0, begun), ranks, order, "ring_end")
     order.due = [grads_other[b] for b in range(chips)]
-    next(attn_ring)
+    order.hold = next(attn_ring)
     order.due = ()
     for mlp_grad in mlp_ring:
         pass
     expand_part, shrink_part = mlp_grad[:, :ff], mlp_grad[:, ff:].T
-    order.due = out_due(2)
+    out_due(2)
+    if chips == 2:
+        out_rows = jnp.concatenate([out_near, out_far]).astype(f32)
+        out_rows = out_rows + jnp.concatenate(order.after(out_gots)).astype(f32)
+    else:
+        out_rows = order.after(residual) + shrink_bias
+        for term in out_terms:
+            out_rows = out_rows + term.astype(f32)
+        low = out_rows.astype(bf16)
+        out_rows = jnp.concatenate([low] + [across(low, step, chips) for step in range(1, chips)])
+    out_rows = out_rows.astype(bf16)
+    order.hold = out_rows
     attn_due = next(attn_ring)
-    order.due = ()
 
     kernel = call(
         functools.partial(first_norm_body, chips=chips),
         (1,),
         [own_half(half, width)] * (2 * chips)
-        + [own_place(half, dim), whole(half, dim), whole(1, dim)]
+        + [own_place(half, dim), whole(half, dim), whole(1, dim), whole(8, dim)]
+        + [whole(pairs, 1, 3 * LANES)] * chips
+        + [whole(1, ff)] * 3
         + [HBM] * 2,
         [whole(half, dim), whole(8, dim)],
         [shape((half, dim), bf16), shape((8, dim), f32)],
@@ -1117,13 +1147,18 @@
         ],
         "first_norm",
     )
-    tokens_low, sums_one = order.run(
+    tokens_low, small = order.run(
         kernel,
         *[grads_qkv[b] for b in range(chips)],
         *[grads_other[b] for b in range(chips)],
         x_rows,
         grad_residual,
         row(first_gain),
+        sums_two,
+        *[qkv_sums[b] for b in range(chips)],
+        first[4],
+        other[4],
+        own[4],
         *both_weights,
     )
 
@@ -1143,45 +1178,17 @@
         )
         return order.run(kernel, *[rows[key][0] for key in keys])
 
-    order.due = attn_due, out_due(3)
-    tokens_low = order.after(tokens_low)
-    order.due = ()
-    grads, outs = {(0, 0): (tokens_low, 0)}, {}
-    for step in range(1, chips):
-        grads[(step, 0)] = across(tokens_low, step, chips), 0
-    next(attn_ring)
-    if chips == 2:
-        out_rows = jnp.concatenate([out_near, out_far]).astype(f32)
-        out_rows = out_rows + jnp.concatenate(order.after(out_gots)).astype(f32)
-    else:
-        out_rows = order.after(residual) + shrink_bias
-        for term in out_terms:
-            out_rows = out_rows + term.astype(f32)
-        low = out_rows.astype(bf16)
-        out_rows = jnp.concatenate([low] + [across(low, step, chips) for step in range(1, chips)])
-    out_rows = out_rows.astype(bf16)
-    out_other = partner(out_rows, chips)
-    for step in range(chips):
-        outs[(step, 0)], outs[(step, 1)] = (out_rows, step), (out_other, step)
-
-    bias_sums = jnp.stack([qkv_sums[b] for b in range(chips)]).reshape(chips, pairs, 3, LANES)
-    bias_sums = jnp.stack([bias_sums[:, :, 0], bias_sums[:, :, 2]], axis=1)
-    hidden_sums = jnp.pad(expand_bias_grad, (0, -ff % dim)).reshape(-1, dim)
-    shared = jnp.concatenate([sums_one[0:2], sums_two[2:3], sums_two[0:2], sums_two[3:4]])
-    shared = shared + partner(shared, chips)
-    small = jnp.concatenate([shared, bias_sums.reshape(-1, dim), hidden_sums])
     bits = [1 << i for i in range(ring.count.bit_length() - 1)]
 
-    def add_ranks(small, bit):
-        pairs = [(r, r ^ bit) for r in range(ring.count)]
-        return small + lax.ppermute(order.after(small), "dp", pairs)
+    def from_rank(small, bit):
+        return lax.ppermute(small, "dp", [(r, r ^ bit) for r in range(ring.count)])
 
     def add_chips(small):
-        shared = small[:6]
+        shared = small[:6] + partner(small[:6], chips)
         own, *others = small[6:7].reshape(chips, 2 * part)
         if chips == 2:
             sent = jnp.concatenate([shared.reshape(-1), others[0]])
-            got = across(order.after(sent), 1, chips)
+            got = across(sent, 1, chips)
             shared = shared + got[: 6 * dim].reshape(6, dim)
             own = own + got[6 * dim :]
         else:
@@ -1195,26 +1202,47 @@
         own = jnp.pad(own, (0, dim - 2 * part)).reshape(1, dim)
         return jnp.concatenate([shared, own, small[7:]])
 
+    order.due = attn_due
+    tokens_low = order.after(tokens_low)
+    grads, outs = {(0, 0): (tokens_low, 0)}, {}
+    for step in range(1, chips):
+        grads[(step, 0)] = across(tokens_low, step, chips), 0
+    order.due = ()
+    next(attn_ring)
+    out_other = partner(order.after(out_rows), chips)
+    for step in range(chips):
+        outs[(step, 0)], outs[(step, 1)] = (out_rows, step), (out_other, step)
+
+    got = from_rank(order.after(small), bits[0])
     outputs = assemble(outs, bf16)
-    small = add_ranks(small, bits[0])
-    order.hold = (small, expand_part, shrink_part)
+    small = small + order.after(got)
+    order.hold = (expand_part, shrink_part)
+    order.due = small
     next(attn_ring)
+    order.due = ()
     grads[(0, 1)] = partner(order.after(tokens_low), chips), 0
     for step in range(1, chips):
         grads[(step, 1)] = partner(order.after(grads[(step, 0)][0]), chips), 0
-    small = add_chips(small)
-    grad_tokens = assemble(grads, f32)
+    small = add_chips(order.after(small))
     for attn_sum in attn_ring:
         pass
-    for bit in bits[1:]:
-        small = add_ranks(small, bit)
+    small = order.after(small)
+    attn_low = order.after(attn_sum.astype(bf16))
+    sent = {}
+    for step in range(1, chips):
+        columns = slice(step * (width + part), (step + 1) * (width + part))
+        sent[step] = across(attn_low[:, columns], chips - step, chips)
+    got = from_rank(small, bits[1])
+    grad_tokens = assemble(grads, f32)
+    small = small + order.after(got)
+    for bit in bits[2:]:
+        small = small + from_rank(small, bit)
     shared = small[:6]
     bias_own = small[6, : 2 * part].reshape(2, part)
     expand_bias_grad = small[7:].reshape(-1)[:ff]
     attn_part = attn_sum[:, : width + part]
     for step in range(1, chips):
-        sent = attn_sum[:, step * (width + part) : (step + 1) * (width + part)].astype(bf16)
-        attn_part = attn_part + across(sent, chips - step, chips).astype(f32)
+        attn_part = attn_part + order.after(sent[step]).astype(f32)
 
     qkv_part = attn_part[:, :width].reshape(unit_rows, pairs, 3, LANES)
     qkv_part = qkv_part.transpose(0, 2, 1, 3).reshape(unit_rows, 3, part)

time: 340 us -> 329 us (0.968)
  waiting for transfers between devices: 65.3 us -> 57.4 us
  local copies, waits for them, and re-layouts: 41.4 us -> 35.7 us
    ppermute x3, waiting for transfers between devices: 8.1 us -> 1.09 us  [from_rank(): return lax.ppermute(small, 'dp', [(r, r ^ bit) for r in range(ring.count)])]
    ppermute x16, waiting for transfers between devices: 20.4 us -> 26.3 us  [send_ahead(): return lax.ppermute(value, 'dp', self.ahead)]
    unnamed x184 -> x155, local copies, waits for them, and re-layouts: 32.8 us -> 29.1 us
    ppermute x14 -> x13, waiting for transfers between devices: 19.2 us -> 15.9 us  [across(): return lax.ppermute(value, 'mp', pairs)]
    ppermute x14 -> x13, starting transfers between devices: 15.9 us -> 16.9 us  [across(): return lax.ppermute(value, 'mp', pairs)]
  transfers between devices with their start and end apart: 65 -> 64, of which waited for: 29 -> 25; matrix products, arithmetic and copies ran while one was open for 6% -> 6% of each run, Pallas kernels for 43% -> 45%
where the time goes in v2:
time: 329 us; the launch traced here: 328 us
  Pallas kernels  162 us (49%)
  waiting for transfers between devices  57.4 us (17%)
  starting transfers between devices  57.1 us (17%)
  local copies, waits for them, and re-layouts  35.7 us (11%)
  other arithmetic  13.8 us (4%)
    pallas_call x28, Pallas kernels, run(): out = kernel(tie(self.info, self.now, wait, self.hold), *values)  162 us
    unnamed x155, local copies, waits for them, and re-layouts  29.1 us
    ppermute x16, waiting for transfers between devices, send_ahead(): return lax.ppermute(value, 'dp', self.ahead)  26.3 us
    ppermute x16, starting transfers between devices, send_ahead(): return lax.ppermute(value, 'dp', self.ahead)  20.4 us
    ppermute x13, starting transfers between devices, across(): return lax.ppermute(value, 'mp', pairs)  16.9 us
    ppermute x13, waiting for transfers between devices, across(): return lax.ppermute(value, 'mp', pairs)  15.9 us
    ppermute x16, starting transfers between devices, send_behind(): return lax.ppermute(value, 'dp', self.behind)  13.6 us
    ppermute x16, waiting for transfers between devices, partner(): return lax.ppermute(value, 'mp', [(m, m ^ 1) for m in range(2 * chips)])  7.3 us
  transfers between devices with their start and end apart: 64, of which 25 were waited for; matrix products, arithmetic and copies ran while one was open for 6% of the time, Pallas kernels for 45%

profile of v2, /device:TPU:0, one launch (start us, length us, event | category | flops | bytes accessed | tf_op | source)
XLA Modules:
  0.0 328.1 jit_solution(464276275680407324)
XLA Ops:
  3.9 3.0 collective-permute-start.1
  7.7 1.9 collective-permute-start
  9.7 3.6 %collective-permute-done.1.rest_1_ = bf16[128,1024]{1,0:T(8,128)(2,1)S(1)} collective-permute-done((bf16[128,1024]{1,0:T(8,128)(2,1)S(1)}, bf16[128,1024]{1,0:T(8,128)(2,1)S(1)}, u32[]{:S(2)}, u32[]{:S(2)}) %collective-permute-start.1) | collective-permute-done | bytes 262176 | tf_op jit(solution)/shard_map/ppermute | solution.py:131
  19.0 2.2 copy-done.23
  21.2 3.0 pad.83.x_ref.refs_4_
  24.3 2.1 first_low.1.x_ref.first_ref
  26.4 2.0 copy-done.8
  32.8 1.8 convert_element_type.99
  34.7 1.9 copy.90
  38.7 1.9 pad_maximum_fusion.4.rest_0_
  43.3 1.7 collective-permute-done.10.rest_11_
  52.2 2.2 copy-done.24
  54.4 3.0 pad.84.cot_ref
  57.4 2.0 copy-done.7
  62.7 7.3 %qkv.1 = (bf16[1056,1536]{1,0:T(8,128)(2,1)S(1)}, bf16[1024,2048]{1,0:T(8,128)(2,1)S(1)}) custom-call(s32[24]{0:T(128)S(1)} %concatenate.49.info, bf16[1056,1024]{1,0:T(8,128)(2,1)S(1)} %first_low.1.x_ref.first_ref, f32[1,1536]{1,0:T(1,128)S(1)} %pad_maximum_fusion.10.bias_ref, bf16[128,1024]{1,0:T(8,128)(2,1)S(1)} %pad_maximum_fusion.6.rest_0_, ...), custom_call_target="tpu_custom_call" | custom-call | flops 1 | bytes 1 | tf_op jit(solution)/shard_map/qkv/pallas_call | solution.py:94
  75.0 12.4 %attend.1 = (bf16[1056,512]{1,0:T(8,128)(2,1)S(1)}, f32[3,4,2,352]{3,2,1,0:T(2,128)S(1)}) custom-call(s32[24]{0:T(128)S(1)} %concatenate.49.info, bf16[1056,1536]{1,0:T(8,128)(2,1)S(1)} %get-tuple-element.207.qkv_ref, s32[3,352,1]{2,1,0:T(8,128)S(1)} %broadcast_select_fusion.key_ids, s32[3,1,352]{2,1,0:T(1,128)S(1)} %broadcast_select_fusion.1.query_ids), custom_call_target="tpu_custom_call" | custom-call | flops 1 | bytes 1 | tf_op jit(solution)/shard_map/attend/pallas_call | solution.py:94
  87.4 1.7 copy-done.15
  91.9 3.3 %proj_norm.1 = (f32[528,1024]{1,0:T(8,128)S(1)}, bf16[528,1024]{1,0:T(8,128)(2,1)S(1)}) custom-call(s32[24]{0:T(128)S(1)} %concatenate.49.info, bf16[1056,512]{1,0:T(8,128)(2,1)S(1)} %get-tuple-element.221.own_ref.att_own.att_got, bf16[1056,512]{1,0:T(8,128)(2,1)S(1)} %collective-permute-done.20.got_ref, bf16[2112,1024]{1,0:T(8,128)(2,1)S(1)} %bitcast.57, ...), custom_call_target="tpu_custom_call" | custom-call | flops 1 | bytes 1 | tf_op jit(solution)/shard_map/proj_norm/pallas_call | solution.py:94
  103.0 19.3 %mlp.3 = (bf16[1056,1024]{1,0:T(8,128)(2,1)}, bf16[1056,1024]{1,0:T(8,128)(2,1)}, bf16[528,1024]{1,0:T(8,128)(2,1)}, bf16[528,1024]{1,0:T(8,128)(2,1)}, bf16[528...) custom-call(s32[24]{0:T(128)} %copy-done.39, bf16[2112,1024]{1,0:T(8,128)(2,1)} %copy-done.7, ...), custom_call_target="tpu_custom_call" | custom-call | flops 1 | bytes 1 | tf_op jit(solution)/shard_map/mlp/pallas_call | solution.py:94
  122.3 3.3 %collective-permute-done.24.rest_9_.rest_3_ = bf16[528,1024]{1,0:T(8,128)(2,1)S(1)} collective-permute-done((bf16[528,1024]{1,0:T(8,128)(2,1)S(1)}, bf16[528,1024]{1,0:T(8,128)(2,1)S(1)}, u32[]{:S(2)}, u32[]{:S(2)}) %collective-permute-start.24) | collective-permute-done | bytes 1081376 | tf_op jit(solution)/shard_map/ppermute | solution.py:227
  125.6 2.7 collective-permute-done.25.rest_9_.rest_2_
  129.3 10.9 %mlp.4 = (bf16[528,1024]{1,0:T(8,128)(2,1)}, bf16[528,1024]{1,0:T(8,128)(2,1)}, bf16[528,1024]{1,0:T(8,128)(2,1)}, bf16[528,1024]{1,0:T(8,128)(2,1)}, f32[1,1024]{1,0:T(1,128)}) custom-call(s32[24]{0:T(128)} %copy-done.39, bf16[2112,1024]{1,0:T(8,128)(2,1)} %copy-done.7, f32[1,1024]{1,0:T(1,128)} %bitcast.75, bf16[128,2048]{1,0:T(8,128)(2,1)} %pad_maximum_fusion.4.rest_0_, ...), custom_call_target="tpu_custom_call" | custom-call | flops 1 | bytes 1 | tf_op jit(solution)/shard_map/mlp/pallas_call | solution.py:94
  140.8 2.6 collective-permute-done.26.rest_10_
  144.3 11.2 %mlp.5 = (bf16[528,1024]{1,0:T(8,128)(2,1)}, bf16[528,1024]{1,0:T(8,128)(2,1)}, bf16[528,1024]{1,0:T(8,128)(2,1)}, bf16[528,1024]{1,0:T(8,128)(2,1)}, f32[1,1024]{1,0:T(1,128)}) custom-call(s32[24]{0:T(128)} %copy-done.39, bf16[2112,1024]{1,0:T(8,128)(2,1)} %copy-done.7, f32[1,1024]{1,0:T(1,128)} %bitcast.76, bf16[128,2048]{1,0:T(8,128)(2,1)} %pad_maximum_fusion.4.rest_0_, ...), custom_call_target="tpu_custom_call" | custom-call | flops 1 | bytes 1 | tf_op jit(solution)/shard_map/mlp/pallas_call | solution.py:94
  156.9 16.5 %mlp_grad.1.ahead_ref.behind_ref.own_ref = bf16[1024,2048]{1,0:T(8,128)(2,1)} custom-call(s32[24]{0:T(128)} %copy-done.39, bf16[2112,1024]{1,0:T(8,128)(2,1)} %copy-done.7, bf16[528,1024]{1,0:T(8,128)(2,1)} %copy-done.22, bf16[528,1024]{1,0:T(8,128)(2,1)} %copy-done.55, bf16[528,1024]{1,0:T(8,128)(2,1)} %copy-done.57, bf16[528,1024]{1,0:T(8,128)(2,1)} %copy-done.56, ...), custom_call_target="tpu_custom_call" | custom-call | flops 1 | bytes 1 | tf_op jit(solution)/shard_map/mlp_grad/pallas_call | solution.py:94
  173.4 2.2 copy-done.5
  178.3 3.5 %collective-permute-done.28.rest_2_ = bf16[528,1024]{1,0:T(8,128)(2,1)} collective-permute-done((bf16[528,1024]{1,0:T(8,128)(2,1)}, bf16[528,1024]{1,0:T(8,128)(2,1)}, u32[]{:S(2)}, u32[]{:S(2)}) %collective-permute-start.28) | collective-permute-done | bytes 1081376 | tf_op jit(solution)/shard_map/ppermute | solution.py:227
  184.7 6.3 %residual_back.1 = (f32[528,1024]{1,0:T(8,128)S(1)}, bf16[528,1024]{1,0:T(8,128)(2,1)S(1)}, bf16[528,512]{1,0:T(8,128)(2,1)S(1)}, bf16[528,512]{1,0:T(8,128)(2,1)S(1)}, f32[8,1024]{1,0:T(8,128)S(1)}) custom-call(s32[24]{0:T(128)S(1)} %copy-done.40, f32[528,1024]{1,0:T(8,128)S(1)} %copy-done.18, bf16[2112,1024]{1,0:T(8,128)(2,1)S(1)} %bitcast.55, ...), custom_call_target="tpu_custom_call" | custom-call | flops 1 | bytes 1 | tf_op jit(solution)/shard_map/residual_back/pallas_call | solution.py:94
  193.4 1.8 add_convert_fusion.2
  198.6 9.8 %attend_back.2 = (bf16[1056,768]{1,0:T(8,128)(2,1)S(1)}, f32[2,1,384]{2,1,0:T(1,128)S(1)}) custom-call(s32[24]{0:T(128)S(1)} %copy-done.40, bf16[1056,1536]{1,0:T(8,128)(2,1)S(1)} %copy-done.16, s32[3,352,1]{2,1,0:T(8,128)S(1)} %broadcast_select_fusion.key_ids, s32[3,1,352]{2,1,0:T(1,128)S(1)} %broadcast_select_fusion.1.query_ids, ...), custom_call_target="tpu_custom_call" | custom-call | flops 1 | bytes 1 | tf_op jit(solution)/shard_map/attend_back/pallas_call | solution.py:94
  208.4 1.9 collective-permute-done.32.got_ahead
  216.0 5.1 %qkv_grad.2.rest_0_ = bf16[1024,2048]{1,0:T(8,128)(2,1)S(1)} custom-call(s32[24]{0:T(128)S(1)} %copy-done.40, bf16[1056,1024]{1,0:T(8,128)(2,1)S(1)} %copy-done.14, bf16[1056,768]{1,0:T(8,128)(2,1)S(1)} %get-tuple-element.278.grad_ref.refs_1_, bf16[528,1024]{1,0:T(8,128)(2,1)S(1)} %get-tuple-element.264.own_ref, ...), custom_call_target="tpu_custom_call" | custom-call | flops 1 | bytes 1 | tf_op jit(solution)/shard_map/qkv_grad/pallas_call | solution.py:94
  221.1 9.8 %attend_back.3 = (bf16[1056,768]{1,0:T(8,128)(2,1)S(1)}, f32[2,1,384]{2,1,0:T(1,128)S(1)}) custom-call(s32[24]{0:T(128)S(1)} %copy-done.40, bf16[1056,1536]{1,0:T(8,128)(2,1)S(1)} %copy-done.16, s32[3,352,1]{2,1,0:T(8,128)S(1)} %broadcast_select_fusion.key_ids, s32[3,1,352]{2,1,0:T(1,128)S(1)} %broadcast_select_fusion.1.query_ids, ...), custom_call_target="tpu_custom_call" | custom-call | flops 1 | bytes 1 | tf_op jit(solution)/shard_map/attend_back/pallas_call | solution.py:94
  236.5 5.1 %qkv_grad.3.ahead_ref.behind_ref.own_ref = bf16[1024,2048]{1,0:T(8,128)(2,1)S(1)} custom-call(s32[24]{0:T(128)S(1)} %copy-done.40, bf16[1056,1024]{1,0:T(8,128)(2,1)S(1)} %copy-done.14, bf16[1056,768]{1,0:T(8,128)(2,1)S(1)} %get-tuple-element.284.grad_ref.refs_0_, bf16[528,1024]{1,0:T(8,128)(2,1)S(1)} %get-tuple-element.264.own_ref, ...), custom_call_target="tpu_custom_call", output_to_operand_aliasing={{}: (7, {})} | custom-call | flops 1 | bytes 1 | tf_op jit(solution)/shard_map/qkv_grad/pallas_call | solution.py:94
  244.2 9.8 %collective-permute-done.43.got_ahead = bf16[64,2048]{1,0:T(8,128)(2,1)S(1)} collective-permute-done((bf16[64,2048]{1,0:T(8,128)(2,1)S(1)}, bf16[64,2048]{1,0:T(8,128)(2,1)S(1)}, u32[]{:S(2)}, u32[]{:S(2)}) %collective-permute-start.43) | collective-permute-done | bytes 262176 | tf_op jit(solution)/shard_map/ppermute | solution.py:131
  255.1 2.2 add_convert_fusion.refs_0_.refs_3_
  261.0 12.0 %first_norm.1 = (bf16[528,1024]{1,0:T(8,128)(2,1)}, f32[8,1024]{1,0:T(8,128)}) custom-call(s32[24]{0:T(128)} %copy-done.39, bf16[1056,768]{1,0:T(8,128)(2,1)} %copy-done.21, bf16[1056,768]{1,0:T(8,128)(2,1)} %copy-done.20, bf16[1056,768]{1,0:T(8,128)(2,1)} %copy-done.61, bf16[1056,768]{1,0:T(8,128)(2,1)} %copy-done.60, bf16[2112,1024]{1,0:T(8,128)(2,1)} %copy-done.8, ...), custom_call_target="tpu_custom_call" | custom-call | flops 1 | bytes 1 | tf_op jit(solution)/shard_map/first_norm/pallas_call | solution.py:94
  273.1 2.7 ring_add.10
  281.8 6.6 %assemble.2 = bf16[2070,1024]{1,0:T(8,128)(2,1)} custom-call(s32[24]{0:T(128)} %copy-done.39, bf16[1056,1024]{1,0:T(8,128)(2,1)} %add_convert_fusion.refs_0_.refs_3_, bf16[1056,1024]{1,0:T(8,128)(2,1)} %collective-permute-done.50.refs_1_.refs_2_, bf16[1056,1024]{1,0:T(8,128)(2,1)} %collective-permute-done.50.refs_1_.refs_2_, ...), custom_call_target="tpu_custom_call" | custom-call | flops 1 | bytes 1 | tf_op jit(solution)/shard_map/assemble/pallas_call | solution.py:94
  288.4 3.2 collective-permute-done.51.got_ahead
  292.3 2.5 ring_add.11
  295.2 1.8 collective-permute-start.55
  297.0 5.4 %collective-permute-done.57.refs_3_ = bf16[528,1024]{1,0:T(8,128)(2,1)} collective-permute-done((bf16[528,1024]{1,0:T(8,128)(2,1)}, bf16[528,1024]{1,0:T(8,128)(2,1)}, u32[]{:S(2)}, u32[]{:S(2)}) %collective-permute-start.57) | collective-permute-done | bytes 1081376 | tf_op jit(solution)/shard_map/ppermute | solution.py:227
  302.9 1.6 collective-permute-start.60
  304.6 4.9 %collective-permute-done.54.got_ahead = bf16[128,2048]{1,0:T(8,128)(2,1)S(1)} collective-permute-done((bf16[128,2048]{1,0:T(8,128)(2,1)}, bf16[128,2048]{1,0:T(8,128)(2,1)S(1)}, u32[]{:S(2)}, u32[]{:S(2)}) %collective-permute-start.54) | collective-permute-done | bytes 524320 | tf_op jit(solution)/shard_map/ppermute | solution.py:131
  309.5 2.2 copy-done.4
  314.7 7.0 %assemble.3 = f32[2070,1024]{1,0:T(8,128)} custom-call(s32[24]{0:T(128)} %copy-done.39, bf16[528,1024]{1,0:T(8,128)(2,1)} %get-tuple-element.327.refs_0_, bf16[528,1024]{1,0:T(8,128)(2,1)} %collective-permute-done.56.refs_1_, bf16[528,1024]{1,0:T(8,128)(2,1)} %collective-permute-done.58.refs_2_, bf16[528,1024]{1,0:T(8,128)(2,1)} %collective-permute-done.57.refs_3_), custom_call_target="tpu_custom_call" | custom-call | flops 1 | bytes 1 | tf_op jit(solution)/shard_map/assemble/pallas_call | solution.py:94
  321.7 2.2 collective-permute-start.62
  (329 shorter events, 93.2 us)
Async XLA Ops:
  3.9 9.4 %collective-permute-start.1 = (bf16[128,1024]{1,0:T(8,128)(2,1)S(1)}, bf16[128,1024]{1,0:T(8,128)(2,1)S(1)}, u32[]{:S(2)}, u32[]{:S(2)}) collective-permute-start(bf16[128,1024]{1,0:T(8,128)(2,1)S(1)} %pad_maximum_fusion.6.rest_0_), channel_id=1, source_target_pairs={{4,12},{12,20},{20,28},{28,24},{24,16},{16,8},{8,0},{0,4},{5,13},{... | collective-permute-start | bytes 786440 | tf_op jit(solution)/shard_map/ppermute | solution.py:131
  7.7 9.3 %collective-permute-start = (bf16[144,1024]{1,0:T(8,128)(2,1)S(1)}, bf16[144,1024]{1,0:T(8,128)(2,1)}, u32[]{:S(2)}, u32[]{:S(2)}) collective-permute-start(bf16[144,1024]{1,0:T(8,128)(2,1)S(1)} %pad_maximum_fusion.5), channel_id=1, source_target_pairs={{0,2},{1,3},{2,0},{3,1},{4,6},{5,7},{6,4},{7,5},{8,10},{9,11},{10,... | collective-permute-start | bytes 884744 | tf_op jit(solution)/shard_map/ppermute | solution.py:227
  15.5 13.0 %collective-permute-start.5 = (bf16[256,1024]{1,0:T(8,128)(2,1)}, bf16[256,1024]{1,0:T(8,128)(2,1)}, u32[]{:S(2)}, u32[]{:S(2)}) collective-permute-start(bf16[256,1024]{1,0:T(8,128)(2,1)} %pad_maximum_fusion.1), channel_id=1, source_target_pairs={{0,2},{1,3},{2,0},{3,1},{4,6},{5,7},{6,4},{7,5},{8,10},{9,11},{10,... | collective-permute-start | bytes 1572872 | tf_op jit(solution)/shard_map/ppermute | solution.py:227
  17.0 11.5 %collective-permute-start.3 = (bf16[128,1024]{1,0:T(8,128)(2,1)S(1)}, bf16[128,1024]{1,0:T(8,128)(2,1)S(1)}, u32[]{:S(2)}, u32[]{:S(2)}) collective-permute-start(bf16[128,1024]{1,0:T(8,128)(2,1)S(1)} %collective-permute-done.1.rest_1_), channel_id=1, source_target_pairs={{4,12},{12,20},{20,28},{28,24},{24,16},{16,8},{8,0},{0,4},{5,13},{... | collective-permute-start | bytes 786440 | tf_op jit(solution)/shard_map/ppermute | solution.py:131
  18.6 9.9 %collective-permute-start.4 = (bf16[128,1024]{1,0:T(8,128)(2,1)S(1)}, bf16[128,1024]{1,0:T(8,128)(2,1)S(1)}, u32[]{:S(2)}, u32[]{:S(2)}) collective-permute-start(bf16[128,1024]{1,0:T(8,128)(2,1)S(1)} %collective-permute-done.2.rest_2_), channel_id=1, source_target_pairs={{4,0},{12,4},{20,12},{28,20},{24,28},{16,24},{8,16},{0,8},{5,1},{1... | collective-permute-start | bytes 786440 | tf_op jit(solution)/shard_map/ppermute | solution.py:134
  31.5 13.6 %collective-permute-start.10 = (bf16[256,1024]{1,0:T(8,128)(2,1)}, bf16[256,1024]{1,0:T(8,128)(2,1)}, u32[]{:S(2)}, u32[]{:S(2)}) collective-permute-start(bf16[256,1024]{1,0:T(8,128)(2,1)} %pad_maximum_fusion.2), channel_id=1, source_target_pairs={{0,2},{1,3},{2,0},{3,1},{4,6},{5,7},{6,4},{7,5},{8,10},{9,11},{10,... | collective-permute-start | bytes 1572872 | tf_op jit(solution)/shard_map/ppermute | solution.py:227
  41.5 18.3 %collective-permute-start.11 = (bf16[256,1024]{1,0:T(8,128)(2,1)}, bf16[256,1024]{1,0:T(8,128)(2,1)}, u32[]{:S(2)}, u32[]{:S(2)}) collective-permute-start(bf16[256,1024]{1,0:T(8,128)(2,1)} %pad_maximum_fusion.3), channel_id=1, source_target_pairs={{0,2},{1,3},{2,0},{3,1},{4,6},{5,7},{6,4},{7,5},{8,10},{9,11},{10,... | collective-permute-start | bytes 1572872 | tf_op jit(solution)/shard_map/ppermute | solution.py:227
  45.0 14.8 %collective-permute-start.13 = (bf16[128,2048]{1,0:T(8,128)(2,1)}, bf16[128,2048]{1,0:T(8,128)(2,1)}, u32[]{:S(2)}, u32[]{:S(2)}) collective-permute-start(bf16[128,2048]{1,0:T(8,128)(2,1)} %pad_maximum_fusion.4.rest_0_), channel_id=1, source_target_pairs={{4,12},{12,20},{20,28},{28,24},{24,16},{16,8},{8,0},{0,4},{5,13},{... | collective-permute-start | bytes 1572872 | tf_op jit(solution)/shard_map/ppermute | solution.py:131
  46.6 13.2 %collective-permute-start.14 = (bf16[128,2048]{1,0:T(8,128)(2,1)}, bf16[128,2048]{1,0:T(8,128)(2,1)}, u32[]{:S(2)}, u32[]{:S(2)}) collective-permute-start(bf16[128,2048]{1,0:T(8,128)(2,1)} %pad_maximum_fusion.4.rest_0_), channel_id=1, source_target_pairs={{4,0},{12,4},{20,12},{28,20},{24,28},{16,24},{8,16},{0,8},{5,1},{1... | collective-permute-start | bytes 1572872 | tf_op jit(solution)/shard_map/ppermute | solution.py:134
  48.4 11.4 %collective-permute-start.12 = (bf16[128,1024]{1,0:T(8,128)(2,1)}, bf16[128,1024]{1,0:T(8,128)(2,1)}, u32[]{:S(2)}, u32[]{:S(2)}) collective-permute-start(bf16[128,1024]{1,0:T(8,128)(2,1)} %pad_maximum_fusion.7), channel_id=1, source_target_pairs={{0,2},{1,3},{2,0},{3,1},{4,6},{5,7},{6,4},{7,5},{8,10},{9,11},{10,... | collective-permute-start | bytes 786440 | tf_op jit(solution)/shard_map/ppermute | solution.py:227
  59.8 11.7 %collective-permute-start.15 = (bf16[128,2048]{1,0:T(8,128)(2,1)}, bf16[128,2048]{1,0:T(8,128)(2,1)S(1)}, u32[]{:S(2)}, u32[]{:S(2)}) collective-permute-start(bf16[128,2048]{1,0:T(8,128)(2,1)} %collective-permute-done.13.rest_1_), channel_id=1, source_target_pairs={{4,12},{12,20},{20,28},{28,24},{24,16},{16,8},{8,0},{0,4},{5,13},{... | collective-permute-start | bytes 1572872 | tf_op jit(solution)/shard_map/ppermute | solution.py:131
  61.4 11.4 %collective-permute-start.16 = (bf16[128,2048]{1,0:T(8,128)(2,1)}, bf16[128,2048]{1,0:T(8,128)(2,1)S(1)}, u32[]{:S(2)}, u32[]{:S(2)}) collective-permute-start(bf16[128,2048]{1,0:T(8,128)(2,1)} %collective-permute-done.14.rest_2_), channel_id=1, source_target_pairs={{4,0},{12,4},{20,12},{28,20},{24,28},{16,24},{8,16},{0,8},{5,1},{1... | collective-permute-start | bytes 1572872 | tf_op jit(solution)/shard_map/ppermute | solution.py:134
  72.8 16.2 %collective-permute-start.19 = (bf16[1024,2048]{1,0:T(8,128)(2,1)S(1)}, bf16[1024,2048]{1,0:T(8,128)(2,1)S(1)}, u32[]{:S(2)}, u32[]{:S(2)}) collective-permute-start(bf16[1024,2048]{1,0:T(8,128)(2,1)S(1)} %get-tuple-element.220.rest_0_.rest_3_.refs_13_), channel_id=1, source_target_pairs={{0,1},{1,0},{2,3},{3,2},{4,5},{5,4},{6,7},{7,6},{8,9},{9,8},{10,11... | collective-permute-start | bytes 12582920 | tf_op jit(solution)/shard_map/ppermute | solution.py:231
  72.9 16.1 %collective-permute-start.17 = (bf16[128,2048]{1,0:T(8,128)(2,1)S(1)}, bf16[128,2048]{1,0:T(8,128)(2,1)S(1)}, u32[]{:S(2)}, u32[]{:S(2)}) collective-permute-start(bf16[128,2048]{1,0:T(8,128)(2,1)S(1)} %collective-permute-done.15.rest_3_), channel_id=1, source_target_pairs={{4,12},{12,20},{20,28},{28,24},{24,16},{16,8},{8,0},{0,4},{5,13},{... | collective-permute-start | bytes 1572872 | tf_op jit(solution)/shard_map/ppermute | solution.py:131
  74.6 14.5 %collective-permute-start.18 = (bf16[128,2048]{1,0:T(8,128)(2,1)S(1)}, bf16[128,2048]{1,0:T(8,128)(2,1)S(1)}, u32[]{:S(2)}, u32[]{:S(2)}) collective-permute-start(bf16[128,2048]{1,0:T(8,128)(2,1)S(1)} %collective-permute-done.16.rest_4_), channel_id=1, source_target_pairs={{4,0},{12,4},{20,12},{28,20},{24,28},{16,24},{8,16},{0,8},{5,1},{1... | collective-permute-start | bytes 1572872 | tf_op jit(solution)/shard_map/ppermute | solution.py:134
  99.3 26.3 %collective-permute-start.24 = (bf16[528,1024]{1,0:T(8,128)(2,1)S(1)}, bf16[528,1024]{1,0:T(8,128)(2,1)S(1)}, u32[]{:S(2)}, u32[]{:S(2)}) collective-permute-start(bf16[528,1024]{1,0:T(8,128)(2,1)S(1)} %get-tuple-element.227.rest_9_.rest_0_), channel_id=1, source_target_pairs={{0,2},{1,3},{2,0},{3,1},{4,6},{5,7},{6,4},{7,5},{8,10},{9,11},{10,... | collective-permute-start | bytes 3244040 | tf_op jit(solution)/shard_map/ppermute | solution.py:227
  140.4 37.9 %collective-permute-start.27 = (bf16[528,1024]{1,0:T(8,128)(2,1)}, bf16[528,1024]{1,0:T(8,128)(2,1)}, u32[]{:S(2)}, u32[]{:S(2)}) collective-permute-start(bf16[528,1024]{1,0:T(8,128)(2,1)} %get-tuple-element.243), channel_id=1, source_target_pairs={{0,1},{1,0},{2,3},{3,2},{4,5},{5,4},{6,7},{7,6},{8,9},{9,8},{10,11... | collective-permute-start | bytes 3244040 | tf_op jit(solution)/shard_map/ppermute | solution.py:231
  155.5 26.3 %collective-permute-start.28 = (bf16[528,1024]{1,0:T(8,128)(2,1)}, bf16[528,1024]{1,0:T(8,128)(2,1)}, u32[]{:S(2)}, u32[]{:S(2)}) collective-permute-start(bf16[528,1024]{1,0:T(8,128)(2,1)} %get-tuple-element.244), channel_id=1, source_target_pairs={{0,2},{1,3},{2,0},{3,1},{4,6},{5,7},{6,4},{7,5},{8,10},{9,11},{10,... | collective-permute-start | bytes 3244040 | tf_op jit(solution)/shard_map/ppermute | solution.py:227
  156.9 36.2 %collective-permute-start.37 = (bf16[528,1024]{1,0:T(8,128)(2,1)}, bf16[528,1024]{1,0:T(8,128)(2,1)}, u32[]{:S(2)}, u32[]{:S(2)}) collective-permute-start(bf16[528,1024]{1,0:T(8,128)(2,1)} %get-tuple-element.276), channel_id=1, source_target_pairs={{0,1},{1,0},{2,3},{3,2},{4,5},{5,4},{6,7},{7,6},{8,9},{9,8},{10,11... | collective-permute-start | bytes 3244040 | tf_op jit(solution)/shard_map/ppermute | solution.py:231
  176.2 14.8 %collective-permute-start.29 = (bf16[64,2048]{1,0:T(8,128)(2,1)S(1)}, bf16[64,2048]{1,0:T(8,128)(2,1)S(1)}, u32[]{:S(2)}, u32[]{:S(2)}) collective-permute-start(bf16[64,2048]{1,0:T(8,128)(2,1)S(1)} %get-tuple-element.247), channel_id=1, source_target_pairs={{4,12},{12,20},{20,28},{28,24},{24,16},{16,8},{8,0},{0,4},{5,13},{... | collective-permute-start | bytes 786440 | tf_op jit(solution)/shard_map/ppermute | solution.py:131
  177.8 13.2 %collective-permute-start.30 = (bf16[64,2048]{1,0:T(8,128)(2,1)S(1)}, bf16[64,2048]{1,0:T(8,128)(2,1)S(1)}, u32[]{:S(2)}, u32[]{:S(2)}) collective-permute-start(bf16[64,2048]{1,0:T(8,128)(2,1)S(1)} %get-tuple-element.249), channel_id=1, source_target_pairs={{4,0},{12,4},{20,12},{28,20},{24,28},{16,24},{8,16},{0,8},{5,1},{1... | collective-permute-start | bytes 786440 | tf_op jit(solution)/shard_map/ppermute | solution.py:134
  191.0 20.5 %collective-permute-start.34 = (bf16[528,1024]{1,0:T(8,128)(2,1)S(1)}, bf16[528,1024]{1,0:T(8,128)(2,1)S(1)}, u32[]{:S(2)}, u32[]{:S(2)}) collective-permute-start(bf16[528,1024]{1,0:T(8,128)(2,1)S(1)} %get-tuple-element.264.own_ref), channel_id=1, source_target_pairs={{0,1},{1,0},{2,3},{3,2},{4,5},{5,4},{6,7},{7,6},{8,9},{9,8},{10,11... | collective-permute-start | bytes 3244040 | tf_op jit(solution)/shard_map/ppermute | solution.py:231
  193.0 18.5 %collective-permute-start.40 = (bf16[528,1024]{1,0:T(8,128)(2,1)S(1)}, bf16[528,1024]{1,0:T(8,128)(2,1)S(1)}, u32[]{:S(2)}, u32[]{:S(2)}) collective-permute-start(bf16[528,1024]{1,0:T(8,128)(2,1)S(1)} %copy-done.70), channel_id=1, source_target_pairs={{0,1},{1,0},{2,3},{3,2},{4,5},{5,4},{6,7},{7,6},{8,9},{9,8},{10,11... | collective-permute-start | bytes 3244040 | tf_op jit(solution)/shard_map/ppermute | solution.py:231
  195.2 16.3 %collective-permute-start.38 = (bf16[264,1024]{1,0:T(8,128)(2,1)S(1)}, bf16[264,1024]{1,0:T(8,128)(2,1)S(1)}, u32[]{:S(2)}, u32[]{:S(2)}) collective-permute-start(bf16[264,1024]{1,0:T(8,128)(2,1)S(1)} %slice.179), channel_id=1, source_target_pairs={{0,2},{1,3},{2,0},{3,1},{4,6},{5,7},{6,4},{7,5},{8,10},{9,11},{10,... | collective-permute-start | bytes 1622024 | tf_op jit(solution)/shard_map/ppermute | solution.py:227
  196.5 13.7 %collective-permute-start.32 = (bf16[128,2048]{1,0:T(8,128)(2,1)S(1)}, bf16[128,2048]{1,0:T(8,128)(2,1)S(1)}, u32[]{:S(2)}, u32[]{:S(2)}) collective-permute-start(bf16[128,2048]{1,0:T(8,128)(2,1)S(1)} %get-tuple-element.258), channel_id=1, source_target_pairs={{4,12},{12,20},{20,28},{28,24},{24,16},{16,8},{8,0},{0,4},{5,13},{... | collective-permute-start | bytes 1572872 | tf_op jit(solution)/shard_map/ppermute | solution.py:131
  198.1 13.5 %collective-permute-start.33 = (bf16[128,2048]{1,0:T(8,128)(2,1)S(1)}, bf16[128,2048]{1,0:T(8,128)(2,1)S(1)}, u32[]{:S(2)}, u32[]{:S(2)}) collective-permute-start(bf16[128,2048]{1,0:T(8,128)(2,1)S(1)} %get-tuple-element.260), channel_id=1, source_target_pairs={{4,0},{12,4},{20,12},{28,20},{24,28},{16,24},{8,16},{0,8},{5,1},{1... | collective-permute-start | bytes 1572872 | tf_op jit(solution)/shard_map/ppermute | solution.py:134
  211.5 21.1 %collective-permute-start.39 = (bf16[1056,768]{1,0:T(8,128)(2,1)S(1)}, bf16[1056,768]{1,0:T(8,128)(2,1)S(1)}, u32[]{:S(2)}, u32[]{:S(2)}) collective-permute-start(bf16[1056,768]{1,0:T(8,128)(2,1)S(1)} %get-tuple-element.278.grad_ref.refs_1_), channel_id=1, source_target_pairs={{0,1},{1,0},{2,3},{3,2},{4,5},{5,4},{6,7},{7,6},{8,9},{9,8},{10,11... | collective-permute-start | bytes 4866056 | tf_op jit(solution)/shard_map/ppermute | solution.py:231
  212.3 20.3 %collective-permute-start.41 = (bf16[392,1024]{1,0:T(8,128)(2,1)S(1)}, bf16[392,1024]{1,0:T(8,128)(2,1)S(1)}, u32[]{:S(2)}, u32[]{:S(2)}) collective-permute-start(bf16[392,1024]{1,0:T(8,128)(2,1)S(1)} %pad_maximum_fusion), channel_id=1, source_target_pairs={{0,2},{1,3},{2,0},{3,1},{4,6},{5,7},{6,4},{7,5},{8,10},{9,11},{10,... | collective-permute-start | bytes 2408456 | tf_op jit(solution)/shard_map/ppermute | solution.py:227
  213.9 17.0 %collective-permute-start.35 = (bf16[128,2048]{1,0:T(8,128)(2,1)S(1)}, bf16[128,2048]{1,0:T(8,128)(2,1)S(1)}, u32[]{:S(2)}, u32[]{:S(2)}) collective-permute-start(bf16[128,2048]{1,0:T(8,128)(2,1)S(1)} %get-tuple-element.268), channel_id=1, source_target_pairs={{4,12},{12,20},{20,28},{28,24},{24,16},{16,8},{8,0},{0,4},{5,13},{... | collective-permute-start | bytes 1572872 | tf_op jit(solution)/shard_map/ppermute | solution.py:131
  214.5 16.5 %collective-permute-start.36 = (bf16[128,2048]{1,0:T(8,128)(2,1)S(1)}, bf16[128,2048]{1,0:T(8,128)(2,1)S(1)}, u32[]{:S(2)}, u32[]{:S(2)}) collective-permute-start(bf16[128,2048]{1,0:T(8,128)(2,1)S(1)} %get-tuple-element.270), channel_id=1, source_target_pairs={{4,0},{12,4},{20,12},{28,20},{24,28},{16,24},{8,16},{0,8},{5,1},{1... | collective-permute-start | bytes 1572872 | tf_op jit(solution)/shard_map/ppermute | solution.py:134
  232.6 9.5 %collective-permute-start.42 = (bf16[1056,768]{1,0:T(8,128)(2,1)S(1)}, bf16[1056,768]{1,0:T(8,128)(2,1)S(1)}, u32[]{:S(2)}, u32[]{:S(2)}) collective-permute-start(bf16[1056,768]{1,0:T(8,128)(2,1)S(1)} %get-tuple-element.284.grad_ref.refs_0_), channel_id=1, source_target_pairs={{0,1},{1,0},{2,3},{3,2},{4,5},{5,4},{6,7},{7,6},{8,9},{9,8},{10,11... | collective-permute-start | bytes 4866056 | tf_op jit(solution)/shard_map/ppermute | solution.py:231
  232.7 22.4 %collective-permute-start.47 = (bf16[400,1024]{1,0:T(8,128)(2,1)S(1)}, bf16[400,1024]{1,0:T(8,128)(2,1)S(1)}, u32[]{:S(2)}, u32[]{:S(2)}) collective-permute-start(bf16[400,1024]{1,0:T(8,128)(2,1)S(1)} %slice.180), channel_id=1, source_target_pairs={{0,2},{1,3},{2,0},{3,1},{4,6},{5,7},{6,4},{7,5},{8,10},{9,11},{10,... | collective-permute-start | bytes 2457608 | tf_op jit(solution)/shard_map/ppermute | solution.py:227
  234.4 20.0 %collective-permute-start.45 = (bf16[128,2048]{1,0:T(8,128)(2,1)S(1)}, bf16[128,2048]{1,0:T(8,128)(2,1)S(1)}, u32[]{:S(2)}, u32[]{:S(2)}) collective-permute-start(bf16[128,2048]{1,0:T(8,128)(2,1)S(1)} %get-tuple-element.289), channel_id=1, source_target_pairs={{4,12},{12,20},{20,28},{28,24},{24,16},{16,8},{8,0},{0,4},{5,13},{... | collective-permute-start | bytes 1572872 | tf_op jit(solution)/shard_map/ppermute | solution.py:131
  234.9 19.4 %collective-permute-start.46 = (bf16[128,2048]{1,0:T(8,128)(2,1)S(1)}, bf16[128,2048]{1,0:T(8,128)(2,1)S(1)}, u32[]{:S(2)}, u32[]{:S(2)}) collective-permute-start(bf16[128,2048]{1,0:T(8,128)(2,1)S(1)} %get-tuple-element.291), channel_id=1, source_target_pairs={{4,0},{12,4},{20,12},{28,20},{24,28},{16,24},{8,16},{0,8},{5,1},{1... | collective-permute-start | bytes 1572872 | tf_op jit(solution)/shard_map/ppermute | solution.py:134
  242.2 11.9 %collective-permute-start.43 = (bf16[64,2048]{1,0:T(8,128)(2,1)S(1)}, bf16[64,2048]{1,0:T(8,128)(2,1)S(1)}, u32[]{:S(2)}, u32[]{:S(2)}) collective-permute-start(bf16[64,2048]{1,0:T(8,128)(2,1)S(1)} %get-tuple-element.285), channel_id=1, source_target_pairs={{4,12},{12,20},{20,28},{28,24},{24,16},{16,8},{8,0},{0,4},{5,13},{... | collective-permute-start | bytes 786440 | tf_op jit(solution)/shard_map/ppermute | solution.py:131
  242.7 11.6 %collective-permute-start.44 = (bf16[64,2048]{1,0:T(8,128)(2,1)S(1)}, bf16[64,2048]{1,0:T(8,128)(2,1)S(1)}, u32[]{:S(2)}, u32[]{:S(2)}) collective-permute-start(bf16[64,2048]{1,0:T(8,128)(2,1)S(1)} %get-tuple-element.287), channel_id=1, source_target_pairs={{4,0},{12,4},{20,12},{28,20},{24,28},{16,24},{8,16},{0,8},{5,1},{1... | collective-permute-start | bytes 786440 | tf_op jit(solution)/shard_map/ppermute | solution.py:134
  259.0 14.1 %collective-permute-start.48 = (bf16[128,2048]{1,0:T(8,128)(2,1)}, bf16[128,2048]{1,0:T(8,128)(2,1)S(1)}, u32[]{:S(2)}, u32[]{:S(2)}) collective-permute-start(bf16[128,2048]{1,0:T(8,128)(2,1)} %get-tuple-element.307), channel_id=1, source_target_pairs={{4,12},{12,20},{20,28},{28,24},{24,16},{16,8},{8,0},{0,4},{5,13},{... | collective-permute-start | bytes 1572872 | tf_op jit(solution)/shard_map/ppermute | solution.py:131
  259.5 13.5 %collective-permute-start.49 = (bf16[128,2048]{1,0:T(8,128)(2,1)}, bf16[128,2048]{1,0:T(8,128)(2,1)}, u32[]{:S(2)}, u32[]{:S(2)}) collective-permute-start(bf16[128,2048]{1,0:T(8,128)(2,1)} %get-tuple-element.309), channel_id=1, source_target_pairs={{4,0},{12,4},{20,12},{28,20},{24,28},{16,24},{8,16},{0,8},{5,1},{1... | collective-permute-start | bytes 1572872 | tf_op jit(solution)/shard_map/ppermute | solution.py:134
  275.8 26.6 %collective-permute-start.57 = (bf16[528,1024]{1,0:T(8,128)(2,1)}, bf16[528,1024]{1,0:T(8,128)(2,1)}, u32[]{:S(2)}, u32[]{:S(2)}) collective-permute-start(bf16[528,1024]{1,0:T(8,128)(2,1)} %get-tuple-element.327.refs_0_), channel_id=1, source_target_pairs={{0,2},{1,3},{2,0},{3,1},{4,6},{5,7},{6,4},{7,5},{8,10},{9,11},{10,... | collective-permute-start | bytes 3244040 | tf_op jit(solution)/shard_map/ppermute | solution.py:227
  277.4 14.3 %collective-permute-start.51 = (bf16[128,2048]{1,0:T(8,128)(2,1)}, bf16[128,2048]{1,0:T(8,128)(2,1)S(1)}, u32[]{:S(2)}, u32[]{:S(2)}) collective-permute-start(bf16[128,2048]{1,0:T(8,128)(2,1)} %get-tuple-element.314), channel_id=1, source_target_pairs={{4,12},{12,20},{20,28},{28,24},{24,16},{16,8},{8,0},{0,4},{5,13},{... | collective-permute-start | bytes 1572872 | tf_op jit(solution)/shard_map/ppermute | solution.py:131
  277.9 14.4 %collective-permute-start.52 = (bf16[128,2048]{1,0:T(8,128)(2,1)}, bf16[128,2048]{1,0:T(8,128)(2,1)}, u32[]{:S(2)}, u32[]{:S(2)}) collective-permute-start(bf16[128,2048]{1,0:T(8,128)(2,1)} %get-tuple-element.316), channel_id=1, source_target_pairs={{4,0},{12,4},{20,12},{28,20},{24,28},{16,24},{8,16},{0,8},{5,1},{1... | collective-permute-start | bytes 1572872 | tf_op jit(solution)/shard_map/ppermute | solution.py:134
  279.4 15.4 %collective-permute-start.53 = (f32[8,1024]{1,0:T(8,128)S(1)}, f32[8,1024]{1,0:T(8,128)S(1)}, u32[]{:S(2)}, u32[]{:S(2)}) collective-permute-start(f32[8,1024]{1,0:T(8,128)S(1)} %copy-done.65), channel_id=1, source_target_pairs={{0,4},{4,0},{8,12},{12,8},{16,20},{20,16},{24,28},{28,24},{1,5},{5... | collective-permute-start | bytes 98312 | tf_op jit(solution)/shard_map/ppermute | solution.py:1184
  294.9 14.5 %collective-permute-start.54 = (bf16[128,2048]{1,0:T(8,128)(2,1)}, bf16[128,2048]{1,0:T(8,128)(2,1)S(1)}, u32[]{:S(2)}, u32[]{:S(2)}) collective-permute-start(bf16[128,2048]{1,0:T(8,128)(2,1)} %get-tuple-element.322), channel_id=1, source_target_pairs={{4,12},{12,20},{20,28},{28,24},{24,16},{16,8},{8,0},{0,4},{5,13},{... | collective-permute-start | bytes 1572872 | tf_op jit(solution)/shard_map/ppermute | solution.py:131
  295.2 14.3 %collective-permute-start.55 = (bf16[128,2048]{1,0:T(8,128)(2,1)S(1)}, bf16[128,2048]{1,0:T(8,128)(2,1)S(1)}, u32[]{:S(2)}, u32[]{:S(2)}) collective-permute-start(bf16[128,2048]{1,0:T(8,128)(2,1)S(1)} %get-tuple-element.324), channel_id=1, source_target_pairs={{4,0},{12,4},{20,12},{28,20},{24,28},{16,24},{8,16},{0,8},{5,1},{1... | collective-permute-start | bytes 1572872 | tf_op jit(solution)/shard_map/ppermute | solution.py:134
  302.4 12.3 %collective-permute-start.56 = (bf16[528,1024]{1,0:T(8,128)(2,1)}, bf16[528,1024]{1,0:T(8,128)(2,1)}, u32[]{:S(2)}, u32[]{:S(2)}) collective-permute-start(bf16[528,1024]{1,0:T(8,128)(2,1)} %get-tuple-element.327.refs_0_), channel_id=1, source_target_pairs={{0,1},{1,0},{2,3},{3,2},{4,5},{5,4},{6,7},{7,6},{8,9},{9,8},{10,11... | collective-permute-start | bytes 3244040 | tf_op jit(solution)/shard_map/ppermute | solution.py:231
  302.4 12.3 %collective-permute-start.58 = (bf16[528,1024]{1,0:T(8,128)(2,1)}, bf16[528,1024]{1,0:T(8,128)(2,1)}, u32[]{:S(2)}, u32[]{:S(2)}) collective-permute-start(bf16[528,1024]{1,0:T(8,128)(2,1)} %collective-permute-done.57.refs_3_), channel_id=1, source_target_pairs={{0,1},{1,0},{2,3},{3,2},{4,5},{5,4},{6,7},{7,6},{8,9},{9,8},{10,11... | collective-permute-start | bytes 3244040 | tf_op jit(solution)/shard_map/ppermute | solution.py:231
  302.9 10.1 %collective-permute-start.60 = (f32[6656]{0:T(1024)S(1)}, f32[6656]{0:T(1024)S(1)}, u32[]{:S(2)}, u32[]{:S(2)}) collective-permute-start(f32[6656]{0:T(1024)S(1)} %pad_maximum_fusion.9), channel_id=1, source_target_pairs={{0,2},{1,3},{2,0},{3,1},{4,6},{5,7},{6,4},{7,5},{8,10},{9,11},{10,... | collective-permute-start | bytes 79880 | tf_op jit(solution)/shard_map/ppermute | solution.py:227
  312.5 9.2 %collective-permute-start.63 = (bf16[128,1024]{1,0:T(8,128)(2,1)S(1)}, bf16[128,1024]{1,0:T(8,128)(2,1)S(1)}, u32[]{:S(2)}, u32[]{:S(2)}) collective-permute-start(bf16[128,1024]{1,0:T(8,128)(2,1)S(1)} %slice.163), channel_id=1, source_target_pairs={{0,2},{1,3},{2,0},{3,1},{4,6},{5,7},{6,4},{7,5},{8,10},{9,11},{10,... | collective-permute-start | bytes 786440 | tf_op jit(solution)/shard_map/ppermute | solution.py:227
  (91 other events, 882.5 us)

commit v3 on v2

--- a/solution.py
+++ b/solution.py
@@ -44,10 +44,10 @@
     "attend_back": 12,
     "proj_norm": 20,
     "mlp": 58,
-    "mlp_grad": 58,
+    "mlp_grad": 54,
     "residual_back": 16,
     "qkv_grad": 20,
-    "first_norm": 58,
+    "first_norm": 54,
 }
 
 
@@ -983,6 +983,12 @@
     mlp_ring = ring.scatter_steps(mlp_grad, ranks, order)
     mlp_due = next(mlp_ring)
 
+    if chips == 2:
+        out_far = own[3][0].astype(f32)
+        out_far = (out_far + partner(other[3][0], chips).astype(f32)).astype(bf16)
+        out_near = order.after(residual) + shrink_bias + first[3][0].astype(f32)
+        out_near = (out_near + partner(first[3][1], chips).astype(f32)).astype(bf16)
+        order.hold = out_far, out_near
     step_rows = row_step(half)
     cot_rows = pl.BlockSpec(
         (step_rows, dim), lambda i, info: (info[place_base] * (half // step_rows) + i, 0)
@@ -1014,10 +1020,6 @@
     order.due = ()
     mlp_due = next(mlp_ring)
     if chips == 2:
-        out_near = order.after(residual) + shrink_bias + first[3][0].astype(f32)
-        out_near = (out_near + partner(order.after(first[3][1]), chips).astype(f32)).astype(bf16)
-        out_far = own[3][0].astype(f32)
-        out_far = (out_far + partner(other[3][0], chips).astype(f32)).astype(bf16)
         out_rows = jnp.concatenate([out_far, out_near])
         cuts = [0, half // 16 * 8, half * 5 // 32 * 8, 2 * half]
         out_sends = iter([out_rows[i:j] for i, j in zip(cuts, cuts[1:])])

time: 329 us -> 323 us (0.982)
  Pallas kernels: 162 us -> 158 us
  local copies, waits for them, and re-layouts: 35.7 us -> 39.5 us
    pallas_call x28, Pallas kernels: 162 us -> 158 us  [run(): out = kernel(tie(self.info, self.now, wait, self.hold), *values)]
    unnamed x155 -> x161, local copies, waits for them, and re-layouts: 29.1 us -> 32.9 us
  transfers between devices with their start and end apart: 64 -> 64, of which waited for: 25 -> 25; matrix products, arithmetic and copies ran while one was open for 6% -> 5% of each run, Pallas kernels for 45% -> 45%
where the time goes in v3:
time: 323 us; the launch traced here: 322 us
  Pallas kernels  158 us (49%)
  waiting for transfers between devices  56.5 us (17%)
  starting transfers between devices  54.1 us (17%)
  local copies, waits for them, and re-layouts  39.5 us (12%)
  other arithmetic  12.7 us (4%)
    pallas_call x28, Pallas kernels, run(): out = kernel(tie(self.info, self.now, wait, self.hold), *values)  158 us
    unnamed x161, local copies, waits for them, and re-layouts  32.9 us
    ppermute x16, waiting for transfers between devices, send_ahead(): return lax.ppermute(value, 'dp', self.ahead)  23.3 us
    ppermute x16, starting transfers between devices, send_ahead(): return lax.ppermute(value, 'dp', self.ahead)  22.9 us
    ppermute x13, starting transfers between devices, across(): return lax.ppermute(value, 'mp', pairs)  14.1 us
    ppermute x13, waiting for transfers between devices, across(): return lax.ppermute(value, 'mp', pairs)  14.1 us
    ppermute x16, starting transfers between devices, send_behind(): return lax.ppermute(value, 'dp', self.behind)  11.2 us
    ppermute x16, waiting for transfers between devices, send_behind(): return lax.ppermute(value, 'dp', self.behind)  8.42 us
  transfers between devices with their start and end apart: 64, of which 25 were waited for; matrix products, arithmetic and copies ran while one was open for 5% of the time, Pallas kernels for 45%

profile of v3, /device:TPU:0, one launch (start us, length us, event | category | flops | bytes accessed | tf_op | source)
XLA Modules:
  0.0 322.5 jit_solution(6244117621461538649)
XLA Ops:
  3.9 3.0 collective-permute-start.1
  7.2 1.9 collective-permute-start
  9.1 4.2 %collective-permute-done.1.rest_1_ = bf16[128,1024]{1,0:T(8,128)(2,1)S(1)} collective-permute-done((bf16[128,1024]{1,0:T(8,128)(2,1)S(1)}, bf16[128,1024]{1,0:T(8,128)(2,1)S(1)}, u32[]{:S(2)}, u32[]{:S(2)}) %collective-permute-start.1) | collective-permute-done | bytes 262176 | tf_op jit(solution)/shard_map/ppermute | solution.py:131
  18.3 2.2 copy-done.22
  20.5 3.0 pad.83.x_ref.refs_4_
  23.5 2.1 first_low.1.x_ref.first_ref
  25.7 2.1 copy-done.8
  29.2 1.6 collective-permute-start.6
  34.6 1.9 copy.90
  39.3 1.8 pad_maximum_fusion.4.rest_0_
  43.8 2.1 collective-permute-done.10.rest_11_
  49.4 1.6 collective-permute-start.12
  53.2 2.2 copy-done.23
  55.5 3.0 pad.84.cot_ref
  58.5 2.0 copy-done.7
  67.5 5.5 %qkv.1 = (bf16[1056,1536]{1,0:T(8,128)(2,1)S(1)}, bf16[1024,2048]{1,0:T(8,128)(2,1)S(1)}) custom-call(s32[24]{0:T(128)S(1)} %concatenate.49.info, bf16[1056,1024]{1,0:T(8,128)(2,1)S(1)} %copy-done.14, f32[1,1536]{1,0:T(1,128)S(1)} %pad_maximum_fusion.10.bias_ref, bf16[128,1024]{1,0:T(8,128)(2,1)S(1)} %pad_maximum_fusion.6.rest_0_, ...), custom_call_target="tpu_custom_call" | custom-call | flops 1 | bytes 1 | tf_op jit(solution)/shard_map/qkv/pallas_call | solution.py:94
  77.0 12.3 %attend.1 = (bf16[1056,512]{1,0:T(8,128)(2,1)S(1)}, f32[3,4,2,352]{3,2,1,0:T(2,128)S(1)}) custom-call(s32[24]{0:T(128)S(1)} %concatenate.49.info, bf16[1056,1536]{1,0:T(8,128)(2,1)S(1)} %get-tuple-element.206.qkv_ref, s32[3,352,1]{2,1,0:T(8,128)S(1)} %broadcast_select_fusion.key_ids, s32[3,1,352]{2,1,0:T(1,128)S(1)} %broadcast_select_fusion.1.query_ids), custom_call_target="tpu_custom_call" | custom-call | flops 1 | bytes 1 | tf_op jit(solution)/shard_map/attend/pallas_call | solution.py:94
  89.3 1.7 copy-done.16
  91.2 1.7 collective-permute-start.21
  93.9 4.3 %proj_norm.1 = (f32[528,1024]{1,0:T(8,128)S(1)}, bf16[528,1024]{1,0:T(8,128)(2,1)}) custom-call(s32[24]{0:T(128)S(1)} %concatenate.49.info, bf16[1056,512]{1,0:T(8,128)(2,1)S(1)} %get-tuple-element.220.own_ref.att_own.att_got, bf16[1056,512]{1,0:T(8,128)(2,1)S(1)} %collective-permute-done.20.got_ref, bf16[2112,1024]{1,0:T(8,128)(2,1)S(1)} %bitcast.57, ...), custom_call_target="tpu_custom_call" | custom-call | flops 1 | bytes 1 | tf_op jit(solution)/shard_map/proj_norm/pallas_call | solution.py:94
  101.3 2.9 collective-permute-done.23.rest_10_.rest_1_
  105.2 19.3 %mlp.3 = (bf16[1056,1024]{1,0:T(8,128)(2,1)}, bf16[1056,1024]{1,0:T(8,128)(2,1)}, bf16[528,1024]{1,0:T(8,128)(2,1)}, bf16[528,1024]{1,0:T(8,128)(2,1)}, bf16[528...) custom-call(s32[24]{0:T(128)} %copy-done.40, bf16[2112,1024]{1,0:T(8,128)(2,1)} %copy-done.7, ...), custom_call_target="tpu_custom_call" | custom-call | flops 1 | bytes 1 | tf_op jit(solution)/shard_map/mlp/pallas_call | solution.py:94
  124.5 3.3 %collective-permute-done.24.rest_9_.rest_3_ = bf16[528,1024]{1,0:T(8,128)(2,1)S(1)} collective-permute-done((bf16[528,1024]{1,0:T(8,128)(2,1)}, bf16[528,1024]{1,0:T(8,128)(2,1)S(1)}, u32[]{:S(2)}, u32[]{:S(2)}) %collective-permute-start.24) | collective-permute-done | bytes 1081376 | tf_op jit(solution)/shard_map/ppermute | solution.py:227
  127.8 2.7 collective-permute-done.25.rest_9_.rest_2_
  131.5 10.9 %mlp.4 = (bf16[528,1024]{1,0:T(8,128)(2,1)}, bf16[528,1024]{1,0:T(8,128)(2,1)}, bf16[528,1024]{1,0:T(8,128)(2,1)}, bf16[528,1024]{1,0:T(8,128)(2,1)}, f32[1,1024]{1,0:T(1,128)}) custom-call(s32[24]{0:T(128)} %copy-done.40, bf16[2112,1024]{1,0:T(8,128)(2,1)} %copy-done.7, f32[1,1024]{1,0:T(1,128)} %bitcast.75, bf16[128,2048]{1,0:T(8,128)(2,1)} %pad_maximum_fusion.4.rest_0_, ...), custom_call_target="tpu_custom_call" | custom-call | flops 1 | bytes 1 | tf_op jit(solution)/shard_map/mlp/pallas_call | solution.py:94
  143.5 2.1 collective-permute-done.26.rest_10_
  146.6 11.2 %mlp.5 = (bf16[528,1024]{1,0:T(8,128)(2,1)}, bf16[528,1024]{1,0:T(8,128)(2,1)}, bf16[528,1024]{1,0:T(8,128)(2,1)}, bf16[528,1024]{1,0:T(8,128)(2,1)}, f32[1,1024]{1,0:T(1,128)}) custom-call(s32[24]{0:T(128)} %copy-done.40, bf16[2112,1024]{1,0:T(8,128)(2,1)} %copy-done.7, f32[1,1024]{1,0:T(1,128)} %bitcast.76, bf16[128,2048]{1,0:T(8,128)(2,1)} %pad_maximum_fusion.4.rest_0_, ...), custom_call_target="tpu_custom_call" | custom-call | flops 1 | bytes 1 | tf_op jit(solution)/shard_map/mlp/pallas_call | solution.py:94
  158.1 16.1 %mlp_grad.1.ahead_ref.behind_ref.own_ref = bf16[1024,2048]{1,0:T(8,128)(2,1)} custom-call(s32[24]{0:T(128)} %copy-done.40, bf16[2112,1024]{1,0:T(8,128)(2,1)} %copy-done.7, bf16[528,1024]{1,0:T(8,128)(2,1)} %get-tuple-element.226.rest_9_.rest_0_, bf16[528,1024]{1,0:T(8,128)(2,1)} %copy-done.60, bf16[528,1024]{1,0:T(8,128)(2,1)} %copy-done.62, ...), custom_call_target="tpu_custom_call" | custom-call | flops 1 | bytes 1 | tf_op jit(solution)/shard_map/mlp_grad/pallas_call | solution.py:94
  174.2 2.2 copy-done.5
  179.1 2.0 add_convert_fusion.1
  181.1 2.3 add_convert_fusion.2
  184.0 6.2 %residual_back.1 = (f32[528,1024]{1,0:T(8,128)S(1)}, bf16[528,1024]{1,0:T(8,128)(2,1)S(1)}, bf16[528,512]{1,0:T(8,128)(2,1)S(1)}, bf16[528,512]{1,0:T(8,128)(2,1)S(1)}, f32[8,1024]{1,0:T(8,128)S(1)}) custom-call(s32[24]{0:T(128)S(1)} %copy-done.41, f32[528,1024]{1,0:T(8,128)S(1)} %copy-done.19, bf16[2112,1024]{1,0:T(8,128)(2,1)S(1)} %bitcast.55, ...), custom_call_target="tpu_custom_call" | custom-call | flops 1 | bytes 1 | tf_op jit(solution)/shard_map/residual_back/pallas_call | solution.py:94
  196.4 9.8 %attend_back.2 = (bf16[1056,768]{1,0:T(8,128)(2,1)S(1)}, f32[2,1,384]{2,1,0:T(1,128)S(1)}) custom-call(s32[24]{0:T(128)S(1)} %copy-done.41, bf16[1056,1536]{1,0:T(8,128)(2,1)S(1)} %copy-done.17, s32[3,352,1]{2,1,0:T(8,128)S(1)} %broadcast_select_fusion.key_ids, s32[3,1,352]{2,1,0:T(1,128)S(1)} %broadcast_select_fusion.1.query_ids, ...), custom_call_target="tpu_custom_call" | custom-call | flops 1 | bytes 1 | tf_op jit(solution)/shard_map/attend_back/pallas_call | solution.py:94
  206.2 1.8 collective-permute-done.34.got_ahead
  212.4 5.1 %qkv_grad.2.rest_0_ = bf16[1024,2048]{1,0:T(8,128)(2,1)S(1)} custom-call(s32[24]{0:T(128)S(1)} %copy-done.41, bf16[1056,1024]{1,0:T(8,128)(2,1)S(1)} %copy-done.15, bf16[1056,768]{1,0:T(8,128)(2,1)S(1)} %get-tuple-element.280.grad_ref.refs_1_, bf16[528,1024]{1,0:T(8,128)(2,1)S(1)} %get-tuple-element.268.own_ref, ...), custom_call_target="tpu_custom_call" | custom-call | flops 1 | bytes 1 | tf_op jit(solution)/shard_map/qkv_grad/pallas_call | solution.py:94
  217.5 9.8 %attend_back.3 = (bf16[1056,768]{1,0:T(8,128)(2,1)S(1)}, f32[2,1,384]{2,1,0:T(1,128)S(1)}) custom-call(s32[24]{0:T(128)S(1)} %copy-done.41, bf16[1056,1536]{1,0:T(8,128)(2,1)S(1)} %copy-done.17, s32[3,352,1]{2,1,0:T(8,128)S(1)} %broadcast_select_fusion.key_ids, s32[3,1,352]{2,1,0:T(1,128)S(1)} %broadcast_select_fusion.1.query_ids, ...), custom_call_target="tpu_custom_call" | custom-call | flops 1 | bytes 1 | tf_op jit(solution)/shard_map/attend_back/pallas_call | solution.py:94
  227.4 1.8 collective-permute-done.41
  232.9 5.1 %qkv_grad.3.ahead_ref.behind_ref.own_ref = bf16[1024,2048]{1,0:T(8,128)(2,1)S(1)} custom-call(s32[24]{0:T(128)S(1)} %copy-done.41, bf16[1056,1024]{1,0:T(8,128)(2,1)S(1)} %copy-done.15, bf16[1056,768]{1,0:T(8,128)(2,1)S(1)} %get-tuple-element.282.grad_ref.refs_0_, bf16[528,1024]{1,0:T(8,128)(2,1)S(1)} %get-tuple-element.268.own_ref, ...), custom_call_target="tpu_custom_call", output_to_operand_aliasing={{}: (7, {})} | custom-call | flops 1 | bytes 1 | tf_op jit(solution)/shard_map/qkv_grad/pallas_call | solution.py:94
  240.6 9.9 %collective-permute-done.43.got_ahead = bf16[64,2048]{1,0:T(8,128)(2,1)S(1)} collective-permute-done((bf16[64,2048]{1,0:T(8,128)(2,1)S(1)}, bf16[64,2048]{1,0:T(8,128)(2,1)S(1)}, u32[]{:S(2)}, u32[]{:S(2)}) %collective-permute-start.43) | collective-permute-done | bytes 262176 | tf_op jit(solution)/shard_map/ppermute | solution.py:131
  252.3 2.2 add_convert_fusion.refs_0_.refs_3_
  257.3 12.1 %first_norm.1 = (bf16[528,1024]{1,0:T(8,128)(2,1)}, f32[8,1024]{1,0:T(8,128)}) custom-call(s32[24]{0:T(128)} %copy-done.40, bf16[1056,768]{1,0:T(8,128)(2,1)} %copy-done.21, bf16[1056,768]{1,0:T(8,128)(2,1)} %copy-done.20, bf16[1056,768]{1,0:T(8,128)(2,1)} %copy-done.66, bf16[1056,768]{1,0:T(8,128)(2,1)} %copy-done.65, bf16[2112,1024]{1,0:T(8,128)(2,1)} %copy-done.8, ...), custom_call_target="tpu_custom_call" | custom-call | flops 1 | bytes 1 | tf_op jit(solution)/shard_map/first_norm/pallas_call | solution.py:94
  277.2 6.6 %assemble.2 = bf16[2070,1024]{1,0:T(8,128)(2,1)} custom-call(s32[24]{0:T(128)} %copy-done.40, bf16[1056,1024]{1,0:T(8,128)(2,1)} %add_convert_fusion.refs_0_.refs_3_, bf16[1056,1024]{1,0:T(8,128)(2,1)} %collective-permute-done.50.refs_1_.refs_2_, bf16[1056,1024]{1,0:T(8,128)(2,1)} %collective-permute-done.50.refs_1_.refs_2_, ...), custom_call_target="tpu_custom_call" | custom-call | flops 1 | bytes 1 | tf_op jit(solution)/shard_map/assemble/pallas_call | solution.py:94
  283.8 2.7 collective-permute-done.51.got_ahead
  291.1 6.4 %collective-permute-done.57.refs_3_ = bf16[528,1024]{1,0:T(8,128)(2,1)} collective-permute-done((bf16[528,1024]{1,0:T(8,128)(2,1)}, bf16[528,1024]{1,0:T(8,128)(2,1)}, u32[]{:S(2)}, u32[]{:S(2)}) %collective-permute-start.57) | collective-permute-done | bytes 1081376 | tf_op jit(solution)/shard_map/ppermute | solution.py:227
  299.5 4.1 %collective-permute-done.54.got_ahead = bf16[128,2048]{1,0:T(8,128)(2,1)S(1)} collective-permute-done((bf16[128,2048]{1,0:T(8,128)(2,1)}, bf16[128,2048]{1,0:T(8,128)(2,1)S(1)}, u32[]{:S(2)}, u32[]{:S(2)}) %collective-permute-start.54) | collective-permute-done | bytes 524320 | tf_op jit(solution)/shard_map/ppermute | solution.py:131
  303.5 2.2 copy-done.4
  309.0 7.0 %assemble.3 = f32[2070,1024]{1,0:T(8,128)} custom-call(s32[24]{0:T(128)} %copy-done.40, bf16[528,1024]{1,0:T(8,128)(2,1)} %get-tuple-element.325.refs_0_, bf16[528,1024]{1,0:T(8,128)(2,1)} %collective-permute-done.56.refs_1_, bf16[528,1024]{1,0:T(8,128)(2,1)} %collective-permute-done.58.refs_2_, bf16[528,1024]{1,0:T(8,128)(2,1)} %collective-permute-done.57.refs_3_), custom_call_target="tpu_custom_call" | custom-call | flops 1 | bytes 1 | tf_op jit(solution)/shard_map/assemble/pallas_call | solution.py:94
  318.9 2.4 collective-permute-done.62
  (335 shorter events, 90.4 us)
Async XLA Ops:
  3.9 9.4 %collective-permute-start.1 = (bf16[128,1024]{1,0:T(8,128)(2,1)S(1)}, bf16[128,1024]{1,0:T(8,128)(2,1)S(1)}, u32[]{:S(2)}, u32[]{:S(2)}) collective-permute-start(bf16[128,1024]{1,0:T(8,128)(2,1)S(1)} %pad_maximum_fusion.6.rest_0_), channel_id=1, source_target_pairs={{4,12},{12,20},{20,28},{28,24},{24,16},{16,8},{8,0},{0,4},{5,13},{... | collective-permute-start | bytes 786440 | tf_op jit(solution)/shard_map/ppermute | solution.py:131
  14.7 14.4 %collective-permute-start.5 = (bf16[256,1024]{1,0:T(8,128)(2,1)S(1)}, bf16[256,1024]{1,0:T(8,128)(2,1)S(1)}, u32[]{:S(2)}, u32[]{:S(2)}) collective-permute-start(bf16[256,1024]{1,0:T(8,128)(2,1)S(1)} %pad_maximum_fusion.1), channel_id=1, source_target_pairs={{0,2},{1,3},{2,0},{3,1},{4,6},{5,7},{6,4},{7,5},{8,10},{9,11},{10,... | collective-permute-start | bytes 1572872 | tf_op jit(solution)/shard_map/ppermute | solution.py:227
  16.3 12.8 %collective-permute-start.3 = (bf16[128,1024]{1,0:T(8,128)(2,1)S(1)}, bf16[128,1024]{1,0:T(8,128)(2,1)S(1)}, u32[]{:S(2)}, u32[]{:S(2)}) collective-permute-start(bf16[128,1024]{1,0:T(8,128)(2,1)S(1)} %collective-permute-done.1.rest_1_), channel_id=1, source_target_pairs={{4,12},{12,20},{20,28},{28,24},{24,16},{16,8},{8,0},{0,4},{5,13},{... | collective-permute-start | bytes 786440 | tf_op jit(solution)/shard_map/ppermute | solution.py:131
  17.9 11.3 %collective-permute-start.4 = (bf16[128,1024]{1,0:T(8,128)(2,1)S(1)}, bf16[128,1024]{1,0:T(8,128)(2,1)S(1)}, u32[]{:S(2)}, u32[]{:S(2)}) collective-permute-start(bf16[128,1024]{1,0:T(8,128)(2,1)S(1)} %collective-permute-done.2.rest_2_), channel_id=1, source_target_pairs={{4,0},{12,4},{20,12},{28,20},{24,28},{16,24},{8,16},{0,8},{5,1},{1... | collective-permute-start | bytes 786440 | tf_op jit(solution)/shard_map/ppermute | solution.py:134
  32.1 13.8 %collective-permute-start.10 = (bf16[256,1024]{1,0:T(8,128)(2,1)}, bf16[256,1024]{1,0:T(8,128)(2,1)S(1)}, u32[]{:S(2)}, u32[]{:S(2)}) collective-permute-start(bf16[256,1024]{1,0:T(8,128)(2,1)} %pad_maximum_fusion.2), channel_id=1, source_target_pairs={{0,2},{1,3},{2,0},{3,1},{4,6},{5,7},{6,4},{7,5},{8,10},{9,11},{10,... | collective-permute-start | bytes 1572872 | tf_op jit(solution)/shard_map/ppermute | solution.py:227
  41.9 19.4 %collective-permute-start.11 = (bf16[256,1024]{1,0:T(8,128)(2,1)}, bf16[256,1024]{1,0:T(8,128)(2,1)S(1)}, u32[]{:S(2)}, u32[]{:S(2)}) collective-permute-start(bf16[256,1024]{1,0:T(8,128)(2,1)} %pad_maximum_fusion.3), channel_id=1, source_target_pairs={{0,2},{1,3},{2,0},{3,1},{4,6},{5,7},{6,4},{7,5},{8,10},{9,11},{10,... | collective-permute-start | bytes 1572872 | tf_op jit(solution)/shard_map/ppermute | solution.py:227
  46.6 15.4 %collective-permute-start.13 = (bf16[128,2048]{1,0:T(8,128)(2,1)}, bf16[128,2048]{1,0:T(8,128)(2,1)}, u32[]{:S(2)}, u32[]{:S(2)}) collective-permute-start(bf16[128,2048]{1,0:T(8,128)(2,1)} %pad_maximum_fusion.4.rest_0_), channel_id=1, source_target_pairs={{4,12},{12,20},{20,28},{28,24},{24,16},{16,8},{8,0},{0,4},{5,13},{... | collective-permute-start | bytes 1572872 | tf_op jit(solution)/shard_map/ppermute | solution.py:131
  48.2 13.9 %collective-permute-start.14 = (bf16[128,2048]{1,0:T(8,128)(2,1)}, bf16[128,2048]{1,0:T(8,128)(2,1)}, u32[]{:S(2)}, u32[]{:S(2)}) collective-permute-start(bf16[128,2048]{1,0:T(8,128)(2,1)} %pad_maximum_fusion.4.rest_0_), channel_id=1, source_target_pairs={{4,0},{12,4},{20,12},{28,20},{24,28},{16,24},{8,16},{0,8},{5,1},{1... | collective-permute-start | bytes 1572872 | tf_op jit(solution)/shard_map/ppermute | solution.py:134
  49.4 11.2 %collective-permute-start.12 = (bf16[128,1024]{1,0:T(8,128)(2,1)S(1)}, bf16[128,1024]{1,0:T(8,128)(2,1)S(1)}, u32[]{:S(2)}, u32[]{:S(2)}) collective-permute-start(bf16[128,1024]{1,0:T(8,128)(2,1)S(1)} %pad_maximum_fusion.7), channel_id=1, source_target_pairs={{0,2},{1,3},{2,0},{3,1},{4,6},{5,7},{6,4},{7,5},{8,10},{9,11},{10,... | collective-permute-start | bytes 786440 | tf_op jit(solution)/shard_map/ppermute | solution.py:227
  62.1 11.3 %collective-permute-start.15 = (bf16[128,2048]{1,0:T(8,128)(2,1)}, bf16[128,2048]{1,0:T(8,128)(2,1)S(1)}, u32[]{:S(2)}, u32[]{:S(2)}) collective-permute-start(bf16[128,2048]{1,0:T(8,128)(2,1)} %collective-permute-done.13.rest_1_), channel_id=1, source_target_pairs={{4,12},{12,20},{20,28},{28,24},{24,16},{16,8},{8,0},{0,4},{5,13},{... | collective-permute-start | bytes 1572872 | tf_op jit(solution)/shard_map/ppermute | solution.py:131
  63.3 11.5 %collective-permute-start.16 = (bf16[128,2048]{1,0:T(8,128)(2,1)}, bf16[128,2048]{1,0:T(8,128)(2,1)S(1)}, u32[]{:S(2)}, u32[]{:S(2)}) collective-permute-start(bf16[128,2048]{1,0:T(8,128)(2,1)} %collective-permute-done.14.rest_2_), channel_id=1, source_target_pairs={{4,0},{12,4},{20,12},{28,20},{24,28},{16,24},{8,16},{0,8},{5,1},{1... | collective-permute-start | bytes 1572872 | tf_op jit(solution)/shard_map/ppermute | solution.py:134
  74.8 16.2 %collective-permute-start.19 = (bf16[1024,2048]{1,0:T(8,128)(2,1)S(1)}, bf16[1024,2048]{1,0:T(8,128)(2,1)S(1)}, u32[]{:S(2)}, u32[]{:S(2)}) collective-permute-start(bf16[1024,2048]{1,0:T(8,128)(2,1)S(1)} %get-tuple-element.219.rest_0_.rest_3_.refs_13_), channel_id=1, source_target_pairs={{0,1},{1,0},{2,3},{3,2},{4,5},{5,4},{6,7},{7,6},{8,9},{9,8},{10,11... | collective-permute-start | bytes 12582920 | tf_op jit(solution)/shard_map/ppermute | solution.py:231
  74.9 16.1 %collective-permute-start.17 = (bf16[128,2048]{1,0:T(8,128)(2,1)S(1)}, bf16[128,2048]{1,0:T(8,128)(2,1)S(1)}, u32[]{:S(2)}, u32[]{:S(2)}) collective-permute-start(bf16[128,2048]{1,0:T(8,128)(2,1)S(1)} %collective-permute-done.15.rest_3_), channel_id=1, source_target_pairs={{4,12},{12,20},{20,28},{28,24},{24,16},{16,8},{8,0},{0,4},{5,13},{... | collective-permute-start | bytes 1572872 | tf_op jit(solution)/shard_map/ppermute | solution.py:131
  76.5 14.5 %collective-permute-start.18 = (bf16[128,2048]{1,0:T(8,128)(2,1)S(1)}, bf16[128,2048]{1,0:T(8,128)(2,1)S(1)}, u32[]{:S(2)}, u32[]{:S(2)}) collective-permute-start(bf16[128,2048]{1,0:T(8,128)(2,1)S(1)} %collective-permute-done.16.rest_4_), channel_id=1, source_target_pairs={{4,0},{12,4},{20,12},{28,20},{24,28},{16,24},{8,16},{0,8},{5,1},{1... | collective-permute-start | bytes 1572872 | tf_op jit(solution)/shard_map/ppermute | solution.py:134
  101.3 26.5 %collective-permute-start.24 = (bf16[528,1024]{1,0:T(8,128)(2,1)}, bf16[528,1024]{1,0:T(8,128)(2,1)S(1)}, u32[]{:S(2)}, u32[]{:S(2)}) collective-permute-start(bf16[528,1024]{1,0:T(8,128)(2,1)} %get-tuple-element.226.rest_9_.rest_0_), channel_id=1, source_target_pairs={{0,2},{1,3},{2,0},{3,1},{4,6},{5,7},{6,4},{7,5},{8,10},{9,11},{10,... | collective-permute-start | bytes 3244040 | tf_op jit(solution)/shard_map/ppermute | solution.py:227
  142.6 35.5 %collective-permute-start.28 = (bf16[528,1024]{1,0:T(8,128)(2,1)S(1)}, bf16[528,1024]{1,0:T(8,128)(2,1)}, u32[]{:S(2)}, u32[]{:S(2)}) collective-permute-start(bf16[528,1024]{1,0:T(8,128)(2,1)S(1)} %copy-done.73), channel_id=1, source_target_pairs={{0,1},{1,0},{2,3},{3,2},{4,5},{5,4},{6,7},{7,6},{8,9},{9,8},{10,11... | collective-permute-start | bytes 3244040 | tf_op jit(solution)/shard_map/ppermute | solution.py:231
  143.0 38.1 %collective-permute-start.27 = (bf16[528,1024]{1,0:T(8,128)(2,1)}, bf16[528,1024]{1,0:T(8,128)(2,1)}, u32[]{:S(2)}, u32[]{:S(2)}) collective-permute-start(bf16[528,1024]{1,0:T(8,128)(2,1)} %get-tuple-element.241), channel_id=1, source_target_pairs={{0,1},{1,0},{2,3},{3,2},{4,5},{5,4},{6,7},{7,6},{8,9},{9,8},{10,11... | collective-permute-start | bytes 3244040 | tf_op jit(solution)/shard_map/ppermute | solution.py:231
  143.1 40.4 %collective-permute-start.29 = (bf16[528,1024]{1,0:T(8,128)(2,1)}, bf16[528,1024]{1,0:T(8,128)(2,1)}, u32[]{:S(2)}, u32[]{:S(2)}) collective-permute-start(bf16[528,1024]{1,0:T(8,128)(2,1)} %get-tuple-element.247), channel_id=1, source_target_pairs={{0,1},{1,0},{2,3},{3,2},{4,5},{5,4},{6,7},{7,6},{8,9},{9,8},{10,11... | collective-permute-start | bytes 3244040 | tf_op jit(solution)/shard_map/ppermute | solution.py:231
  157.8 26.2 %collective-permute-start.30 = (bf16[528,1024]{1,0:T(8,128)(2,1)}, bf16[528,1024]{1,0:T(8,128)(2,1)S(1)}, u32[]{:S(2)}, u32[]{:S(2)}) collective-permute-start(bf16[528,1024]{1,0:T(8,128)(2,1)} %get-tuple-element.248), channel_id=1, source_target_pairs={{0,2},{1,3},{2,0},{3,1},{4,6},{5,7},{6,4},{7,5},{8,10},{9,11},{10,... | collective-permute-start | bytes 3244040 | tf_op jit(solution)/shard_map/ppermute | solution.py:227
  177.0 14.6 %collective-permute-start.31 = (bf16[64,2048]{1,0:T(8,128)(2,1)S(1)}, bf16[64,2048]{1,0:T(8,128)(2,1)S(1)}, u32[]{:S(2)}, u32[]{:S(2)}) collective-permute-start(bf16[64,2048]{1,0:T(8,128)(2,1)S(1)} %get-tuple-element.251), channel_id=1, source_target_pairs={{4,12},{12,20},{20,28},{28,24},{24,16},{16,8},{8,0},{0,4},{5,13},{... | collective-permute-start | bytes 786440 | tf_op jit(solution)/shard_map/ppermute | solution.py:131
  178.1 13.5 %collective-permute-start.32 = (bf16[64,2048]{1,0:T(8,128)(2,1)S(1)}, bf16[64,2048]{1,0:T(8,128)(2,1)S(1)}, u32[]{:S(2)}, u32[]{:S(2)}) collective-permute-start(bf16[64,2048]{1,0:T(8,128)(2,1)S(1)} %get-tuple-element.253), channel_id=1, source_target_pairs={{4,0},{12,4},{20,12},{28,20},{24,28},{16,24},{8,16},{0,8},{5,1},{1... | collective-permute-start | bytes 786440 | tf_op jit(solution)/shard_map/ppermute | solution.py:134
  191.6 17.1 %collective-permute-start.36 = (bf16[528,1024]{1,0:T(8,128)(2,1)S(1)}, bf16[528,1024]{1,0:T(8,128)(2,1)S(1)}, u32[]{:S(2)}, u32[]{:S(2)}) collective-permute-start(bf16[528,1024]{1,0:T(8,128)(2,1)S(1)} %get-tuple-element.268.own_ref), channel_id=1, source_target_pairs={{0,1},{1,0},{2,3},{3,2},{4,5},{5,4},{6,7},{7,6},{8,9},{9,8},{10,11... | collective-permute-start | bytes 3244040 | tf_op jit(solution)/shard_map/ppermute | solution.py:231
  193.0 15.7 %collective-permute-start.39 = (bf16[264,1024]{1,0:T(8,128)(2,1)S(1)}, bf16[264,1024]{1,0:T(8,128)(2,1)S(1)}, u32[]{:S(2)}, u32[]{:S(2)}) collective-permute-start(bf16[264,1024]{1,0:T(8,128)(2,1)S(1)} %slice.179), channel_id=1, source_target_pairs={{0,2},{1,3},{2,0},{3,1},{4,6},{5,7},{6,4},{7,5},{8,10},{9,11},{10,... | collective-permute-start | bytes 1622024 | tf_op jit(solution)/shard_map/ppermute | solution.py:227
  194.4 13.6 %collective-permute-start.34 = (bf16[128,2048]{1,0:T(8,128)(2,1)S(1)}, bf16[128,2048]{1,0:T(8,128)(2,1)S(1)}, u32[]{:S(2)}, u32[]{:S(2)}) collective-permute-start(bf16[128,2048]{1,0:T(8,128)(2,1)S(1)} %get-tuple-element.262), channel_id=1, source_target_pairs={{4,12},{12,20},{20,28},{28,24},{24,16},{16,8},{8,0},{0,4},{5,13},{... | collective-permute-start | bytes 1572872 | tf_op jit(solution)/shard_map/ppermute | solution.py:131
  195.4 13.3 %collective-permute-start.35 = (bf16[128,2048]{1,0:T(8,128)(2,1)S(1)}, bf16[128,2048]{1,0:T(8,128)(2,1)S(1)}, u32[]{:S(2)}, u32[]{:S(2)}) collective-permute-start(bf16[128,2048]{1,0:T(8,128)(2,1)S(1)} %get-tuple-element.264), channel_id=1, source_target_pairs={{4,0},{12,4},{20,12},{28,20},{24,28},{16,24},{8,16},{0,8},{5,1},{1... | collective-permute-start | bytes 1572872 | tf_op jit(solution)/shard_map/ppermute | solution.py:134
  208.7 20.4 %collective-permute-start.40 = (bf16[1056,768]{1,0:T(8,128)(2,1)S(1)}, bf16[1056,768]{1,0:T(8,128)(2,1)S(1)}, u32[]{:S(2)}, u32[]{:S(2)}) collective-permute-start(bf16[1056,768]{1,0:T(8,128)(2,1)S(1)} %get-tuple-element.280.grad_ref.refs_1_), channel_id=1, source_target_pairs={{0,1},{1,0},{2,3},{3,2},{4,5},{5,4},{6,7},{7,6},{8,9},{9,8},{10,11... | collective-permute-start | bytes 4866056 | tf_op jit(solution)/shard_map/ppermute | solution.py:231
  208.8 20.4 %collective-permute-start.41 = (bf16[392,1024]{1,0:T(8,128)(2,1)S(1)}, bf16[392,1024]{1,0:T(8,128)(2,1)S(1)}, u32[]{:S(2)}, u32[]{:S(2)}) collective-permute-start(bf16[392,1024]{1,0:T(8,128)(2,1)S(1)} %pad_maximum_fusion), channel_id=1, source_target_pairs={{0,2},{1,3},{2,0},{3,1},{4,6},{5,7},{6,4},{7,5},{8,10},{9,11},{10,... | collective-permute-start | bytes 2408456 | tf_op jit(solution)/shard_map/ppermute | solution.py:227
  210.3 17.0 %collective-permute-start.37 = (bf16[128,2048]{1,0:T(8,128)(2,1)S(1)}, bf16[128,2048]{1,0:T(8,128)(2,1)S(1)}, u32[]{:S(2)}, u32[]{:S(2)}) collective-permute-start(bf16[128,2048]{1,0:T(8,128)(2,1)S(1)} %get-tuple-element.272), channel_id=1, source_target_pairs={{4,12},{12,20},{20,28},{28,24},{24,16},{16,8},{8,0},{0,4},{5,13},{... | collective-permute-start | bytes 1572872 | tf_op jit(solution)/shard_map/ppermute | solution.py:131
  211.7 15.6 %collective-permute-start.38 = (bf16[128,2048]{1,0:T(8,128)(2,1)S(1)}, bf16[128,2048]{1,0:T(8,128)(2,1)S(1)}, u32[]{:S(2)}, u32[]{:S(2)}) collective-permute-start(bf16[128,2048]{1,0:T(8,128)(2,1)S(1)} %get-tuple-element.274), channel_id=1, source_target_pairs={{4,0},{12,4},{20,12},{28,20},{24,28},{16,24},{8,16},{0,8},{5,1},{1... | collective-permute-start | bytes 1572872 | tf_op jit(solution)/shard_map/ppermute | solution.py:134
  229.1 9.4 %collective-permute-start.42 = (bf16[1056,768]{1,0:T(8,128)(2,1)S(1)}, bf16[1056,768]{1,0:T(8,128)(2,1)S(1)}, u32[]{:S(2)}, u32[]{:S(2)}) collective-permute-start(bf16[1056,768]{1,0:T(8,128)(2,1)S(1)} %get-tuple-element.282.grad_ref.refs_0_), channel_id=1, source_target_pairs={{0,1},{1,0},{2,3},{3,2},{4,5},{5,4},{6,7},{7,6},{8,9},{9,8},{10,11... | collective-permute-start | bytes 4866056 | tf_op jit(solution)/shard_map/ppermute | solution.py:231
  229.2 23.1 %collective-permute-start.47 = (bf16[400,1024]{1,0:T(8,128)(2,1)S(1)}, bf16[400,1024]{1,0:T(8,128)(2,1)S(1)}, u32[]{:S(2)}, u32[]{:S(2)}) collective-permute-start(bf16[400,1024]{1,0:T(8,128)(2,1)S(1)} %slice.180), channel_id=1, source_target_pairs={{0,2},{1,3},{2,0},{3,1},{4,6},{5,7},{6,4},{7,5},{8,10},{9,11},{10,... | collective-permute-start | bytes 2457608 | tf_op jit(solution)/shard_map/ppermute | solution.py:227
  230.8 20.8 %collective-permute-start.45 = (bf16[128,2048]{1,0:T(8,128)(2,1)S(1)}, bf16[128,2048]{1,0:T(8,128)(2,1)S(1)}, u32[]{:S(2)}, u32[]{:S(2)}) collective-permute-start(bf16[128,2048]{1,0:T(8,128)(2,1)S(1)} %get-tuple-element.287), channel_id=1, source_target_pairs={{4,12},{12,20},{20,28},{28,24},{24,16},{16,8},{8,0},{0,4},{5,13},{... | collective-permute-start | bytes 1572872 | tf_op jit(solution)/shard_map/ppermute | solution.py:131
  232.2 19.4 %collective-permute-start.46 = (bf16[128,2048]{1,0:T(8,128)(2,1)S(1)}, bf16[128,2048]{1,0:T(8,128)(2,1)S(1)}, u32[]{:S(2)}, u32[]{:S(2)}) collective-permute-start(bf16[128,2048]{1,0:T(8,128)(2,1)S(1)} %get-tuple-element.289), channel_id=1, source_target_pairs={{4,0},{12,4},{20,12},{28,20},{24,28},{16,24},{8,16},{0,8},{5,1},{1... | collective-permute-start | bytes 1572872 | tf_op jit(solution)/shard_map/ppermute | solution.py:134
  238.5 11.9 %collective-permute-start.43 = (bf16[64,2048]{1,0:T(8,128)(2,1)S(1)}, bf16[64,2048]{1,0:T(8,128)(2,1)S(1)}, u32[]{:S(2)}, u32[]{:S(2)}) collective-permute-start(bf16[64,2048]{1,0:T(8,128)(2,1)S(1)} %get-tuple-element.283), channel_id=1, source_target_pairs={{4,12},{12,20},{20,28},{28,24},{24,16},{16,8},{8,0},{0,4},{5,13},{... | collective-permute-start | bytes 786440 | tf_op jit(solution)/shard_map/ppermute | solution.py:131
  239.9 11.6 %collective-permute-start.44 = (bf16[64,2048]{1,0:T(8,128)(2,1)S(1)}, bf16[64,2048]{1,0:T(8,128)(2,1)S(1)}, u32[]{:S(2)}, u32[]{:S(2)}) collective-permute-start(bf16[64,2048]{1,0:T(8,128)(2,1)S(1)} %get-tuple-element.285), channel_id=1, source_target_pairs={{4,0},{12,4},{20,12},{28,20},{24,28},{16,24},{8,16},{0,8},{5,1},{1... | collective-permute-start | bytes 786440 | tf_op jit(solution)/shard_map/ppermute | solution.py:134
  255.2 14.2 %collective-permute-start.48 = (bf16[128,2048]{1,0:T(8,128)(2,1)S(1)}, bf16[128,2048]{1,0:T(8,128)(2,1)S(1)}, u32[]{:S(2)}, u32[]{:S(2)}) collective-permute-start(bf16[128,2048]{1,0:T(8,128)(2,1)S(1)} %get-tuple-element.305), channel_id=1, source_target_pairs={{4,12},{12,20},{20,28},{28,24},{24,16},{16,8},{8,0},{0,4},{5,13},{... | collective-permute-start | bytes 1572872 | tf_op jit(solution)/shard_map/ppermute | solution.py:131
  256.3 13.1 %collective-permute-start.49 = (bf16[128,2048]{1,0:T(8,128)(2,1)S(1)}, bf16[128,2048]{1,0:T(8,128)(2,1)S(1)}, u32[]{:S(2)}, u32[]{:S(2)}) collective-permute-start(bf16[128,2048]{1,0:T(8,128)(2,1)S(1)} %get-tuple-element.307), channel_id=1, source_target_pairs={{4,0},{12,4},{20,12},{28,20},{24,28},{16,24},{8,16},{0,8},{5,1},{1... | collective-permute-start | bytes 1572872 | tf_op jit(solution)/shard_map/ppermute | solution.py:134
  270.9 26.6 %collective-permute-start.57 = (bf16[528,1024]{1,0:T(8,128)(2,1)}, bf16[528,1024]{1,0:T(8,128)(2,1)}, u32[]{:S(2)}, u32[]{:S(2)}) collective-permute-start(bf16[528,1024]{1,0:T(8,128)(2,1)} %get-tuple-element.325.refs_0_), channel_id=1, source_target_pairs={{0,2},{1,3},{2,0},{3,1},{4,6},{5,7},{6,4},{7,5},{8,10},{9,11},{10,... | collective-permute-start | bytes 3244040 | tf_op jit(solution)/shard_map/ppermute | solution.py:227
  272.2 14.3 %collective-permute-start.51 = (bf16[128,2048]{1,0:T(8,128)(2,1)}, bf16[128,2048]{1,0:T(8,128)(2,1)S(1)}, u32[]{:S(2)}, u32[]{:S(2)}) collective-permute-start(bf16[128,2048]{1,0:T(8,128)(2,1)} %get-tuple-element.312), channel_id=1, source_target_pairs={{4,12},{12,20},{20,28},{28,24},{24,16},{16,8},{8,0},{0,4},{5,13},{... | collective-permute-start | bytes 1572872 | tf_op jit(solution)/shard_map/ppermute | solution.py:131
  273.2 14.1 %collective-permute-start.52 = (bf16[128,2048]{1,0:T(8,128)(2,1)S(1)}, bf16[128,2048]{1,0:T(8,128)(2,1)S(1)}, u32[]{:S(2)}, u32[]{:S(2)}) collective-permute-start(bf16[128,2048]{1,0:T(8,128)(2,1)S(1)} %get-tuple-element.314), channel_id=1, source_target_pairs={{4,0},{12,4},{20,12},{28,20},{24,28},{16,24},{8,16},{0,8},{5,1},{1... | collective-permute-start | bytes 1572872 | tf_op jit(solution)/shard_map/ppermute | solution.py:134
  274.3 14.6 %collective-permute-start.53 = (f32[8,1024]{1,0:T(8,128)S(1)}, f32[8,1024]{1,0:T(8,128)S(1)}, u32[]{:S(2)}, u32[]{:S(2)}) collective-permute-start(f32[8,1024]{1,0:T(8,128)S(1)} %copy-done.70), channel_id=1, source_target_pairs={{0,4},{4,0},{8,12},{12,8},{16,20},{20,16},{24,28},{28,24},{1,5},{5... | collective-permute-start | bytes 98312 | tf_op jit(solution)/shard_map/ppermute | solution.py:1186
  288.9 9.1 %collective-permute-start.59 = (f32[6,1024]{1,0:T(8,128)S(1)}, f32[6,1024]{1,0:T(8,128)S(1)}, u32[]{:S(2)}, u32[]{:S(2)}) collective-permute-start(f32[6,1024]{1,0:T(8,128)S(1)} %bitcast.72), channel_id=1, source_target_pairs={{0,1},{1,0},{2,3},{3,2},{4,5},{5,4},{6,7},{7,6},{8,9},{9,8},{10,11... | collective-permute-start | bytes 73736 | tf_op jit(solution)/shard_map/ppermute | solution.py:231
  289.0 14.5 %collective-permute-start.54 = (bf16[128,2048]{1,0:T(8,128)(2,1)}, bf16[128,2048]{1,0:T(8,128)(2,1)S(1)}, u32[]{:S(2)}, u32[]{:S(2)}) collective-permute-start(bf16[128,2048]{1,0:T(8,128)(2,1)} %get-tuple-element.320), channel_id=1, source_target_pairs={{4,12},{12,20},{20,28},{28,24},{24,16},{16,8},{8,0},{0,4},{5,13},{... | collective-permute-start | bytes 1572872 | tf_op jit(solution)/shard_map/ppermute | solution.py:131
  289.5 14.0 %collective-permute-start.55 = (bf16[128,2048]{1,0:T(8,128)(2,1)S(1)}, bf16[128,2048]{1,0:T(8,128)(2,1)S(1)}, u32[]{:S(2)}, u32[]{:S(2)}) collective-permute-start(bf16[128,2048]{1,0:T(8,128)(2,1)S(1)} %get-tuple-element.322), channel_id=1, source_target_pairs={{4,0},{12,4},{20,12},{28,20},{24,28},{16,24},{8,16},{0,8},{5,1},{1... | collective-permute-start | bytes 1572872 | tf_op jit(solution)/shard_map/ppermute | solution.py:134
  297.5 11.5 %collective-permute-start.56 = (bf16[528,1024]{1,0:T(8,128)(2,1)}, bf16[528,1024]{1,0:T(8,128)(2,1)}, u32[]{:S(2)}, u32[]{:S(2)}) collective-permute-start(bf16[528,1024]{1,0:T(8,128)(2,1)} %get-tuple-element.325.refs_0_), channel_id=1, source_target_pairs={{0,1},{1,0},{2,3},{3,2},{4,5},{5,4},{6,7},{7,6},{8,9},{9,8},{10,11... | collective-permute-start | bytes 3244040 | tf_op jit(solution)/shard_map/ppermute | solution.py:231
  297.5 11.5 %collective-permute-start.58 = (bf16[528,1024]{1,0:T(8,128)(2,1)}, bf16[528,1024]{1,0:T(8,128)(2,1)}, u32[]{:S(2)}, u32[]{:S(2)}) collective-permute-start(bf16[528,1024]{1,0:T(8,128)(2,1)} %collective-permute-done.57.refs_3_), channel_id=1, source_target_pairs={{0,1},{1,0},{2,3},{3,2},{4,5},{5,4},{6,7},{7,6},{8,9},{9,8},{10,11... | collective-permute-start | bytes 3244040 | tf_op jit(solution)/shard_map/ppermute | solution.py:231
  298.1 9.3 %collective-permute-start.60 = (f32[6656]{0:T(1024)S(1)}, f32[6656]{0:T(1024)S(1)}, u32[]{:S(2)}, u32[]{:S(2)}) collective-permute-start(f32[6656]{0:T(1024)S(1)} %pad_maximum_fusion.9), channel_id=1, source_target_pairs={{0,2},{1,3},{2,0},{3,1},{4,6},{5,7},{6,4},{7,5},{8,10},{9,11},{10,... | collective-permute-start | bytes 79880 | tf_op jit(solution)/shard_map/ppermute | solution.py:227
  306.6 9.4 %collective-permute-start.63 = (bf16[128,1024]{1,0:T(8,128)(2,1)S(1)}, bf16[128,1024]{1,0:T(8,128)(2,1)S(1)}, u32[]{:S(2)}, u32[]{:S(2)}) collective-permute-start(bf16[128,1024]{1,0:T(8,128)(2,1)S(1)} %slice.163), channel_id=1, source_target_pairs={{0,2},{1,3},{2,0},{3,1},{4,6},{5,7},{6,4},{7,5},{8,10},{9,11},{10,... | collective-permute-start | bytes 786440 | tf_op jit(solution)/shard_map/ppermute | solution.py:227
  (94 other events, 864.7 us)

commit v4 on v3

--- a/solution.py
+++ b/solution.py
@@ -198,26 +198,27 @@
             near = middle - step
             if near == 0:
                 break
+            final = near == 1
             kernel = call(
                 ring_add_body,
                 grid,
-                [block(near), block(-near)] + [plain(forward.shape[0])] * 2,
-                [plain(rows)] * 2,
-                [shape((rows, columns), bf16)] * 2,
+                [block(near), block(-near)] + [block(0)] * final + [plain(forward.shape[0])] * 2,
+                [plain(rows)] * (2 + final),
+                [shape((rows, columns), bf16)] * (2 + final),
                 [],
                 "ring_add",
             )
-            forward, backward = order.run(kernel, whole, whole, forward, backward)
+            forward, backward, *own = order.run(kernel, *[whole] * (2 + final), forward, backward)
         kernel = call(
             ring_last_body,
             grid,
-            [block(0)] + [plain(rows)] * 2,
+            [plain(rows)] * 3,
             plain(rows),
             shape((rows, columns), f32),
             [],
             last,
         )
-        yield order.run(kernel, whole, forward, backward)
+        yield order.run(kernel, *own, forward, backward)
 
 
 def across(value, step, chips):
@@ -265,7 +266,11 @@
     behind_out[...] = behind_ref[...]
 
 
-def ring_add_body(info, ahead_ref, behind_ref, got_ahead, got_behind, ahead_out, behind_out):
+def ring_add_body(info, ahead_ref, behind_ref, *rest):
+    if len(rest) == 6:
+        own_ref, *rest, own_out = rest
+        own_out[...] = own_ref[...]
+    got_ahead, got_behind, ahead_out, behind_out = rest
     rows, part = ahead_out.shape[0], got_ahead.shape[0]
     first, last = slice(0, part), slice(rows - part, rows)
     total = ahead_ref[first, :].astype(f32) + got_ahead[...].astype(f32)

time: 323 us -> 321 us (level)
    unnamed x161 -> x159, local copies, waits for them, and re-layouts: 32.9 us -> 30.7 us
  transfers between devices with their start and end apart: 64 -> 64, of which waited for: 25 -> 26; matrix products, arithmetic and copies ran while one was open for 5% -> 5% of each run, Pallas kernels for 45% -> 45%
where the time goes in v4:
time: 321 us
  Pallas kernels  158 us (49%)
  waiting for transfers between devices  56.4 us (18%)
  starting transfers between devices  54.2 us (17%)
  local copies, waits for them, and re-layouts  37.3 us (12%)
  other arithmetic  12.7 us (4%)
    pallas_call x28, Pallas kernels, run(): out = kernel(tie(self.info, self.now, wait, self.hold), *values)  158 us
    unnamed x159, local copies, waits for them, and re-layouts  30.7 us
    ppermute x16, waiting for transfers between devices, send_ahead(): return lax.ppermute(value, 'dp', self.ahead)  23.5 us
    ppermute x16, starting transfers between devices, send_ahead(): return lax.ppermute(value, 'dp', self.ahead)  22.8 us
    ppermute x13, starting transfers between devices, across(): return lax.ppermute(value, 'mp', pairs)  14.2 us
    ppermute x13, waiting for transfers between devices, across(): return lax.ppermute(value, 'mp', pairs)  13.7 us
    ppermute x16, starting transfers between devices, send_behind(): return lax.ppermute(value, 'dp', self.behind)  11.3 us
    ppermute x16, waiting for transfers between devices, send_behind(): return lax.ppermute(value, 'dp', self.behind)  8.58 us
  transfers between devices with their start and end apart: 64, of which 26 were waited for; matrix products, arithmetic and copies ran while one was open for 5% of the time, Pallas kernels for 45%

profile of v4, /device:TPU:0, one launch (start us, length us, event | category | flops | bytes accessed | tf_op | source)
XLA Modules:
  0.0 320.5 jit_solution(187886745201423302)
XLA Ops:
  3.9 3.0 collective-permute-start.1
  7.2 1.9 collective-permute-start
  9.1 4.2 %collective-permute-done.1.rest_1_ = bf16[128,1024]{1,0:T(8,128)(2,1)S(1)} collective-permute-done((bf16[128,1024]{1,0:T(8,128)(2,1)S(1)}, bf16[128,1024]{1,0:T(8,128)(2,1)S(1)}, u32[]{:S(2)}, u32[]{:S(2)}) %collective-permute-start.1) | collective-permute-done | bytes 262176 | tf_op jit(solution)/shard_map/ppermute | solution.py:131
  18.3 2.2 copy-done.21
  20.5 3.0 pad.83.x_ref.refs_4_
  23.5 2.1 first_low.1.x_ref.first_ref
  25.7 2.1 copy-done.7
  29.2 1.6 collective-permute-start.6
  34.6 1.9 copy.90
  39.2 1.8 pad_maximum_fusion.4.rest_0_
  43.8 2.1 collective-permute-done.10.rest_11_
  49.3 1.6 collective-permute-start.12
  53.2 2.2 copy-done.22
  55.5 3.0 pad.84.cot_ref
  58.5 2.0 copy-done.6
  67.5 5.5 %qkv.1 = (bf16[1056,1536]{1,0:T(8,128)(2,1)S(1)}, bf16[1024,2048]{1,0:T(8,128)(2,1)S(1)}) custom-call(s32[24]{0:T(128)S(1)} %concatenate.49.info, bf16[1056,1024]{1,0:T(8,128)(2,1)S(1)} %copy-done.13, f32[1,1536]{1,0:T(1,128)S(1)} %pad_maximum_fusion.10.bias_ref, bf16[128,1024]{1,0:T(8,128)(2,1)S(1)} %pad_maximum_fusion.6.rest_0_, ...), custom_call_target="tpu_custom_call" | custom-call | flops 1 | bytes 1 | tf_op jit(solution)/shard_map/qkv/pallas_call | solution.py:94
  77.0 12.4 %attend.1 = (bf16[1056,512]{1,0:T(8,128)(2,1)S(1)}, f32[3,4,2,352]{3,2,1,0:T(2,128)S(1)}) custom-call(s32[24]{0:T(128)S(1)} %concatenate.49.info, bf16[1056,1536]{1,0:T(8,128)(2,1)S(1)} %get-tuple-element.208.qkv_ref, s32[3,352,1]{2,1,0:T(8,128)S(1)} %broadcast_select_fusion.key_ids, s32[3,1,352]{2,1,0:T(1,128)S(1)} %broadcast_select_fusion.1.query_ids), custom_call_target="tpu_custom_call" | custom-call | flops 1 | bytes 1 | tf_op jit(solution)/shard_map/attend/pallas_call | solution.py:94
  89.3 1.7 copy-done.15
  91.2 1.6 collective-permute-start.21
  93.9 4.3 %proj_norm.1 = (f32[528,1024]{1,0:T(8,128)S(1)}, bf16[528,1024]{1,0:T(8,128)(2,1)}) custom-call(s32[24]{0:T(128)S(1)} %concatenate.49.info, bf16[1056,512]{1,0:T(8,128)(2,1)S(1)} %get-tuple-element.222.own_ref.att_own.att_got, bf16[1056,512]{1,0:T(8,128)(2,1)S(1)} %collective-permute-done.20.got_ref, bf16[2112,1024]{1,0:T(8,128)(2,1)S(1)} %bitcast.57, ...), custom_call_target="tpu_custom_call" | custom-call | flops 1 | bytes 1 | tf_op jit(solution)/shard_map/proj_norm/pallas_call | solution.py:94
  101.3 2.9 collective-permute-done.23.rest_10_.rest_1_
  105.2 19.3 %mlp.3 = (bf16[1056,1024]{1,0:T(8,128)(2,1)}, bf16[1056,1024]{1,0:T(8,128)(2,1)}, bf16[528,1024]{1,0:T(8,128)(2,1)}, bf16[528,1024]{1,0:T(8,128)(2,1)}, bf16[528...) custom-call(s32[24]{0:T(128)} %copy-done.39, bf16[2112,1024]{1,0:T(8,128)(2,1)} %copy-done.6, ...), custom_call_target="tpu_custom_call" | custom-call | flops 1 | bytes 1 | tf_op jit(solution)/shard_map/mlp/pallas_call | solution.py:94
  124.5 3.3 %collective-permute-done.24.rest_9_.rest_3_ = bf16[528,1024]{1,0:T(8,128)(2,1)S(1)} collective-permute-done((bf16[528,1024]{1,0:T(8,128)(2,1)}, bf16[528,1024]{1,0:T(8,128)(2,1)S(1)}, u32[]{:S(2)}, u32[]{:S(2)}) %collective-permute-start.24) | collective-permute-done | bytes 1081376 | tf_op jit(solution)/shard_map/ppermute | solution.py:228
  127.8 2.7 collective-permute-done.25.rest_9_.rest_2_
  131.5 10.8 %mlp.4 = (bf16[528,1024]{1,0:T(8,128)(2,1)}, bf16[528,1024]{1,0:T(8,128)(2,1)}, bf16[528,1024]{1,0:T(8,128)(2,1)}, bf16[528,1024]{1,0:T(8,128)(2,1)}, f32[1,1024]{1,0:T(1,128)}) custom-call(s32[24]{0:T(128)} %copy-done.39, bf16[2112,1024]{1,0:T(8,128)(2,1)} %copy-done.6, f32[1,1024]{1,0:T(1,128)} %bitcast.75, bf16[128,2048]{1,0:T(8,128)(2,1)} %pad_maximum_fusion.4.rest_0_, ...), custom_call_target="tpu_custom_call" | custom-call | flops 1 | bytes 1 | tf_op jit(solution)/shard_map/mlp/pallas_call | solution.py:94
  143.4 2.0 collective-permute-done.26.rest_10_
  146.4 11.2 %mlp.5 = (bf16[528,1024]{1,0:T(8,128)(2,1)}, bf16[528,1024]{1,0:T(8,128)(2,1)}, bf16[528,1024]{1,0:T(8,128)(2,1)}, bf16[528,1024]{1,0:T(8,128)(2,1)}, f32[1,1024]{1,0:T(1,128)}) custom-call(s32[24]{0:T(128)} %copy-done.39, bf16[2112,1024]{1,0:T(8,128)(2,1)} %copy-done.6, f32[1,1024]{1,0:T(1,128)} %bitcast.76, bf16[128,2048]{1,0:T(8,128)(2,1)} %pad_maximum_fusion.4.rest_0_, ...), custom_call_target="tpu_custom_call" | custom-call | flops 1 | bytes 1 | tf_op jit(solution)/shard_map/mlp/pallas_call | solution.py:94
  158.1 16.1 %mlp_grad.1.ahead_ref.behind_ref.rest_0_ = bf16[1024,2048]{1,0:T(8,128)(2,1)} custom-call(s32[24]{0:T(128)} %copy-done.39, bf16[2112,1024]{1,0:T(8,128)(2,1)} %copy-done.6, bf16[528,1024]{1,0:T(8,128)(2,1)} %get-tuple-element.228.rest_9_.rest_0_, bf16[528,1024]{1,0:T(8,128)(2,1)} %copy-done.59, bf16[528,1024]{1,0:T(8,128)(2,1)} %copy-done.61, ...), custom_call_target="tpu_custom_call" | custom-call | flops 1 | bytes 1 | tf_op jit(solution)/shard_map/mlp_grad/pallas_call | solution.py:94
  174.2 2.2 copy-done.4
  179.1 2.0 add_convert_fusion.1
  181.1 2.3 add_convert_fusion.2
  183.8 6.2 %residual_back.1 = (f32[528,1024]{1,0:T(8,128)S(1)}, bf16[528,1024]{1,0:T(8,128)(2,1)S(1)}, bf16[528,512]{1,0:T(8,128)(2,1)S(1)}, bf16[528,512]{1,0:T(8,128)(2,1)S(1)}, f32[8,1024]{1,0:T(8,128)S(1)}) custom-call(s32[24]{0:T(128)S(1)} %copy-done.40, f32[528,1024]{1,0:T(8,128)S(1)} %copy-done.18, bf16[2112,1024]{1,0:T(8,128)(2,1)S(1)} %bitcast.55, ...), custom_call_target="tpu_custom_call" | custom-call | flops 1 | bytes 1 | tf_op jit(solution)/shard_map/residual_back/pallas_call | solution.py:94
  196.2 9.8 %attend_back.2 = (bf16[1056,768]{1,0:T(8,128)(2,1)S(1)}, f32[2,1,384]{2,1,0:T(1,128)S(1)}) custom-call(s32[24]{0:T(128)S(1)} %copy-done.40, bf16[1056,1536]{1,0:T(8,128)(2,1)S(1)} %copy-done.16, s32[3,352,1]{2,1,0:T(8,128)S(1)} %broadcast_select_fusion.key_ids, s32[3,1,352]{2,1,0:T(1,128)S(1)} %broadcast_select_fusion.1.query_ids, ...), custom_call_target="tpu_custom_call" | custom-call | flops 1 | bytes 1 | tf_op jit(solution)/shard_map/attend_back/pallas_call | solution.py:94
  206.0 1.7 collective-permute-done.34.rest_0_
  212.2 5.1 %qkv_grad.2.rest_0_ = bf16[1024,2048]{1,0:T(8,128)(2,1)S(1)} custom-call(s32[24]{0:T(128)S(1)} %copy-done.40, bf16[1056,1024]{1,0:T(8,128)(2,1)S(1)} %copy-done.14, bf16[1056,768]{1,0:T(8,128)(2,1)S(1)} %get-tuple-element.282.grad_ref.refs_1_, bf16[528,1024]{1,0:T(8,128)(2,1)S(1)} %get-tuple-element.270.own_ref, ...), custom_call_target="tpu_custom_call" | custom-call | flops 1 | bytes 1 | tf_op jit(solution)/shard_map/qkv_grad/pallas_call | solution.py:94
  217.3 9.8 %attend_back.3 = (bf16[1056,768]{1,0:T(8,128)(2,1)S(1)}, f32[2,1,384]{2,1,0:T(1,128)S(1)}) custom-call(s32[24]{0:T(128)S(1)} %copy-done.40, bf16[1056,1536]{1,0:T(8,128)(2,1)S(1)} %copy-done.16, s32[3,352,1]{2,1,0:T(8,128)S(1)} %broadcast_select_fusion.key_ids, s32[3,1,352]{2,1,0:T(1,128)S(1)} %broadcast_select_fusion.1.query_ids, ...), custom_call_target="tpu_custom_call" | custom-call | flops 1 | bytes 1 | tf_op jit(solution)/shard_map/attend_back/pallas_call | solution.py:94
  227.2 1.8 collective-permute-done.41
  232.7 5.1 %qkv_grad.3.ahead_ref.behind_ref.rest_0_ = bf16[1024,2048]{1,0:T(8,128)(2,1)S(1)} custom-call(s32[24]{0:T(128)S(1)} %copy-done.40, bf16[1056,1024]{1,0:T(8,128)(2,1)S(1)} %copy-done.14, bf16[1056,768]{1,0:T(8,128)(2,1)S(1)} %get-tuple-element.284.grad_ref.refs_0_, bf16[528,1024]{1,0:T(8,128)(2,1)S(1)} %get-tuple-element.270.own_ref, ...), custom_call_target="tpu_custom_call", output_to_operand_aliasing={{}: (7, {})} | custom-call | flops 1 | bytes 1 | tf_op jit(solution)/shard_map/qkv_grad/pallas_call | solution.py:94
  240.5 9.9 %collective-permute-done.43.rest_0_ = bf16[64,2048]{1,0:T(8,128)(2,1)S(1)} collective-permute-done((bf16[64,2048]{1,0:T(8,128)(2,1)S(1)}, bf16[64,2048]{1,0:T(8,128)(2,1)S(1)}, u32[]{:S(2)}, u32[]{:S(2)}) %collective-permute-start.43) | collective-permute-done | bytes 262176 | tf_op jit(solution)/shard_map/ppermute | solution.py:131
  252.1 2.2 add_convert_fusion.refs_0_.refs_3_
  257.1 12.0 %first_norm.1 = (bf16[528,1024]{1,0:T(8,128)(2,1)}, f32[8,1024]{1,0:T(8,128)}) custom-call(s32[24]{0:T(128)} %copy-done.39, bf16[1056,768]{1,0:T(8,128)(2,1)} %copy-done.20, bf16[1056,768]{1,0:T(8,128)(2,1)} %copy-done.19, bf16[1056,768]{1,0:T(8,128)(2,1)} %copy-done.65, bf16[1056,768]{1,0:T(8,128)(2,1)} %copy-done.64, bf16[2112,1024]{1,0:T(8,128)(2,1)} %copy-done.7, ...), custom_call_target="tpu_custom_call" | custom-call | flops 1 | bytes 1 | tf_op jit(solution)/shard_map/first_norm/pallas_call | solution.py:94
  277.0 6.6 %assemble.2 = bf16[2070,1024]{1,0:T(8,128)(2,1)} custom-call(s32[24]{0:T(128)} %copy-done.39, bf16[1056,1024]{1,0:T(8,128)(2,1)} %add_convert_fusion.refs_0_.refs_3_, bf16[1056,1024]{1,0:T(8,128)(2,1)} %collective-permute-done.50.refs_1_.refs_2_, bf16[1056,1024]{1,0:T(8,128)(2,1)} %collective-permute-done.50.refs_1_.refs_2_, ...), custom_call_target="tpu_custom_call" | custom-call | flops 1 | bytes 1 | tf_op jit(solution)/shard_map/assemble/pallas_call | solution.py:94
  283.6 2.7 collective-permute-done.51.rest_1_
  287.2 1.7 ring_add.11
  291.1 6.2 %collective-permute-done.57.refs_3_ = bf16[528,1024]{1,0:T(8,128)(2,1)} collective-permute-done((bf16[528,1024]{1,0:T(8,128)(2,1)}, bf16[528,1024]{1,0:T(8,128)(2,1)}, u32[]{:S(2)}, u32[]{:S(2)}) %collective-permute-start.57) | collective-permute-done | bytes 1081376 | tf_op jit(solution)/shard_map/ppermute | solution.py:228
  299.3 4.3 %collective-permute-done.54.got_ahead = bf16[128,2048]{1,0:T(8,128)(2,1)S(1)} collective-permute-done((bf16[128,2048]{1,0:T(8,128)(2,1)}, bf16[128,2048]{1,0:T(8,128)(2,1)S(1)}, u32[]{:S(2)}, u32[]{:S(2)}) %collective-permute-start.54) | collective-permute-done | bytes 524320 | tf_op jit(solution)/shard_map/ppermute | solution.py:131
  307.1 7.0 %assemble.3 = f32[2070,1024]{1,0:T(8,128)} custom-call(s32[24]{0:T(128)} %copy-done.39, bf16[528,1024]{1,0:T(8,128)(2,1)} %get-tuple-element.329.refs_0_, bf16[528,1024]{1,0:T(8,128)(2,1)} %collective-permute-done.56.refs_1_, bf16[528,1024]{1,0:T(8,128)(2,1)} %collective-permute-done.58.refs_2_, bf16[528,1024]{1,0:T(8,128)(2,1)} %collective-permute-done.57.refs_3_), custom_call_target="tpu_custom_call" | custom-call | flops 1 | bytes 1 | tf_op jit(solution)/shard_map/assemble/pallas_call | solution.py:94
  316.9 2.4 collective-permute-done.62
  (333 shorter events, 89.1 us)
Async XLA Ops:
  3.9 9.4 %collective-permute-start.1 = (bf16[128,1024]{1,0:T(8,128)(2,1)S(1)}, bf16[128,1024]{1,0:T(8,128)(2,1)S(1)}, u32[]{:S(2)}, u32[]{:S(2)}) collective-permute-start(bf16[128,1024]{1,0:T(8,128)(2,1)S(1)} %pad_maximum_fusion.6.rest_0_), channel_id=1, source_target_pairs={{4,12},{12,20},{20,28},{28,24},{24,16},{16,8},{8,0},{0,4},{5,13},{... | collective-permute-start | bytes 786440 | tf_op jit(solution)/shard_map/ppermute | solution.py:131
  7.2 9.1 %collective-permute-start = (bf16[144,1024]{1,0:T(8,128)(2,1)S(1)}, bf16[144,1024]{1,0:T(8,128)(2,1)S(1)}, u32[]{:S(2)}, u32[]{:S(2)}) collective-permute-start(bf16[144,1024]{1,0:T(8,128)(2,1)S(1)} %pad_maximum_fusion.5), channel_id=1, source_target_pairs={{0,2},{1,3},{2,0},{3,1},{4,6},{5,7},{6,4},{7,5},{8,10},{9,11},{10,... | collective-permute-start | bytes 884744 | tf_op jit(solution)/shard_map/ppermute | solution.py:228
  14.7 14.4 %collective-permute-start.5 = (bf16[256,1024]{1,0:T(8,128)(2,1)S(1)}, bf16[256,1024]{1,0:T(8,128)(2,1)S(1)}, u32[]{:S(2)}, u32[]{:S(2)}) collective-permute-start(bf16[256,1024]{1,0:T(8,128)(2,1)S(1)} %pad_maximum_fusion.1), channel_id=1, source_target_pairs={{0,2},{1,3},{2,0},{3,1},{4,6},{5,7},{6,4},{7,5},{8,10},{9,11},{10,... | collective-permute-start | bytes 1572872 | tf_op jit(solution)/shard_map/ppermute | solution.py:228
  16.3 12.8 %collective-permute-start.3 = (bf16[128,1024]{1,0:T(8,128)(2,1)S(1)}, bf16[128,1024]{1,0:T(8,128)(2,1)S(1)}, u32[]{:S(2)}, u32[]{:S(2)}) collective-permute-start(bf16[128,1024]{1,0:T(8,128)(2,1)S(1)} %collective-permute-done.1.rest_1_), channel_id=1, source_target_pairs={{4,12},{12,20},{20,28},{28,24},{24,16},{16,8},{8,0},{0,4},{5,13},{... | collective-permute-start | bytes 786440 | tf_op jit(solution)/shard_map/ppermute | solution.py:131
  17.9 11.2 %collective-permute-start.4 = (bf16[128,1024]{1,0:T(8,128)(2,1)S(1)}, bf16[128,1024]{1,0:T(8,128)(2,1)S(1)}, u32[]{:S(2)}, u32[]{:S(2)}) collective-permute-start(bf16[128,1024]{1,0:T(8,128)(2,1)S(1)} %collective-permute-done.2.rest_2_), channel_id=1, source_target_pairs={{4,0},{12,4},{20,12},{28,20},{24,28},{16,24},{8,16},{0,8},{5,1},{1... | collective-permute-start | bytes 786440 | tf_op jit(solution)/shard_map/ppermute | solution.py:134
  32.1 13.8 %collective-permute-start.10 = (bf16[256,1024]{1,0:T(8,128)(2,1)}, bf16[256,1024]{1,0:T(8,128)(2,1)S(1)}, u32[]{:S(2)}, u32[]{:S(2)}) collective-permute-start(bf16[256,1024]{1,0:T(8,128)(2,1)} %pad_maximum_fusion.2), channel_id=1, source_target_pairs={{0,2},{1,3},{2,0},{3,1},{4,6},{5,7},{6,4},{7,5},{8,10},{9,11},{10,... | collective-permute-start | bytes 1572872 | tf_op jit(solution)/shard_map/ppermute | solution.py:228
  41.9 19.4 %collective-permute-start.11 = (bf16[256,1024]{1,0:T(8,128)(2,1)}, bf16[256,1024]{1,0:T(8,128)(2,1)S(1)}, u32[]{:S(2)}, u32[]{:S(2)}) collective-permute-start(bf16[256,1024]{1,0:T(8,128)(2,1)} %pad_maximum_fusion.3), channel_id=1, source_target_pairs={{0,2},{1,3},{2,0},{3,1},{4,6},{5,7},{6,4},{7,5},{8,10},{9,11},{10,... | collective-permute-start | bytes 1572872 | tf_op jit(solution)/shard_map/ppermute | solution.py:228
  46.6 15.4 %collective-permute-start.13 = (bf16[128,2048]{1,0:T(8,128)(2,1)}, bf16[128,2048]{1,0:T(8,128)(2,1)}, u32[]{:S(2)}, u32[]{:S(2)}) collective-permute-start(bf16[128,2048]{1,0:T(8,128)(2,1)} %pad_maximum_fusion.4.rest_0_), channel_id=1, source_target_pairs={{4,12},{12,20},{20,28},{28,24},{24,16},{16,8},{8,0},{0,4},{5,13},{... | collective-permute-start | bytes 1572872 | tf_op jit(solution)/shard_map/ppermute | solution.py:131
  48.2 13.9 %collective-permute-start.14 = (bf16[128,2048]{1,0:T(8,128)(2,1)}, bf16[128,2048]{1,0:T(8,128)(2,1)}, u32[]{:S(2)}, u32[]{:S(2)}) collective-permute-start(bf16[128,2048]{1,0:T(8,128)(2,1)} %pad_maximum_fusion.4.rest_0_), channel_id=1, source_target_pairs={{4,0},{12,4},{20,12},{28,20},{24,28},{16,24},{8,16},{0,8},{5,1},{1... | collective-permute-start | bytes 1572872 | tf_op jit(solution)/shard_map/ppermute | solution.py:134
  49.3 11.2 %collective-permute-start.12 = (bf16[128,1024]{1,0:T(8,128)(2,1)S(1)}, bf16[128,1024]{1,0:T(8,128)(2,1)S(1)}, u32[]{:S(2)}, u32[]{:S(2)}) collective-permute-start(bf16[128,1024]{1,0:T(8,128)(2,1)S(1)} %pad_maximum_fusion.7), channel_id=1, source_target_pairs={{0,2},{1,3},{2,0},{3,1},{4,6},{5,7},{6,4},{7,5},{8,10},{9,11},{10,... | collective-permute-start | bytes 786440 | tf_op jit(solution)/shard_map/ppermute | solution.py:228
  62.1 11.3 %collective-permute-start.15 = (bf16[128,2048]{1,0:T(8,128)(2,1)}, bf16[128,2048]{1,0:T(8,128)(2,1)S(1)}, u32[]{:S(2)}, u32[]{:S(2)}) collective-permute-start(bf16[128,2048]{1,0:T(8,128)(2,1)} %collective-permute-done.13.rest_1_), channel_id=1, source_target_pairs={{4,12},{12,20},{20,28},{28,24},{24,16},{16,8},{8,0},{0,4},{5,13},{... | collective-permute-start | bytes 1572872 | tf_op jit(solution)/shard_map/ppermute | solution.py:131
  63.3 11.5 %collective-permute-start.16 = (bf16[128,2048]{1,0:T(8,128)(2,1)}, bf16[128,2048]{1,0:T(8,128)(2,1)S(1)}, u32[]{:S(2)}, u32[]{:S(2)}) collective-permute-start(bf16[128,2048]{1,0:T(8,128)(2,1)} %collective-permute-done.14.rest_2_), channel_id=1, source_target_pairs={{4,0},{12,4},{20,12},{28,20},{24,28},{16,24},{8,16},{0,8},{5,1},{1... | collective-permute-start | bytes 1572872 | tf_op jit(solution)/shard_map/ppermute | solution.py:134
  74.8 16.3 %collective-permute-start.19 = (bf16[1024,2048]{1,0:T(8,128)(2,1)S(1)}, bf16[1024,2048]{1,0:T(8,128)(2,1)S(1)}, u32[]{:S(2)}, u32[]{:S(2)}) collective-permute-start(bf16[1024,2048]{1,0:T(8,128)(2,1)S(1)} %get-tuple-element.221.rest_0_.rest_3_.refs_13_), channel_id=1, source_target_pairs={{0,1},{1,0},{2,3},{3,2},{4,5},{5,4},{6,7},{7,6},{8,9},{9,8},{10,11... | collective-permute-start | bytes 12582920 | tf_op jit(solution)/shard_map/ppermute | solution.py:232
  74.9 16.2 %collective-permute-start.17 = (bf16[128,2048]{1,0:T(8,128)(2,1)S(1)}, bf16[128,2048]{1,0:T(8,128)(2,1)S(1)}, u32[]{:S(2)}, u32[]{:S(2)}) collective-permute-start(bf16[128,2048]{1,0:T(8,128)(2,1)S(1)} %collective-permute-done.15.rest_3_), channel_id=1, source_target_pairs={{4,12},{12,20},{20,28},{28,24},{24,16},{16,8},{8,0},{0,4},{5,13},{... | collective-permute-start | bytes 1572872 | tf_op jit(solution)/shard_map/ppermute | solution.py:131
  76.5 14.5 %collective-permute-start.18 = (bf16[128,2048]{1,0:T(8,128)(2,1)S(1)}, bf16[128,2048]{1,0:T(8,128)(2,1)S(1)}, u32[]{:S(2)}, u32[]{:S(2)}) collective-permute-start(bf16[128,2048]{1,0:T(8,128)(2,1)S(1)} %collective-permute-done.16.rest_4_), channel_id=1, source_target_pairs={{4,0},{12,4},{20,12},{28,20},{24,28},{16,24},{8,16},{0,8},{5,1},{1... | collective-permute-start | bytes 1572872 | tf_op jit(solution)/shard_map/ppermute | solution.py:134
  101.3 26.5 %collective-permute-start.24 = (bf16[528,1024]{1,0:T(8,128)(2,1)}, bf16[528,1024]{1,0:T(8,128)(2,1)S(1)}, u32[]{:S(2)}, u32[]{:S(2)}) collective-permute-start(bf16[528,1024]{1,0:T(8,128)(2,1)} %get-tuple-element.228.rest_9_.rest_0_), channel_id=1, source_target_pairs={{0,2},{1,3},{2,0},{3,1},{4,6},{5,7},{6,4},{7,5},{8,10},{9,11},{10,... | collective-permute-start | bytes 3244040 | tf_op jit(solution)/shard_map/ppermute | solution.py:228
  142.6 35.5 %collective-permute-start.28 = (bf16[528,1024]{1,0:T(8,128)(2,1)S(1)}, bf16[528,1024]{1,0:T(8,128)(2,1)}, u32[]{:S(2)}, u32[]{:S(2)}) collective-permute-start(bf16[528,1024]{1,0:T(8,128)(2,1)S(1)} %copy-done.72), channel_id=1, source_target_pairs={{0,1},{1,0},{2,3},{3,2},{4,5},{5,4},{6,7},{7,6},{8,9},{9,8},{10,11... | collective-permute-start | bytes 3244040 | tf_op jit(solution)/shard_map/ppermute | solution.py:232
  142.9 38.2 %collective-permute-start.27 = (bf16[528,1024]{1,0:T(8,128)(2,1)}, bf16[528,1024]{1,0:T(8,128)(2,1)}, u32[]{:S(2)}, u32[]{:S(2)}) collective-permute-start(bf16[528,1024]{1,0:T(8,128)(2,1)} %get-tuple-element.243), channel_id=1, source_target_pairs={{0,1},{1,0},{2,3},{3,2},{4,5},{5,4},{6,7},{7,6},{8,9},{9,8},{10,11... | collective-permute-start | bytes 3244040 | tf_op jit(solution)/shard_map/ppermute | solution.py:232
  143.1 40.4 %collective-permute-start.29 = (bf16[528,1024]{1,0:T(8,128)(2,1)}, bf16[528,1024]{1,0:T(8,128)(2,1)}, u32[]{:S(2)}, u32[]{:S(2)}) collective-permute-start(bf16[528,1024]{1,0:T(8,128)(2,1)} %get-tuple-element.249), channel_id=1, source_target_pairs={{0,1},{1,0},{2,3},{3,2},{4,5},{5,4},{6,7},{7,6},{8,9},{9,8},{10,11... | collective-permute-start | bytes 3244040 | tf_op jit(solution)/shard_map/ppermute | solution.py:232
  157.6 26.2 %collective-permute-start.30 = (bf16[528,1024]{1,0:T(8,128)(2,1)}, bf16[528,1024]{1,0:T(8,128)(2,1)S(1)}, u32[]{:S(2)}, u32[]{:S(2)}) collective-permute-start(bf16[528,1024]{1,0:T(8,128)(2,1)} %get-tuple-element.250), channel_id=1, source_target_pairs={{0,2},{1,3},{2,0},{3,1},{4,6},{5,7},{6,4},{7,5},{8,10},{9,11},{10,... | collective-permute-start | bytes 3244040 | tf_op jit(solution)/shard_map/ppermute | solution.py:228
  177.0 14.4 %collective-permute-start.31 = (bf16[64,2048]{1,0:T(8,128)(2,1)S(1)}, bf16[64,2048]{1,0:T(8,128)(2,1)S(1)}, u32[]{:S(2)}, u32[]{:S(2)}) collective-permute-start(bf16[64,2048]{1,0:T(8,128)(2,1)S(1)} %get-tuple-element.253), channel_id=1, source_target_pairs={{4,12},{12,20},{20,28},{28,24},{24,16},{16,8},{8,0},{0,4},{5,13},{... | collective-permute-start | bytes 786440 | tf_op jit(solution)/shard_map/ppermute | solution.py:131
  178.0 13.4 %collective-permute-start.32 = (bf16[64,2048]{1,0:T(8,128)(2,1)S(1)}, bf16[64,2048]{1,0:T(8,128)(2,1)S(1)}, u32[]{:S(2)}, u32[]{:S(2)}) collective-permute-start(bf16[64,2048]{1,0:T(8,128)(2,1)S(1)} %get-tuple-element.255), channel_id=1, source_target_pairs={{4,0},{12,4},{20,12},{28,20},{24,28},{16,24},{8,16},{0,8},{5,1},{1... | collective-permute-start | bytes 786440 | tf_op jit(solution)/shard_map/ppermute | solution.py:134
  191.4 17.1 %collective-permute-start.36 = (bf16[528,1024]{1,0:T(8,128)(2,1)S(1)}, bf16[528,1024]{1,0:T(8,128)(2,1)S(1)}, u32[]{:S(2)}, u32[]{:S(2)}) collective-permute-start(bf16[528,1024]{1,0:T(8,128)(2,1)S(1)} %get-tuple-element.270.own_ref), channel_id=1, source_target_pairs={{0,1},{1,0},{2,3},{3,2},{4,5},{5,4},{6,7},{7,6},{8,9},{9,8},{10,11... | collective-permute-start | bytes 3244040 | tf_op jit(solution)/shard_map/ppermute | solution.py:232
  192.8 15.7 %collective-permute-start.39 = (bf16[264,1024]{1,0:T(8,128)(2,1)S(1)}, bf16[264,1024]{1,0:T(8,128)(2,1)S(1)}, u32[]{:S(2)}, u32[]{:S(2)}) collective-permute-start(bf16[264,1024]{1,0:T(8,128)(2,1)S(1)} %slice.179), channel_id=1, source_target_pairs={{0,2},{1,3},{2,0},{3,1},{4,6},{5,7},{6,4},{7,5},{8,10},{9,11},{10,... | collective-permute-start | bytes 1622024 | tf_op jit(solution)/shard_map/ppermute | solution.py:228
  194.2 13.6 %collective-permute-start.34 = (bf16[128,2048]{1,0:T(8,128)(2,1)S(1)}, bf16[128,2048]{1,0:T(8,128)(2,1)S(1)}, u32[]{:S(2)}, u32[]{:S(2)}) collective-permute-start(bf16[128,2048]{1,0:T(8,128)(2,1)S(1)} %get-tuple-element.264), channel_id=1, source_target_pairs={{4,12},{12,20},{20,28},{28,24},{24,16},{16,8},{8,0},{0,4},{5,13},{... | collective-permute-start | bytes 1572872 | tf_op jit(solution)/shard_map/ppermute | solution.py:131
  195.2 13.3 %collective-permute-start.35 = (bf16[128,2048]{1,0:T(8,128)(2,1)S(1)}, bf16[128,2048]{1,0:T(8,128)(2,1)S(1)}, u32[]{:S(2)}, u32[]{:S(2)}) collective-permute-start(bf16[128,2048]{1,0:T(8,128)(2,1)S(1)} %get-tuple-element.266), channel_id=1, source_target_pairs={{4,0},{12,4},{20,12},{28,20},{24,28},{16,24},{8,16},{0,8},{5,1},{1... | collective-permute-start | bytes 1572872 | tf_op jit(solution)/shard_map/ppermute | solution.py:134
  208.5 20.4 %collective-permute-start.40 = (bf16[1056,768]{1,0:T(8,128)(2,1)S(1)}, bf16[1056,768]{1,0:T(8,128)(2,1)S(1)}, u32[]{:S(2)}, u32[]{:S(2)}) collective-permute-start(bf16[1056,768]{1,0:T(8,128)(2,1)S(1)} %get-tuple-element.282.grad_ref.refs_1_), channel_id=1, source_target_pairs={{0,1},{1,0},{2,3},{3,2},{4,5},{5,4},{6,7},{7,6},{8,9},{9,8},{10,11... | collective-permute-start | bytes 4866056 | tf_op jit(solution)/shard_map/ppermute | solution.py:232
  208.6 20.4 %collective-permute-start.41 = (bf16[392,1024]{1,0:T(8,128)(2,1)S(1)}, bf16[392,1024]{1,0:T(8,128)(2,1)S(1)}, u32[]{:S(2)}, u32[]{:S(2)}) collective-permute-start(bf16[392,1024]{1,0:T(8,128)(2,1)S(1)} %pad_maximum_fusion), channel_id=1, source_target_pairs={{0,2},{1,3},{2,0},{3,1},{4,6},{5,7},{6,4},{7,5},{8,10},{9,11},{10,... | collective-permute-start | bytes 2408456 | tf_op jit(solution)/shard_map/ppermute | solution.py:228
  210.1 17.0 %collective-permute-start.37 = (bf16[128,2048]{1,0:T(8,128)(2,1)S(1)}, bf16[128,2048]{1,0:T(8,128)(2,1)S(1)}, u32[]{:S(2)}, u32[]{:S(2)}) collective-permute-start(bf16[128,2048]{1,0:T(8,128)(2,1)S(1)} %get-tuple-element.274), channel_id=1, source_target_pairs={{4,12},{12,20},{20,28},{28,24},{24,16},{16,8},{8,0},{0,4},{5,13},{... | collective-permute-start | bytes 1572872 | tf_op jit(solution)/shard_map/ppermute | solution.py:131
  211.5 15.6 %collective-permute-start.38 = (bf16[128,2048]{1,0:T(8,128)(2,1)S(1)}, bf16[128,2048]{1,0:T(8,128)(2,1)S(1)}, u32[]{:S(2)}, u32[]{:S(2)}) collective-permute-start(bf16[128,2048]{1,0:T(8,128)(2,1)S(1)} %get-tuple-element.276), channel_id=1, source_target_pairs={{4,0},{12,4},{20,12},{28,20},{24,28},{16,24},{8,16},{0,8},{5,1},{1... | collective-permute-start | bytes 1572872 | tf_op jit(solution)/shard_map/ppermute | solution.py:134
  229.0 9.4 %collective-permute-start.42 = (bf16[1056,768]{1,0:T(8,128)(2,1)S(1)}, bf16[1056,768]{1,0:T(8,128)(2,1)S(1)}, u32[]{:S(2)}, u32[]{:S(2)}) collective-permute-start(bf16[1056,768]{1,0:T(8,128)(2,1)S(1)} %get-tuple-element.284.grad_ref.refs_0_), channel_id=1, source_target_pairs={{0,1},{1,0},{2,3},{3,2},{4,5},{5,4},{6,7},{7,6},{8,9},{9,8},{10,11... | collective-permute-start | bytes 4866056 | tf_op jit(solution)/shard_map/ppermute | solution.py:232
  229.0 23.1 %collective-permute-start.47 = (bf16[400,1024]{1,0:T(8,128)(2,1)S(1)}, bf16[400,1024]{1,0:T(8,128)(2,1)S(1)}, u32[]{:S(2)}, u32[]{:S(2)}) collective-permute-start(bf16[400,1024]{1,0:T(8,128)(2,1)S(1)} %slice.180), channel_id=1, source_target_pairs={{0,2},{1,3},{2,0},{3,1},{4,6},{5,7},{6,4},{7,5},{8,10},{9,11},{10,... | collective-permute-start | bytes 2457608 | tf_op jit(solution)/shard_map/ppermute | solution.py:228
  230.6 20.8 %collective-permute-start.45 = (bf16[128,2048]{1,0:T(8,128)(2,1)S(1)}, bf16[128,2048]{1,0:T(8,128)(2,1)S(1)}, u32[]{:S(2)}, u32[]{:S(2)}) collective-permute-start(bf16[128,2048]{1,0:T(8,128)(2,1)S(1)} %get-tuple-element.290), channel_id=1, source_target_pairs={{4,12},{12,20},{20,28},{28,24},{24,16},{16,8},{8,0},{0,4},{5,13},{... | collective-permute-start | bytes 1572872 | tf_op jit(solution)/shard_map/ppermute | solution.py:131
  232.0 19.4 %collective-permute-start.46 = (bf16[128,2048]{1,0:T(8,128)(2,1)S(1)}, bf16[128,2048]{1,0:T(8,128)(2,1)S(1)}, u32[]{:S(2)}, u32[]{:S(2)}) collective-permute-start(bf16[128,2048]{1,0:T(8,128)(2,1)S(1)} %get-tuple-element.292), channel_id=1, source_target_pairs={{4,0},{12,4},{20,12},{28,20},{24,28},{16,24},{8,16},{0,8},{5,1},{1... | collective-permute-start | bytes 1572872 | tf_op jit(solution)/shard_map/ppermute | solution.py:134
  238.4 11.9 %collective-permute-start.43 = (bf16[64,2048]{1,0:T(8,128)(2,1)S(1)}, bf16[64,2048]{1,0:T(8,128)(2,1)S(1)}, u32[]{:S(2)}, u32[]{:S(2)}) collective-permute-start(bf16[64,2048]{1,0:T(8,128)(2,1)S(1)} %get-tuple-element.285), channel_id=1, source_target_pairs={{4,12},{12,20},{20,28},{28,24},{24,16},{16,8},{8,0},{0,4},{5,13},{... | collective-permute-start | bytes 786440 | tf_op jit(solution)/shard_map/ppermute | solution.py:131
  239.8 11.6 %collective-permute-start.44 = (bf16[64,2048]{1,0:T(8,128)(2,1)S(1)}, bf16[64,2048]{1,0:T(8,128)(2,1)S(1)}, u32[]{:S(2)}, u32[]{:S(2)}) collective-permute-start(bf16[64,2048]{1,0:T(8,128)(2,1)S(1)} %get-tuple-element.287), channel_id=1, source_target_pairs={{4,0},{12,4},{20,12},{28,20},{24,28},{16,24},{8,16},{0,8},{5,1},{1... | collective-permute-start | bytes 786440 | tf_op jit(solution)/shard_map/ppermute | solution.py:134
  255.0 14.2 %collective-permute-start.48 = (bf16[128,2048]{1,0:T(8,128)(2,1)S(1)}, bf16[128,2048]{1,0:T(8,128)(2,1)S(1)}, u32[]{:S(2)}, u32[]{:S(2)}) collective-permute-start(bf16[128,2048]{1,0:T(8,128)(2,1)S(1)} %get-tuple-element.308), channel_id=1, source_target_pairs={{4,12},{12,20},{20,28},{28,24},{24,16},{16,8},{8,0},{0,4},{5,13},{... | collective-permute-start | bytes 1572872 | tf_op jit(solution)/shard_map/ppermute | solution.py:131
  256.1 13.1 %collective-permute-start.49 = (bf16[128,2048]{1,0:T(8,128)(2,1)S(1)}, bf16[128,2048]{1,0:T(8,128)(2,1)S(1)}, u32[]{:S(2)}, u32[]{:S(2)}) collective-permute-start(bf16[128,2048]{1,0:T(8,128)(2,1)S(1)} %get-tuple-element.310), channel_id=1, source_target_pairs={{4,0},{12,4},{20,12},{28,20},{24,28},{16,24},{8,16},{0,8},{5,1},{1... | collective-permute-start | bytes 1572872 | tf_op jit(solution)/shard_map/ppermute | solution.py:134
  270.7 26.6 %collective-permute-start.57 = (bf16[528,1024]{1,0:T(8,128)(2,1)}, bf16[528,1024]{1,0:T(8,128)(2,1)}, u32[]{:S(2)}, u32[]{:S(2)}) collective-permute-start(bf16[528,1024]{1,0:T(8,128)(2,1)} %get-tuple-element.329.refs_0_), channel_id=1, source_target_pairs={{0,2},{1,3},{2,0},{3,1},{4,6},{5,7},{6,4},{7,5},{8,10},{9,11},{10,... | collective-permute-start | bytes 3244040 | tf_op jit(solution)/shard_map/ppermute | solution.py:228
  272.1 14.3 %collective-permute-start.51 = (bf16[128,2048]{1,0:T(8,128)(2,1)}, bf16[128,2048]{1,0:T(8,128)(2,1)S(1)}, u32[]{:S(2)}, u32[]{:S(2)}) collective-permute-start(bf16[128,2048]{1,0:T(8,128)(2,1)} %get-tuple-element.315), channel_id=1, source_target_pairs={{4,12},{12,20},{20,28},{28,24},{24,16},{16,8},{8,0},{0,4},{5,13},{... | collective-permute-start | bytes 1572872 | tf_op jit(solution)/shard_map/ppermute | solution.py:131
  273.1 14.1 %collective-permute-start.52 = (bf16[128,2048]{1,0:T(8,128)(2,1)S(1)}, bf16[128,2048]{1,0:T(8,128)(2,1)S(1)}, u32[]{:S(2)}, u32[]{:S(2)}) collective-permute-start(bf16[128,2048]{1,0:T(8,128)(2,1)S(1)} %get-tuple-element.317), channel_id=1, source_target_pairs={{4,0},{12,4},{20,12},{28,20},{24,28},{16,24},{8,16},{0,8},{5,1},{1... | collective-permute-start | bytes 1572872 | tf_op jit(solution)/shard_map/ppermute | solution.py:134
  274.1 14.8 %collective-permute-start.53 = (f32[8,1024]{1,0:T(8,128)S(1)}, f32[8,1024]{1,0:T(8,128)S(1)}, u32[]{:S(2)}, u32[]{:S(2)}) collective-permute-start(f32[8,1024]{1,0:T(8,128)S(1)} %copy-done.69), channel_id=1, source_target_pairs={{0,4},{4,0},{8,12},{12,8},{16,20},{20,16},{24,28},{28,24},{1,5},{5... | collective-permute-start | bytes 98312 | tf_op jit(solution)/shard_map/ppermute | solution.py:1191
  288.9 8.9 %collective-permute-start.59 = (f32[6,1024]{1,0:T(8,128)S(1)}, f32[6,1024]{1,0:T(8,128)S(1)}, u32[]{:S(2)}, u32[]{:S(2)}) collective-permute-start(f32[6,1024]{1,0:T(8,128)S(1)} %bitcast.72), channel_id=1, source_target_pairs={{0,1},{1,0},{2,3},{3,2},{4,5},{5,4},{6,7},{7,6},{8,9},{9,8},{10,11... | collective-permute-start | bytes 73736 | tf_op jit(solution)/shard_map/ppermute | solution.py:232
  289.0 14.5 %collective-permute-start.54 = (bf16[128,2048]{1,0:T(8,128)(2,1)}, bf16[128,2048]{1,0:T(8,128)(2,1)S(1)}, u32[]{:S(2)}, u32[]{:S(2)}) collective-permute-start(bf16[128,2048]{1,0:T(8,128)(2,1)} %get-tuple-element.324), channel_id=1, source_target_pairs={{4,12},{12,20},{20,28},{28,24},{24,16},{16,8},{8,0},{0,4},{5,13},{... | collective-permute-start | bytes 1572872 | tf_op jit(solution)/shard_map/ppermute | solution.py:131
  289.6 14.2 %collective-permute-start.55 = (bf16[128,2048]{1,0:T(8,128)(2,1)}, bf16[128,2048]{1,0:T(8,128)(2,1)S(1)}, u32[]{:S(2)}, u32[]{:S(2)}) collective-permute-start(bf16[128,2048]{1,0:T(8,128)(2,1)} %get-tuple-element.326), channel_id=1, source_target_pairs={{4,0},{12,4},{20,12},{28,20},{24,28},{16,24},{8,16},{0,8},{5,1},{1... | collective-permute-start | bytes 1572872 | tf_op jit(solution)/shard_map/ppermute | solution.py:134
  297.3 9.8 %collective-permute-start.56 = (bf16[528,1024]{1,0:T(8,128)(2,1)}, bf16[528,1024]{1,0:T(8,128)(2,1)}, u32[]{:S(2)}, u32[]{:S(2)}) collective-permute-start(bf16[528,1024]{1,0:T(8,128)(2,1)} %get-tuple-element.329.refs_0_), channel_id=1, source_target_pairs={{0,1},{1,0},{2,3},{3,2},{4,5},{5,4},{6,7},{7,6},{8,9},{9,8},{10,11... | collective-permute-start | bytes 3244040 | tf_op jit(solution)/shard_map/ppermute | solution.py:232
  297.3 9.8 %collective-permute-start.58 = (bf16[528,1024]{1,0:T(8,128)(2,1)}, bf16[528,1024]{1,0:T(8,128)(2,1)}, u32[]{:S(2)}, u32[]{:S(2)}) collective-permute-start(bf16[528,1024]{1,0:T(8,128)(2,1)} %collective-permute-done.57.refs_3_), channel_id=1, source_target_pairs={{0,1},{1,0},{2,3},{3,2},{4,5},{5,4},{6,7},{7,6},{8,9},{9,8},{10,11... | collective-permute-start | bytes 3244040 | tf_op jit(solution)/shard_map/ppermute | solution.py:232
  304.6 9.4 %collective-permute-start.63 = (bf16[128,1024]{1,0:T(8,128)(2,1)S(1)}, bf16[128,1024]{1,0:T(8,128)(2,1)S(1)}, u32[]{:S(2)}, u32[]{:S(2)}) collective-permute-start(bf16[128,1024]{1,0:T(8,128)(2,1)S(1)} %slice.163), channel_id=1, source_target_pairs={{0,2},{1,3},{2,0},{3,1},{4,6},{5,7},{6,4},{7,5},{8,10},{9,11},{10,... | collective-permute-start | bytes 786440 | tf_op jit(solution)/shard_map/ppermute | solution.py:228
  (93 other events, 862.3 us)

commit v5 on v4

--- a/solution.py
+++ b/solution.py
@@ -954,15 +954,19 @@
     first = feed(near)
     for step in range(1, chips):
         seconds[(step, 1)] = partner(order.after(seconds[(step, 0)]), chips)
+    own = feed(far_own)
     other = feed(far_other)
-    own = feed(far_own, [partner(back, chips) for back in other[2]])
+    back_sums = [
+        (mine.astype(f32) + partner(got, chips).astype(f32)).astype(bf16)
+        for mine, got in zip(own[2], other[2])
+    ]
     feeds = [first, other, own]
 
     def along_x(own, sums):
         terms = [own[0], partner(own[1], chips)]
         return terms + [across(value, chips - 1 - i, chips) for i, value in enumerate(sums)]
 
-    back_terms = along_x(first[2], own[2])
+    back_terms = along_x(first[2], back_sums)
     span = 2 * CHUNK
     total_rows = len(keys) * half
     kernel = call(

time: 321 us -> 319 us (level)
    unnamed x159 -> x157, local copies, waits for them, and re-layouts: 30.7 us -> 30.7 us
  transfers between devices with their start and end apart: 64 -> 64, of which waited for: 26 -> 24; matrix products, arithmetic and copies ran while one was open for 5% -> 6% of each run, Pallas kernels for 45% -> 45%
where the time goes in v5:
time: 319 us; the launch traced here: 318 us
  Pallas kernels  157 us (49%)
  waiting for transfers between devices  54.3 us (17%)
  starting transfers between devices  53.7 us (17%)
  local copies, waits for them, and re-layouts  37.3 us (12%)
  other arithmetic  14.4 us (5%)
    pallas_call x28, Pallas kernels, run(): out = kernel(tie(self.info, self.now, wait, self.hold), *values)  157 us
    unnamed x157, local copies, waits for them, and re-layouts  30.7 us
    ppermute x16, waiting for transfers between devices, send_ahead(): return lax.ppermute(value, 'dp', self.ahead)  23.5 us
    ppermute x16, starting transfers between devices, send_ahead(): return lax.ppermute(value, 'dp', self.ahead)  23.4 us
    ppermute x13, waiting for transfers between devices, across(): return lax.ppermute(value, 'mp', pairs)  13.6 us
    ppermute x13, starting transfers between devices, across(): return lax.ppermute(value, 'mp', pairs)  13.5 us
    ppermute x16, starting transfers between devices, send_behind(): return lax.ppermute(value, 'dp', self.behind)  10.7 us
    ppermute x16, waiting for transfers between devices, send_behind(): return lax.ppermute(value, 'dp', self.behind)  8.88 us
  transfers between devices with their start and end apart: 64, of which 24 were waited for; matrix products, arithmetic and copies ran while one was open for 6% of the time, Pallas kernels for 45%

profile of v5, /device:TPU:0, one launch (start us, length us, event | category | flops | bytes accessed | tf_op | source)
XLA Modules:
  0.0 318.4 jit_solution(1953916192287334426)
XLA Ops:
  3.9 3.0 collective-permute-start.1
  7.2 1.9 collective-permute-start
  9.1 4.2 %collective-permute-done.1.rest_1_ = bf16[128,1024]{1,0:T(8,128)(2,1)S(1)} collective-permute-done((bf16[128,1024]{1,0:T(8,128)(2,1)S(1)}, bf16[128,1024]{1,0:T(8,128)(2,1)S(1)}, u32[]{:S(2)}, u32[]{:S(2)}) %collective-permute-start.1) | collective-permute-done | bytes 262176 | tf_op jit(solution)/shard_map/ppermute | solution.py:131
  18.3 2.2 copy-done.21
  20.5 3.0 pad.83.x_ref.refs_4_
  23.5 2.1 first_low.1.x_ref.first_ref
  25.7 2.1 copy-done.7
  34.6 1.9 copy.90
  39.2 1.8 pad_maximum_fusion.4.rest_0_
  43.8 2.1 collective-permute-done.10.rest_11_
  53.2 2.2 copy-done.22
  55.4 3.0 pad.84.cot_ref
  58.5 2.0 copy-done.6
  67.5 5.5 %qkv.1 = (bf16[1056,1536]{1,0:T(8,128)(2,1)S(1)}, bf16[1024,2048]{1,0:T(8,128)(2,1)S(1)}) custom-call(s32[24]{0:T(128)S(1)} %concatenate.49.info, bf16[1056,1024]{1,0:T(8,128)(2,1)S(1)} %copy-done.13, f32[1,1536]{1,0:T(1,128)S(1)} %pad_maximum_fusion.10.bias_ref, bf16[128,1024]{1,0:T(8,128)(2,1)S(1)} %pad_maximum_fusion.6.rest_0_, ...), custom_call_target="tpu_custom_call" | custom-call | flops 1 | bytes 1 | tf_op jit(solution)/shard_map/qkv/pallas_call | solution.py:94
  77.0 12.4 %attend.1 = (bf16[1056,512]{1,0:T(8,128)(2,1)S(1)}, f32[3,4,2,352]{3,2,1,0:T(2,128)S(1)}) custom-call(s32[24]{0:T(128)S(1)} %concatenate.49.info, bf16[1056,1536]{1,0:T(8,128)(2,1)S(1)} %get-tuple-element.208.qkv_ref, s32[3,352,1]{2,1,0:T(8,128)S(1)} %broadcast_select_fusion.key_ids, s32[3,1,352]{2,1,0:T(1,128)S(1)} %broadcast_select_fusion.1.query_ids), custom_call_target="tpu_custom_call" | custom-call | flops 1 | bytes 1 | tf_op jit(solution)/shard_map/attend/pallas_call | solution.py:94
  89.4 1.7 copy-done.15
  94.0 4.3 %proj_norm.1 = (f32[528,1024]{1,0:T(8,128)S(1)}, bf16[528,1024]{1,0:T(8,128)(2,1)}) custom-call(s32[24]{0:T(128)S(1)} %concatenate.49.info, bf16[1056,512]{1,0:T(8,128)(2,1)S(1)} %get-tuple-element.222.own_ref.att_own.att_got, bf16[1056,512]{1,0:T(8,128)(2,1)S(1)} %collective-permute-done.20.got_ref, bf16[2112,1024]{1,0:T(8,128)(2,1)S(1)} %bitcast.57, ...), custom_call_target="tpu_custom_call" | custom-call | flops 1 | bytes 1 | tf_op jit(solution)/shard_map/proj_norm/pallas_call | solution.py:94
  101.3 2.9 collective-permute-done.23.rest_10_.rest_1_
  105.2 19.3 %mlp.3 = (bf16[1056,1024]{1,0:T(8,128)(2,1)}, bf16[1056,1024]{1,0:T(8,128)(2,1)}, bf16[528,1024]{1,0:T(8,128)(2,1)}, bf16[528,1024]{1,0:T(8,128)(2,1)}, bf16[528...) custom-call(s32[24]{0:T(128)} %copy-done.39, bf16[2112,1024]{1,0:T(8,128)(2,1)} %copy-done.6, ...), custom_call_target="tpu_custom_call" | custom-call | flops 1 | bytes 1 | tf_op jit(solution)/shard_map/mlp/pallas_call | solution.py:94
  124.5 3.2 %collective-permute-done.24.rest_9_.rest_3_ = bf16[528,1024]{1,0:T(8,128)(2,1)S(1)} collective-permute-done((bf16[528,1024]{1,0:T(8,128)(2,1)}, bf16[528,1024]{1,0:T(8,128)(2,1)S(1)}, u32[]{:S(2)}, u32[]{:S(2)}) %collective-permute-start.24) | collective-permute-done | bytes 1081376 | tf_op jit(solution)/shard_map/ppermute | solution.py:228
  128.7 10.9 %mlp.4 = (bf16[528,1024]{1,0:T(8,128)(2,1)}, bf16[528,1024]{1,0:T(8,128)(2,1)}, bf16[528,1024]{1,0:T(8,128)(2,1)}, bf16[528,1024]{1,0:T(8,128)(2,1)}, f32[1,1024]{1,0:T(1,128)}) custom-call(s32[24]{0:T(128)} %copy-done.39, bf16[2112,1024]{1,0:T(8,128)(2,1)} %copy-done.6, f32[1,1024]{1,0:T(1,128)} %bitcast.75, bf16[128,2048]{1,0:T(8,128)(2,1)} %pad_maximum_fusion.4.rest_0_, ...), custom_call_target="tpu_custom_call" | custom-call | flops 1 | bytes 1 | tf_op jit(solution)/shard_map/mlp/pallas_call | solution.py:94
  140.6 11.0 %mlp.5 = (bf16[528,1024]{1,0:T(8,128)(2,1)}, bf16[528,1024]{1,0:T(8,128)(2,1)}, bf16[528,1024]{1,0:T(8,128)(2,1)}, bf16[528,1024]{1,0:T(8,128)(2,1)}, f32[1,1024]{1,0:T(1,128)}) custom-call(s32[24]{0:T(128)} %copy-done.39, bf16[2112,1024]{1,0:T(8,128)(2,1)} %copy-done.6, f32[1,1024]{1,0:T(1,128)} %bitcast.76, bf16[128,2048]{1,0:T(8,128)(2,1)} %pad_maximum_fusion.4.rest_0_, ...), custom_call_target="tpu_custom_call" | custom-call | flops 1 | bytes 1 | tf_op jit(solution)/shard_map/mlp/pallas_call | solution.py:94
  152.7 2.6 collective-permute-done.29
  157.0 16.2 %mlp_grad.1.ahead_ref.behind_ref.rest_0_ = bf16[1024,2048]{1,0:T(8,128)(2,1)} custom-call(s32[24]{0:T(128)} %copy-done.39, bf16[2112,1024]{1,0:T(8,128)(2,1)} %copy-done.6, bf16[528,1024]{1,0:T(8,128)(2,1)} %get-tuple-element.228.rest_9_.rest_0_, bf16[528,1024]{1,0:T(8,128)(2,1)} %copy-done.59, bf16[528,1024]{1,0:T(8,128)(2,1)} %copy-done.61, ...), custom_call_target="tpu_custom_call" | custom-call | flops 1 | bytes 1 | tf_op jit(solution)/shard_map/mlp_grad/pallas_call | solution.py:94
  173.2 2.2 copy-done.4
  178.1 2.3 add_convert_fusion.2
  180.5 2.3 add_convert_fusion.3
  182.9 4.9 %residual_back.1 = (f32[528,1024]{1,0:T(8,128)S(1)}, bf16[528,1024]{1,0:T(8,128)(2,1)S(1)}, bf16[528,512]{1,0:T(8,128)(2,1)S(1)}, bf16[528,512]{1,0:T(8,128)(2,1)S(1)}, f32[8,1024]{1,0:T(8,128)S(1)}) custom-call(s32[24]{0:T(128)S(1)} %copy-done.40, f32[528,1024]{1,0:T(8,128)S(1)} %copy-done.18, bf16[2112,1024]{1,0:T(8,128)(2,1)S(1)} %bitcast.55, ...), custom_call_target="tpu_custom_call" | custom-call | flops 1 | bytes 1 | tf_op jit(solution)/shard_map/residual_back/pallas_call | solution.py:94
  190.6 1.8 collective-permute-start.39
  194.4 9.8 %attend_back.2 = (bf16[1056,768]{1,0:T(8,128)(2,1)S(1)}, f32[2,1,384]{2,1,0:T(1,128)S(1)}) custom-call(s32[24]{0:T(128)S(1)} %copy-done.40, bf16[1056,1536]{1,0:T(8,128)(2,1)S(1)} %copy-done.16, s32[3,352,1]{2,1,0:T(8,128)S(1)} %broadcast_select_fusion.key_ids, s32[3,1,352]{2,1,0:T(1,128)S(1)} %broadcast_select_fusion.1.query_ids, ...), custom_call_target="tpu_custom_call" | custom-call | flops 1 | bytes 1 | tf_op jit(solution)/shard_map/attend_back/pallas_call | solution.py:94
  204.2 1.7 collective-permute-done.34.rest_0_
  208.0 1.7 collective-permute-start.37
  210.1 5.1 %qkv_grad.2.rest_0_ = bf16[1024,2048]{1,0:T(8,128)(2,1)S(1)} custom-call(s32[24]{0:T(128)S(1)} %copy-done.40, bf16[1056,1024]{1,0:T(8,128)(2,1)S(1)} %copy-done.14, bf16[1056,768]{1,0:T(8,128)(2,1)S(1)} %get-tuple-element.282.grad_ref.refs_1_, bf16[528,1024]{1,0:T(8,128)(2,1)S(1)} %get-tuple-element.270.own_ref, ...), custom_call_target="tpu_custom_call" | custom-call | flops 1 | bytes 1 | tf_op jit(solution)/shard_map/qkv_grad/pallas_call | solution.py:94
  215.2 9.8 %attend_back.3 = (bf16[1056,768]{1,0:T(8,128)(2,1)S(1)}, f32[2,1,384]{2,1,0:T(1,128)S(1)}) custom-call(s32[24]{0:T(128)S(1)} %copy-done.40, bf16[1056,1536]{1,0:T(8,128)(2,1)S(1)} %copy-done.16, s32[3,352,1]{2,1,0:T(8,128)S(1)} %broadcast_select_fusion.key_ids, s32[3,1,352]{2,1,0:T(1,128)S(1)} %broadcast_select_fusion.1.query_ids, ...), custom_call_target="tpu_custom_call" | custom-call | flops 1 | bytes 1 | tf_op jit(solution)/shard_map/attend_back/pallas_call | solution.py:94
  225.1 2.1 collective-permute-done.41
  228.5 1.7 collective-permute-start.45
  230.6 5.1 %qkv_grad.3.ahead_ref.behind_ref.rest_0_ = bf16[1024,2048]{1,0:T(8,128)(2,1)S(1)} custom-call(s32[24]{0:T(128)S(1)} %copy-done.40, bf16[1056,1024]{1,0:T(8,128)(2,1)S(1)} %copy-done.14, bf16[1056,768]{1,0:T(8,128)(2,1)S(1)} %get-tuple-element.284.grad_ref.refs_0_, bf16[528,1024]{1,0:T(8,128)(2,1)S(1)} %get-tuple-element.270.own_ref, ...), custom_call_target="tpu_custom_call", output_to_operand_aliasing={{}: (7, {})} | custom-call | flops 1 | bytes 1 | tf_op jit(solution)/shard_map/qkv_grad/pallas_call | solution.py:94
  236.3 1.7 collective-permute-start.43
  238.4 9.9 %collective-permute-done.43.rest_0_ = bf16[64,2048]{1,0:T(8,128)(2,1)S(1)} collective-permute-done((bf16[64,2048]{1,0:T(8,128)(2,1)S(1)}, bf16[64,2048]{1,0:T(8,128)(2,1)S(1)}, u32[]{:S(2)}, u32[]{:S(2)}) %collective-permute-start.43) | collective-permute-done | bytes 262176 | tf_op jit(solution)/shard_map/ppermute | solution.py:131
  250.3 2.2 add_convert_fusion.refs_0_.refs_3_
  255.3 12.0 %first_norm.1 = (bf16[528,1024]{1,0:T(8,128)(2,1)}, f32[8,1024]{1,0:T(8,128)}) custom-call(s32[24]{0:T(128)} %copy-done.39, bf16[1056,768]{1,0:T(8,128)(2,1)} %copy-done.20, bf16[1056,768]{1,0:T(8,128)(2,1)} %copy-done.19, bf16[1056,768]{1,0:T(8,128)(2,1)} %copy-done.65, bf16[1056,768]{1,0:T(8,128)(2,1)} %copy-done.64, bf16[2112,1024]{1,0:T(8,128)(2,1)} %copy-done.7, ...), custom_call_target="tpu_custom_call" | custom-call | flops 1 | bytes 1 | tf_op jit(solution)/shard_map/first_norm/pallas_call | solution.py:94
  275.2 6.6 %assemble.2 = bf16[2070,1024]{1,0:T(8,128)(2,1)} custom-call(s32[24]{0:T(128)} %copy-done.39, bf16[1056,1024]{1,0:T(8,128)(2,1)} %add_convert_fusion.refs_0_.refs_3_, bf16[1056,1024]{1,0:T(8,128)(2,1)} %collective-permute-done.50.refs_1_.refs_2_, bf16[1056,1024]{1,0:T(8,128)(2,1)} %collective-permute-done.50.refs_1_.refs_2_, ...), custom_call_target="tpu_custom_call" | custom-call | flops 1 | bytes 1 | tf_op jit(solution)/shard_map/assemble/pallas_call | solution.py:94
  281.8 2.7 collective-permute-done.51.rest_1_
  285.4 1.7 ring_add.11
  289.3 6.2 %collective-permute-done.57.refs_3_ = bf16[528,1024]{1,0:T(8,128)(2,1)} collective-permute-done((bf16[528,1024]{1,0:T(8,128)(2,1)}, bf16[528,1024]{1,0:T(8,128)(2,1)}, u32[]{:S(2)}, u32[]{:S(2)}) %collective-permute-start.57) | collective-permute-done | bytes 1081376 | tf_op jit(solution)/shard_map/ppermute | solution.py:228
  297.5 4.3 %collective-permute-done.54.got_ahead = bf16[128,2048]{1,0:T(8,128)(2,1)S(1)} collective-permute-done((bf16[128,2048]{1,0:T(8,128)(2,1)}, bf16[128,2048]{1,0:T(8,128)(2,1)S(1)}, u32[]{:S(2)}, u32[]{:S(2)}) %collective-permute-start.54) | collective-permute-done | bytes 524320 | tf_op jit(solution)/shard_map/ppermute | solution.py:131
  304.9 7.0 %assemble.3 = f32[2070,1024]{1,0:T(8,128)} custom-call(s32[24]{0:T(128)} %copy-done.39, bf16[528,1024]{1,0:T(8,128)(2,1)} %get-tuple-element.329.refs_0_, bf16[528,1024]{1,0:T(8,128)(2,1)} %collective-permute-done.56.refs_1_, bf16[528,1024]{1,0:T(8,128)(2,1)} %collective-permute-done.58.refs_2_, bf16[528,1024]{1,0:T(8,128)(2,1)} %collective-permute-done.57.refs_3_), custom_call_target="tpu_custom_call" | custom-call | flops 1 | bytes 1 | tf_op jit(solution)/shard_map/assemble/pallas_call | solution.py:94
  314.9 2.2 collective-permute-done.62
  (332 shorter events, 88.1 us)
Async XLA Ops:
  3.9 9.4 %collective-permute-start.1 = (bf16[128,1024]{1,0:T(8,128)(2,1)S(1)}, bf16[128,1024]{1,0:T(8,128)(2,1)S(1)}, u32[]{:S(2)}, u32[]{:S(2)}) collective-permute-start(bf16[128,1024]{1,0:T(8,128)(2,1)S(1)} %pad_maximum_fusion.6.rest_0_), channel_id=1, source_target_pairs={{4,12},{12,20},{20,28},{28,24},{24,16},{16,8},{8,0},{0,4},{5,13},{... | collective-permute-start | bytes 786440 | tf_op jit(solution)/shard_map/ppermute | solution.py:131
  7.2 9.1 %collective-permute-start = (bf16[144,1024]{1,0:T(8,128)(2,1)S(1)}, bf16[144,1024]{1,0:T(8,128)(2,1)S(1)}, u32[]{:S(2)}, u32[]{:S(2)}) collective-permute-start(bf16[144,1024]{1,0:T(8,128)(2,1)S(1)} %pad_maximum_fusion.5), channel_id=1, source_target_pairs={{0,2},{1,3},{2,0},{3,1},{4,6},{5,7},{6,4},{7,5},{8,10},{9,11},{10,... | collective-permute-start | bytes 884744 | tf_op jit(solution)/shard_map/ppermute | solution.py:228
  14.7 14.4 %collective-permute-start.5 = (bf16[256,1024]{1,0:T(8,128)(2,1)S(1)}, bf16[256,1024]{1,0:T(8,128)(2,1)S(1)}, u32[]{:S(2)}, u32[]{:S(2)}) collective-permute-start(bf16[256,1024]{1,0:T(8,128)(2,1)S(1)} %pad_maximum_fusion.1), channel_id=1, source_target_pairs={{0,2},{1,3},{2,0},{3,1},{4,6},{5,7},{6,4},{7,5},{8,10},{9,11},{10,... | collective-permute-start | bytes 1572872 | tf_op jit(solution)/shard_map/ppermute | solution.py:228
  16.3 12.8 %collective-permute-start.3 = (bf16[128,1024]{1,0:T(8,128)(2,1)S(1)}, bf16[128,1024]{1,0:T(8,128)(2,1)S(1)}, u32[]{:S(2)}, u32[]{:S(2)}) collective-permute-start(bf16[128,1024]{1,0:T(8,128)(2,1)S(1)} %collective-permute-done.1.rest_1_), channel_id=1, source_target_pairs={{4,12},{12,20},{20,28},{28,24},{24,16},{16,8},{8,0},{0,4},{5,13},{... | collective-permute-start | bytes 786440 | tf_op jit(solution)/shard_map/ppermute | solution.py:131
  17.9 11.2 %collective-permute-start.4 = (bf16[128,1024]{1,0:T(8,128)(2,1)S(1)}, bf16[128,1024]{1,0:T(8,128)(2,1)S(1)}, u32[]{:S(2)}, u32[]{:S(2)}) collective-permute-start(bf16[128,1024]{1,0:T(8,128)(2,1)S(1)} %collective-permute-done.2.rest_2_), channel_id=1, source_target_pairs={{4,0},{12,4},{20,12},{28,20},{24,28},{16,24},{8,16},{0,8},{5,1},{1... | collective-permute-start | bytes 786440 | tf_op jit(solution)/shard_map/ppermute | solution.py:134
  32.0 13.8 %collective-permute-start.10 = (bf16[256,1024]{1,0:T(8,128)(2,1)}, bf16[256,1024]{1,0:T(8,128)(2,1)S(1)}, u32[]{:S(2)}, u32[]{:S(2)}) collective-permute-start(bf16[256,1024]{1,0:T(8,128)(2,1)} %pad_maximum_fusion.2), channel_id=1, source_target_pairs={{0,2},{1,3},{2,0},{3,1},{4,6},{5,7},{6,4},{7,5},{8,10},{9,11},{10,... | collective-permute-start | bytes 1572872 | tf_op jit(solution)/shard_map/ppermute | solution.py:228
  41.9 19.4 %collective-permute-start.11 = (bf16[256,1024]{1,0:T(8,128)(2,1)}, bf16[256,1024]{1,0:T(8,128)(2,1)S(1)}, u32[]{:S(2)}, u32[]{:S(2)}) collective-permute-start(bf16[256,1024]{1,0:T(8,128)(2,1)} %pad_maximum_fusion.3), channel_id=1, source_target_pairs={{0,2},{1,3},{2,0},{3,1},{4,6},{5,7},{6,4},{7,5},{8,10},{9,11},{10,... | collective-permute-start | bytes 1572872 | tf_op jit(solution)/shard_map/ppermute | solution.py:228
  46.6 15.5 %collective-permute-start.13 = (bf16[128,2048]{1,0:T(8,128)(2,1)}, bf16[128,2048]{1,0:T(8,128)(2,1)}, u32[]{:S(2)}, u32[]{:S(2)}) collective-permute-start(bf16[128,2048]{1,0:T(8,128)(2,1)} %pad_maximum_fusion.4.rest_0_), channel_id=1, source_target_pairs={{4,12},{12,20},{20,28},{28,24},{24,16},{16,8},{8,0},{0,4},{5,13},{... | collective-permute-start | bytes 1572872 | tf_op jit(solution)/shard_map/ppermute | solution.py:131
  48.2 13.9 %collective-permute-start.14 = (bf16[128,2048]{1,0:T(8,128)(2,1)}, bf16[128,2048]{1,0:T(8,128)(2,1)}, u32[]{:S(2)}, u32[]{:S(2)}) collective-permute-start(bf16[128,2048]{1,0:T(8,128)(2,1)} %pad_maximum_fusion.4.rest_0_), channel_id=1, source_target_pairs={{4,0},{12,4},{20,12},{28,20},{24,28},{16,24},{8,16},{0,8},{5,1},{1... | collective-permute-start | bytes 1572872 | tf_op jit(solution)/shard_map/ppermute | solution.py:134
  49.3 11.2 %collective-permute-start.12 = (bf16[128,1024]{1,0:T(8,128)(2,1)S(1)}, bf16[128,1024]{1,0:T(8,128)(2,1)S(1)}, u32[]{:S(2)}, u32[]{:S(2)}) collective-permute-start(bf16[128,1024]{1,0:T(8,128)(2,1)S(1)} %pad_maximum_fusion.7), channel_id=1, source_target_pairs={{0,2},{1,3},{2,0},{3,1},{4,6},{5,7},{6,4},{7,5},{8,10},{9,11},{10,... | collective-permute-start | bytes 786440 | tf_op jit(solution)/shard_map/ppermute | solution.py:228
  62.1 11.3 %collective-permute-start.15 = (bf16[128,2048]{1,0:T(8,128)(2,1)}, bf16[128,2048]{1,0:T(8,128)(2,1)S(1)}, u32[]{:S(2)}, u32[]{:S(2)}) collective-permute-start(bf16[128,2048]{1,0:T(8,128)(2,1)} %collective-permute-done.13.rest_1_), channel_id=1, source_target_pairs={{4,12},{12,20},{20,28},{28,24},{24,16},{16,8},{8,0},{0,4},{5,13},{... | collective-permute-start | bytes 1572872 | tf_op jit(solution)/shard_map/ppermute | solution.py:131
  63.3 11.5 %collective-permute-start.16 = (bf16[128,2048]{1,0:T(8,128)(2,1)}, bf16[128,2048]{1,0:T(8,128)(2,1)S(1)}, u32[]{:S(2)}, u32[]{:S(2)}) collective-permute-start(bf16[128,2048]{1,0:T(8,128)(2,1)} %collective-permute-done.14.rest_2_), channel_id=1, source_target_pairs={{4,0},{12,4},{20,12},{28,20},{24,28},{16,24},{8,16},{0,8},{5,1},{1... | collective-permute-start | bytes 1572872 | tf_op jit(solution)/shard_map/ppermute | solution.py:134
  74.8 16.3 %collective-permute-start.19 = (bf16[1024,2048]{1,0:T(8,128)(2,1)S(1)}, bf16[1024,2048]{1,0:T(8,128)(2,1)S(1)}, u32[]{:S(2)}, u32[]{:S(2)}) collective-permute-start(bf16[1024,2048]{1,0:T(8,128)(2,1)S(1)} %get-tuple-element.221.rest_0_.rest_3_.refs_13_), channel_id=1, source_target_pairs={{0,1},{1,0},{2,3},{3,2},{4,5},{5,4},{6,7},{7,6},{8,9},{9,8},{10,11... | collective-permute-start | bytes 12582920 | tf_op jit(solution)/shard_map/ppermute | solution.py:232
  74.9 16.2 %collective-permute-start.17 = (bf16[128,2048]{1,0:T(8,128)(2,1)S(1)}, bf16[128,2048]{1,0:T(8,128)(2,1)S(1)}, u32[]{:S(2)}, u32[]{:S(2)}) collective-permute-start(bf16[128,2048]{1,0:T(8,128)(2,1)S(1)} %collective-permute-done.15.rest_3_), channel_id=1, source_target_pairs={{4,12},{12,20},{20,28},{28,24},{24,16},{16,8},{8,0},{0,4},{5,13},{... | collective-permute-start | bytes 1572872 | tf_op jit(solution)/shard_map/ppermute | solution.py:131
  76.5 14.5 %collective-permute-start.18 = (bf16[128,2048]{1,0:T(8,128)(2,1)S(1)}, bf16[128,2048]{1,0:T(8,128)(2,1)S(1)}, u32[]{:S(2)}, u32[]{:S(2)}) collective-permute-start(bf16[128,2048]{1,0:T(8,128)(2,1)S(1)} %collective-permute-done.16.rest_4_), channel_id=1, source_target_pairs={{4,0},{12,4},{20,12},{28,20},{24,28},{16,24},{8,16},{0,8},{5,1},{1... | collective-permute-start | bytes 1572872 | tf_op jit(solution)/shard_map/ppermute | solution.py:134
  101.3 26.5 %collective-permute-start.24 = (bf16[528,1024]{1,0:T(8,128)(2,1)}, bf16[528,1024]{1,0:T(8,128)(2,1)S(1)}, u32[]{:S(2)}, u32[]{:S(2)}) collective-permute-start(bf16[528,1024]{1,0:T(8,128)(2,1)} %get-tuple-element.228.rest_9_.rest_0_), channel_id=1, source_target_pairs={{0,2},{1,3},{2,0},{3,1},{4,6},{5,7},{6,4},{7,5},{8,10},{9,11},{10,... | collective-permute-start | bytes 3244040 | tf_op jit(solution)/shard_map/ppermute | solution.py:228
  127.8 11.9 %collective-permute-start.25 = (bf16[528,1024]{1,0:T(8,128)(2,1)S(1)}, bf16[528,1024]{1,0:T(8,128)(2,1)S(1)}, u32[]{:S(2)}, u32[]{:S(2)}) collective-permute-start(bf16[528,1024]{1,0:T(8,128)(2,1)S(1)} %collective-permute-done.24.rest_9_.rest_3_), channel_id=1, source_target_pairs={{0,1},{1,0},{2,3},{3,2},{4,5},{5,4},{6,7},{7,6},{8,9},{9,8},{10,11... | collective-permute-start | bytes 3244040 | tf_op jit(solution)/shard_map/ppermute | solution.py:232
  151.7 25.4 %collective-permute-start.27 = (bf16[528,1024]{1,0:T(8,128)(2,1)S(1)}, bf16[528,1024]{1,0:T(8,128)(2,1)}, u32[]{:S(2)}, u32[]{:S(2)}) collective-permute-start(bf16[528,1024]{1,0:T(8,128)(2,1)S(1)} %copy-done.71), channel_id=1, source_target_pairs={{0,1},{1,0},{2,3},{3,2},{4,5},{5,4},{6,7},{7,6},{8,9},{9,8},{10,11... | collective-permute-start | bytes 3244040 | tf_op jit(solution)/shard_map/ppermute | solution.py:232
  152.2 28.2 %collective-permute-start.26 = (bf16[528,1024]{1,0:T(8,128)(2,1)}, bf16[528,1024]{1,0:T(8,128)(2,1)}, u32[]{:S(2)}, u32[]{:S(2)}) collective-permute-start(bf16[528,1024]{1,0:T(8,128)(2,1)} %get-tuple-element.242), channel_id=1, source_target_pairs={{0,1},{1,0},{2,3},{3,2},{4,5},{5,4},{6,7},{7,6},{8,9},{9,8},{10,11... | collective-permute-start | bytes 3244040 | tf_op jit(solution)/shard_map/ppermute | solution.py:232
  152.3 30.5 %collective-permute-start.28 = (bf16[528,1024]{1,0:T(8,128)(2,1)}, bf16[528,1024]{1,0:T(8,128)(2,1)S(1)}, u32[]{:S(2)}, u32[]{:S(2)}) collective-permute-start(bf16[528,1024]{1,0:T(8,128)(2,1)} %get-tuple-element.248), channel_id=1, source_target_pairs={{0,1},{1,0},{2,3},{3,2},{4,5},{5,4},{6,7},{7,6},{8,9},{9,8},{10,11... | collective-permute-start | bytes 3244040 | tf_op jit(solution)/shard_map/ppermute | solution.py:232
  156.7 26.1 %collective-permute-start.30 = (bf16[528,1024]{1,0:T(8,128)(2,1)}, bf16[528,1024]{1,0:T(8,128)(2,1)S(1)}, u32[]{:S(2)}, u32[]{:S(2)}) collective-permute-start(bf16[528,1024]{1,0:T(8,128)(2,1)} %add_convert_fusion.1), channel_id=1, source_target_pairs={{0,2},{1,3},{2,0},{3,1},{4,6},{5,7},{6,4},{7,5},{8,10},{9,11},{10,... | collective-permute-start | bytes 3244040 | tf_op jit(solution)/shard_map/ppermute | solution.py:228
  176.0 13.2 %collective-permute-start.31 = (bf16[64,2048]{1,0:T(8,128)(2,1)S(1)}, bf16[64,2048]{1,0:T(8,128)(2,1)S(1)}, u32[]{:S(2)}, u32[]{:S(2)}) collective-permute-start(bf16[64,2048]{1,0:T(8,128)(2,1)S(1)} %get-tuple-element.253), channel_id=1, source_target_pairs={{4,12},{12,20},{20,28},{28,24},{24,16},{16,8},{8,0},{0,4},{5,13},{... | collective-permute-start | bytes 786440 | tf_op jit(solution)/shard_map/ppermute | solution.py:131
  177.1 12.1 %collective-permute-start.32 = (bf16[64,2048]{1,0:T(8,128)(2,1)S(1)}, bf16[64,2048]{1,0:T(8,128)(2,1)S(1)}, u32[]{:S(2)}, u32[]{:S(2)}) collective-permute-start(bf16[64,2048]{1,0:T(8,128)(2,1)S(1)} %get-tuple-element.255), channel_id=1, source_target_pairs={{4,0},{12,4},{20,12},{28,20},{24,28},{16,24},{8,16},{0,8},{5,1},{1... | collective-permute-start | bytes 786440 | tf_op jit(solution)/shard_map/ppermute | solution.py:134
  189.2 17.6 %collective-permute-start.36 = (bf16[528,1024]{1,0:T(8,128)(2,1)S(1)}, bf16[528,1024]{1,0:T(8,128)(2,1)S(1)}, u32[]{:S(2)}, u32[]{:S(2)}) collective-permute-start(bf16[528,1024]{1,0:T(8,128)(2,1)S(1)} %get-tuple-element.270.own_ref), channel_id=1, source_target_pairs={{0,1},{1,0},{2,3},{3,2},{4,5},{5,4},{6,7},{7,6},{8,9},{9,8},{10,11... | collective-permute-start | bytes 3244040 | tf_op jit(solution)/shard_map/ppermute | solution.py:232
  190.6 16.2 %collective-permute-start.39 = (bf16[264,1024]{1,0:T(8,128)(2,1)S(1)}, bf16[264,1024]{1,0:T(8,128)(2,1)S(1)}, u32[]{:S(2)}, u32[]{:S(2)}) collective-permute-start(bf16[264,1024]{1,0:T(8,128)(2,1)S(1)} %slice.179), channel_id=1, source_target_pairs={{0,2},{1,3},{2,0},{3,1},{4,6},{5,7},{6,4},{7,5},{8,10},{9,11},{10,... | collective-permute-start | bytes 1622024 | tf_op jit(solution)/shard_map/ppermute | solution.py:228
  192.4 13.6 %collective-permute-start.34 = (bf16[128,2048]{1,0:T(8,128)(2,1)S(1)}, bf16[128,2048]{1,0:T(8,128)(2,1)S(1)}, u32[]{:S(2)}, u32[]{:S(2)}) collective-permute-start(bf16[128,2048]{1,0:T(8,128)(2,1)S(1)} %get-tuple-element.264), channel_id=1, source_target_pairs={{4,12},{12,20},{20,28},{28,24},{24,16},{16,8},{8,0},{0,4},{5,13},{... | collective-permute-start | bytes 1572872 | tf_op jit(solution)/shard_map/ppermute | solution.py:131
  193.4 13.3 %collective-permute-start.35 = (bf16[128,2048]{1,0:T(8,128)(2,1)S(1)}, bf16[128,2048]{1,0:T(8,128)(2,1)S(1)}, u32[]{:S(2)}, u32[]{:S(2)}) collective-permute-start(bf16[128,2048]{1,0:T(8,128)(2,1)S(1)} %get-tuple-element.266), channel_id=1, source_target_pairs={{4,0},{12,4},{20,12},{28,20},{24,28},{16,24},{8,16},{0,8},{5,1},{1... | collective-permute-start | bytes 1572872 | tf_op jit(solution)/shard_map/ppermute | solution.py:134
  206.8 20.4 %collective-permute-start.40 = (bf16[1056,768]{1,0:T(8,128)(2,1)S(1)}, bf16[1056,768]{1,0:T(8,128)(2,1)S(1)}, u32[]{:S(2)}, u32[]{:S(2)}) collective-permute-start(bf16[1056,768]{1,0:T(8,128)(2,1)S(1)} %get-tuple-element.282.grad_ref.refs_1_), channel_id=1, source_target_pairs={{0,1},{1,0},{2,3},{3,2},{4,5},{5,4},{6,7},{7,6},{8,9},{9,8},{10,11... | collective-permute-start | bytes 4866056 | tf_op jit(solution)/shard_map/ppermute | solution.py:232
  206.8 20.4 %collective-permute-start.41 = (bf16[392,1024]{1,0:T(8,128)(2,1)S(1)}, bf16[392,1024]{1,0:T(8,128)(2,1)S(1)}, u32[]{:S(2)}, u32[]{:S(2)}) collective-permute-start(bf16[392,1024]{1,0:T(8,128)(2,1)S(1)} %pad_maximum_fusion), channel_id=1, source_target_pairs={{0,2},{1,3},{2,0},{3,1},{4,6},{5,7},{6,4},{7,5},{8,10},{9,11},{10,... | collective-permute-start | bytes 2408456 | tf_op jit(solution)/shard_map/ppermute | solution.py:228
  208.0 17.0 %collective-permute-start.37 = (bf16[128,2048]{1,0:T(8,128)(2,1)S(1)}, bf16[128,2048]{1,0:T(8,128)(2,1)S(1)}, u32[]{:S(2)}, u32[]{:S(2)}) collective-permute-start(bf16[128,2048]{1,0:T(8,128)(2,1)S(1)} %get-tuple-element.274), channel_id=1, source_target_pairs={{4,12},{12,20},{20,28},{28,24},{24,16},{16,8},{8,0},{0,4},{5,13},{... | collective-permute-start | bytes 1572872 | tf_op jit(solution)/shard_map/ppermute | solution.py:131
  209.7 15.4 %collective-permute-start.38 = (bf16[128,2048]{1,0:T(8,128)(2,1)S(1)}, bf16[128,2048]{1,0:T(8,128)(2,1)S(1)}, u32[]{:S(2)}, u32[]{:S(2)}) collective-permute-start(bf16[128,2048]{1,0:T(8,128)(2,1)S(1)} %get-tuple-element.276), channel_id=1, source_target_pairs={{4,0},{12,4},{20,12},{28,20},{24,28},{16,24},{8,16},{0,8},{5,1},{1... | collective-permute-start | bytes 1572872 | tf_op jit(solution)/shard_map/ppermute | solution.py:134
  227.2 9.1 %collective-permute-start.42 = (bf16[1056,768]{1,0:T(8,128)(2,1)S(1)}, bf16[1056,768]{1,0:T(8,128)(2,1)S(1)}, u32[]{:S(2)}, u32[]{:S(2)}) collective-permute-start(bf16[1056,768]{1,0:T(8,128)(2,1)S(1)} %get-tuple-element.284.grad_ref.refs_0_), channel_id=1, source_target_pairs={{0,1},{1,0},{2,3},{3,2},{4,5},{5,4},{6,7},{7,6},{8,9},{9,8},{10,11... | collective-permute-start | bytes 4866056 | tf_op jit(solution)/shard_map/ppermute | solution.py:232
  227.3 23.0 %collective-permute-start.47 = (bf16[400,1024]{1,0:T(8,128)(2,1)S(1)}, bf16[400,1024]{1,0:T(8,128)(2,1)S(1)}, u32[]{:S(2)}, u32[]{:S(2)}) collective-permute-start(bf16[400,1024]{1,0:T(8,128)(2,1)S(1)} %slice.180), channel_id=1, source_target_pairs={{0,2},{1,3},{2,0},{3,1},{4,6},{5,7},{6,4},{7,5},{8,10},{9,11},{10,... | collective-permute-start | bytes 2457608 | tf_op jit(solution)/shard_map/ppermute | solution.py:228
  228.5 21.0 %collective-permute-start.45 = (bf16[128,2048]{1,0:T(8,128)(2,1)S(1)}, bf16[128,2048]{1,0:T(8,128)(2,1)S(1)}, u32[]{:S(2)}, u32[]{:S(2)}) collective-permute-start(bf16[128,2048]{1,0:T(8,128)(2,1)S(1)} %get-tuple-element.290), channel_id=1, source_target_pairs={{4,12},{12,20},{20,28},{28,24},{24,16},{16,8},{8,0},{0,4},{5,13},{... | collective-permute-start | bytes 1572872 | tf_op jit(solution)/shard_map/ppermute | solution.py:131
  230.2 19.4 %collective-permute-start.46 = (bf16[128,2048]{1,0:T(8,128)(2,1)S(1)}, bf16[128,2048]{1,0:T(8,128)(2,1)S(1)}, u32[]{:S(2)}, u32[]{:S(2)}) collective-permute-start(bf16[128,2048]{1,0:T(8,128)(2,1)S(1)} %get-tuple-element.292), channel_id=1, source_target_pairs={{4,0},{12,4},{20,12},{28,20},{24,28},{16,24},{8,16},{0,8},{5,1},{1... | collective-permute-start | bytes 1572872 | tf_op jit(solution)/shard_map/ppermute | solution.py:134
  236.3 11.9 %collective-permute-start.43 = (bf16[64,2048]{1,0:T(8,128)(2,1)S(1)}, bf16[64,2048]{1,0:T(8,128)(2,1)S(1)}, u32[]{:S(2)}, u32[]{:S(2)}) collective-permute-start(bf16[64,2048]{1,0:T(8,128)(2,1)S(1)} %get-tuple-element.285), channel_id=1, source_target_pairs={{4,12},{12,20},{20,28},{28,24},{24,16},{16,8},{8,0},{0,4},{5,13},{... | collective-permute-start | bytes 786440 | tf_op jit(solution)/shard_map/ppermute | solution.py:131
  238.0 11.6 %collective-permute-start.44 = (bf16[64,2048]{1,0:T(8,128)(2,1)S(1)}, bf16[64,2048]{1,0:T(8,128)(2,1)S(1)}, u32[]{:S(2)}, u32[]{:S(2)}) collective-permute-start(bf16[64,2048]{1,0:T(8,128)(2,1)S(1)} %get-tuple-element.287), channel_id=1, source_target_pairs={{4,0},{12,4},{20,12},{28,20},{24,28},{16,24},{8,16},{0,8},{5,1},{1... | collective-permute-start | bytes 786440 | tf_op jit(solution)/shard_map/ppermute | solution.py:134
  253.2 14.1 %collective-permute-start.48 = (bf16[128,2048]{1,0:T(8,128)(2,1)S(1)}, bf16[128,2048]{1,0:T(8,128)(2,1)S(1)}, u32[]{:S(2)}, u32[]{:S(2)}) collective-permute-start(bf16[128,2048]{1,0:T(8,128)(2,1)S(1)} %get-tuple-element.308), channel_id=1, source_target_pairs={{4,12},{12,20},{20,28},{28,24},{24,16},{16,8},{8,0},{0,4},{5,13},{... | collective-permute-start | bytes 1572872 | tf_op jit(solution)/shard_map/ppermute | solution.py:131
  254.0 13.4 %collective-permute-start.49 = (bf16[128,2048]{1,0:T(8,128)(2,1)S(1)}, bf16[128,2048]{1,0:T(8,128)(2,1)S(1)}, u32[]{:S(2)}, u32[]{:S(2)}) collective-permute-start(bf16[128,2048]{1,0:T(8,128)(2,1)S(1)} %get-tuple-element.310), channel_id=1, source_target_pairs={{4,0},{12,4},{20,12},{28,20},{24,28},{16,24},{8,16},{0,8},{5,1},{1... | collective-permute-start | bytes 1572872 | tf_op jit(solution)/shard_map/ppermute | solution.py:134
  268.9 26.6 %collective-permute-start.57 = (bf16[528,1024]{1,0:T(8,128)(2,1)}, bf16[528,1024]{1,0:T(8,128)(2,1)}, u32[]{:S(2)}, u32[]{:S(2)}) collective-permute-start(bf16[528,1024]{1,0:T(8,128)(2,1)} %get-tuple-element.329.refs_0_), channel_id=1, source_target_pairs={{0,2},{1,3},{2,0},{3,1},{4,6},{5,7},{6,4},{7,5},{8,10},{9,11},{10,... | collective-permute-start | bytes 3244040 | tf_op jit(solution)/shard_map/ppermute | solution.py:228
  270.3 14.3 %collective-permute-start.51 = (bf16[128,2048]{1,0:T(8,128)(2,1)}, bf16[128,2048]{1,0:T(8,128)(2,1)S(1)}, u32[]{:S(2)}, u32[]{:S(2)}) collective-permute-start(bf16[128,2048]{1,0:T(8,128)(2,1)} %get-tuple-element.315), channel_id=1, source_target_pairs={{4,12},{12,20},{20,28},{28,24},{24,16},{16,8},{8,0},{0,4},{5,13},{... | collective-permute-start | bytes 1572872 | tf_op jit(solution)/shard_map/ppermute | solution.py:131
  271.3 14.1 %collective-permute-start.52 = (bf16[128,2048]{1,0:T(8,128)(2,1)S(1)}, bf16[128,2048]{1,0:T(8,128)(2,1)S(1)}, u32[]{:S(2)}, u32[]{:S(2)}) collective-permute-start(bf16[128,2048]{1,0:T(8,128)(2,1)S(1)} %get-tuple-element.317), channel_id=1, source_target_pairs={{4,0},{12,4},{20,12},{28,20},{24,28},{16,24},{8,16},{0,8},{5,1},{1... | collective-permute-start | bytes 1572872 | tf_op jit(solution)/shard_map/ppermute | solution.py:134
  272.3 14.8 %collective-permute-start.53 = (f32[8,1024]{1,0:T(8,128)S(1)}, f32[8,1024]{1,0:T(8,128)S(1)}, u32[]{:S(2)}, u32[]{:S(2)}) collective-permute-start(f32[8,1024]{1,0:T(8,128)S(1)} %copy-done.68), channel_id=1, source_target_pairs={{0,4},{4,0},{8,12},{12,8},{16,20},{20,16},{24,28},{28,24},{1,5},{5... | collective-permute-start | bytes 98312 | tf_op jit(solution)/shard_map/ppermute | solution.py:1195
  287.2 14.5 %collective-permute-start.54 = (bf16[128,2048]{1,0:T(8,128)(2,1)}, bf16[128,2048]{1,0:T(8,128)(2,1)S(1)}, u32[]{:S(2)}, u32[]{:S(2)}) collective-permute-start(bf16[128,2048]{1,0:T(8,128)(2,1)} %get-tuple-element.324), channel_id=1, source_target_pairs={{4,12},{12,20},{20,28},{28,24},{24,16},{16,8},{8,0},{0,4},{5,13},{... | collective-permute-start | bytes 1572872 | tf_op jit(solution)/shard_map/ppermute | solution.py:131
  287.8 14.2 %collective-permute-start.55 = (bf16[128,2048]{1,0:T(8,128)(2,1)}, bf16[128,2048]{1,0:T(8,128)(2,1)S(1)}, u32[]{:S(2)}, u32[]{:S(2)}) collective-permute-start(bf16[128,2048]{1,0:T(8,128)(2,1)} %get-tuple-element.326), channel_id=1, source_target_pairs={{4,0},{12,4},{20,12},{28,20},{24,28},{16,24},{8,16},{0,8},{5,1},{1... | collective-permute-start | bytes 1572872 | tf_op jit(solution)/shard_map/ppermute | solution.py:134
  295.5 9.5 %collective-permute-start.56 = (bf16[528,1024]{1,0:T(8,128)(2,1)}, bf16[528,1024]{1,0:T(8,128)(2,1)}, u32[]{:S(2)}, u32[]{:S(2)}) collective-permute-start(bf16[528,1024]{1,0:T(8,128)(2,1)} %get-tuple-element.329.refs_0_), channel_id=1, source_target_pairs={{0,1},{1,0},{2,3},{3,2},{4,5},{5,4},{6,7},{7,6},{8,9},{9,8},{10,11... | collective-permute-start | bytes 3244040 | tf_op jit(solution)/shard_map/ppermute | solution.py:232
  295.5 9.5 %collective-permute-start.58 = (bf16[528,1024]{1,0:T(8,128)(2,1)}, bf16[528,1024]{1,0:T(8,128)(2,1)}, u32[]{:S(2)}, u32[]{:S(2)}) collective-permute-start(bf16[528,1024]{1,0:T(8,128)(2,1)} %collective-permute-done.57.refs_3_), channel_id=1, source_target_pairs={{0,1},{1,0},{2,3},{3,2},{4,5},{5,4},{6,7},{7,6},{8,9},{9,8},{10,11... | collective-permute-start | bytes 3244040 | tf_op jit(solution)/shard_map/ppermute | solution.py:232
  302.8 9.0 %collective-permute-start.63 = (bf16[128,1024]{1,0:T(8,128)(2,1)S(1)}, bf16[128,1024]{1,0:T(8,128)(2,1)S(1)}, u32[]{:S(2)}, u32[]{:S(2)}) collective-permute-start(bf16[128,1024]{1,0:T(8,128)(2,1)S(1)} %slice.163), channel_id=1, source_target_pairs={{0,2},{1,3},{2,0},{3,1},{4,6},{5,7},{6,4},{7,5},{8,10},{9,11},{10,... | collective-permute-start | bytes 786440 | tf_op jit(solution)/shard_map/ppermute | solution.py:228
  (92 other events, 844.7 us)
